TPU v7x, 768 devices: a whole 4x8x12 slice. The times are simulated.
768 devices in a mesh: gx: 12 (over z), gy: 64 (over x, y, core).
Axes of the slice: x: 4, y: 8, z: 12, core: 2. Of those that a mesh axis runs over, the one named last changes fastest.
Arguments:
- flow_state: float32 [4, 96, 512, 128], P(None, 'gx', 'gy'), may hold values from -4.5 to 4.5, as said below
- building_height: int32 [12, 64], P('gx', 'gy'), may hold values from 0 to 8
- pressure_old: float32 [96, 512, 128], P('gx', 'gy'), may hold values from -0.3 to 0.3
Outputs:
- new_state: float32 [4, 96, 512, 128], P(None, 'gx', 'gy')
- pressure: float32 [96, 512, 128], P('gx', 'gy')
Inputs may be any that keep to these rules, and one draw needn't show every extreme that they name: `flow_state`: velocity and temperature fluctuations whose size varies across the district.
All inputs are finite; a program needn't handle non-finite values.
Results may differ from a plain program's by a relative error of at most 0.0003.
Values sent between devices are 32-bit elements; how exact they have to be, the bound alone decides.
No kernel may reach another device: no remote copies, remote signals or barrier semaphores. Data moves between devices by JAX's collectives and lax.ppermute only.
A program may use at most 32 MiB of HBM per device.

v0:
```python
import math

import jax
import jax.numpy as jnp
import numpy as np
from jax import lax
from jax.sharding import PartitionSpec as P

ITERS = 2


HIGHEST = lax.Precision.HIGHEST
viscosity = 0.05
time_step = 0.01
drag_strength = 20.0
heating = 40.0
buoyancy = 10.0
helmholtz_shift = 0.001
local_shift = 0.5
coarse_shift = 0.02
gll_points = (
    -1.0,
    -0.8717401485096066,
    -0.5917001814331423,
    -0.2092992179024789,
    0.2092992179024789,
    0.5917001814331423,
    0.8717401485096066,
    1.0,
)


def padded_2(cells, sides, width):
    for axis, dim in sides:
        count = lax.axis_size(axis)
        head = lax.slice_in_dim(cells, 0, width, axis=dim)
        tail = lax.slice_in_dim(cells, cells.shape[dim] - width, cells.shape[dim], axis=dim)
        cells = jnp.concatenate(
            [
                lax.ppermute(tail, axis, [(i, (i + 1) % count) for i in range(count)]),
                cells,
                lax.ppermute(head, axis, [((i + 1) % count, i) for i in range(count)]),
            ],
            axis=dim,
        )
    return cells


def legendre_seven(points):
    squared = points * points
    return points * (((429.0 * squared - 693.0) * squared + 315.0) * squared - 35.0) / 16.0


def jacobi_eigen(matrix):
    current = np.array(matrix)
    basis = np.eye(8)
    for rounds in range(12):
        for first in range(7):
            for second in range(first + 1, 8):
                rotation_angle = 0.5 * math.atan2(
                    2.0 * float(current[first, second]),
                    float(current[second, second] - current[first, first]),
                )
                cosine = math.cos(rotation_angle)
                sine = math.sin(rotation_angle)
                rotation = np.eye(8)
                rotation[first, first] = cosine
                rotation[second, second] = cosine
                rotation[first, second] = sine
                rotation[second, first] = -sine
                current = rotation.T @ current @ rotation
                basis = basis @ rotation
    return (np.sum(current * np.eye(8), axis=0), basis)


def gll_tables():
    gll_nodes = np.array(gll_points)
    values = legendre_seven(gll_nodes)
    weights = 2.0 / (56.0 * values * values)
    differ = gll_nodes[:, None] - gll_nodes[None, :] + np.eye(8)
    derivative = values[:, None] / values[None, :] / differ * (1.0 - np.eye(8))
    derivative = (
        derivative + np.eye(8) * np.array([-14.0, 0.0, 0.0, 0.0, 0.0, 0.0, 0.0, 14.0])[None, :]
    )
    stiffness = derivative.T @ (weights[:, None] * derivative)
    scaled = stiffness / np.sqrt(np.outer(weights, weights))
    scaled = 0.5 * (scaled + scaled.T)
    eigen_values, eigen_vectors = jacobi_eigen(scaled)
    eigen_basis = eigen_vectors / np.sqrt(weights)[:, None]
    return (gll_nodes, weights, derivative, eigen_basis, np.maximum(eigen_values, 0.0))


def tables():
    return tuple((jnp.asarray(table, dtype=jnp.float32) for table in gll_tables()))


def along_x(field, matrix):
    first, second, third, fourth = field.shape
    blocks = field.reshape(first, second // 8, 8, third, fourth)
    return jnp.einsum("ij,cejyz->ceiyz", matrix, blocks, precision=HIGHEST).reshape(field.shape)


def along_y(field, matrix):
    first, second, third, fourth = field.shape
    blocks = field.reshape(first, second, third // 8, 8, fourth)
    return jnp.einsum("ij,cxejz->cxeiz", matrix, blocks, precision=HIGHEST).reshape(field.shape)


def along_z(field, matrix):
    first, second, third, fourth = field.shape
    banded = jnp.kron(jnp.eye(fourth // 8, dtype=jnp.float32), matrix)
    rows = field.reshape(first * second * third, fourth)
    return jnp.dot(rows, banded.T, precision=HIGHEST).reshape(field.shape)


def weight_grid(weights, width, depth, height):
    return (
        jnp.tile(weights, width // 8)[:, None, None]
        * jnp.tile(weights, depth // 8)[None, :, None]
        * jnp.tile(weights, height // 8)[None, None, :]
    )


def face_counts(count):
    index = jnp.arange(count, dtype=jnp.int32) % 8
    return jnp.where((index == 0) | (index == 7), 2.0, 1.0).astype(jnp.float32)


def multiplicity(width, depth, height):
    vertical_index = jnp.arange(height, dtype=jnp.int32)
    ends = (vertical_index == 0) | (vertical_index == height - 1)
    vertical = jnp.where(ends, 1.0, face_counts(height))
    return (
        face_counts(width)[:, None, None]
        * face_counts(depth)[None, :, None]
        * vertical[None, None, :]
    )


def canopy_mask(building_height, height):
    column = jnp.repeat(jnp.repeat(building_height, 8, axis=0), 8, axis=1)
    layer = jnp.arange(height, dtype=jnp.int32) // 8
    return (layer[None, None, :] < column[:, :, None]).astype(jnp.float32)


def stiffness_action(field, mass, derivative):
    term = along_x(mass * along_x(field, derivative), derivative.T)
    term = term + along_y(mass * along_y(field, derivative), derivative.T)
    return term + along_z(mass * along_z(field, derivative), derivative.T)


def pair_z(field):
    first, second, third, fourth = field.shape
    index = jnp.arange(fourth, dtype=jnp.int32)
    source_index = index[:, None]
    target_index = index[None, :]
    upper = (source_index % 8 == 7) & (target_index == source_index + 1)
    lower = (source_index % 8 == 0) & (target_index == source_index - 1) & (source_index > 0)
    joining = ((source_index == target_index) | upper | lower).astype(jnp.float32)
    rows = field.reshape(first * second * third, fourth)
    return jnp.dot(rows, joining, precision=HIGHEST).reshape(field.shape)


def pair_x_padded(padded):
    first, second, third, fourth = padded.shape
    inner = padded[:, 1:-1].reshape(first, (second - 2) // 8, 8, third, fourth)
    lasts = jnp.concatenate([padded[:, :1], inner[:, :, 7]], axis=1)
    starts = jnp.concatenate([inner[:, :, 0], padded[:, -1:]], axis=1)
    sums = lasts + starts
    joined = jnp.concatenate([sums[:, :-1, None], inner[:, :, 1:7], sums[:, 1:, None]], axis=2)
    return joined.reshape(first, second - 2, third, fourth)


def pair_y_padded(padded):
    first, second, third, fourth = padded.shape
    inner = padded[:, :, 1:-1].reshape(first, second, (third - 2) // 8, 8, fourth)
    lasts = jnp.concatenate([padded[:, :, :1], inner[:, :, :, 7]], axis=2)
    starts = jnp.concatenate([inner[:, :, :, 0], padded[:, :, -1:]], axis=2)
    sums = lasts + starts
    joined = jnp.concatenate(
        [sums[:, :, :-1, None], inner[:, :, :, 1:7], sums[:, :, 1:, None]], axis=3
    )
    return joined.reshape(first, second, third - 2, fourth)


def assemble(field):
    padded = padded_2(field, (("gx", 1), ("gy", 2)), 1)
    return pair_z(pair_y_padded(pair_x_padded(padded)))


def local_solve(field, eigen_basis, eigen_values):
    first, width, depth, height = field.shape
    spectrum = (
        jnp.tile(eigen_values, width // 8)[:, None, None]
        + jnp.tile(eigen_values, depth // 8)[None, :, None]
        + jnp.tile(eigen_values, height // 8)[None, None, :]
    )
    inverse = eigen_basis.T
    modal = along_z(along_y(along_x(field, inverse), inverse), inverse)
    modal = modal / (spectrum + local_shift)
    return along_z(along_y(along_x(modal, eigen_basis), eigen_basis), eigen_basis)


def interpolation(width, gll_nodes):
    count = width // 8
    columns = count + 1
    position = jnp.tile(gll_nodes, count)
    element = jnp.arange(width, dtype=jnp.int32) // 8
    following = element + 1
    target = jnp.arange(columns, dtype=jnp.int32)[None, :]
    left = jnp.where(target == element[:, None], (1.0 - position)[:, None] / 2.0, 0.0)
    right = jnp.where(target == following[:, None], (1.0 + position)[:, None] / 2.0, 0.0)
    return left + right


def restrict(field, across, along, vertical):
    reduced = jnp.einsum("xa,xyz->ayz", across, field, precision=HIGHEST)
    reduced = jnp.einsum("yb,ayz->abz", along, reduced, precision=HIGHEST)
    return jnp.einsum("zc,abz->abc", vertical, reduced, precision=HIGHEST)


def prolong(coarse, across, along, vertical):
    fine = jnp.einsum("zc,abc->abz", vertical, coarse, precision=HIGHEST)
    fine = jnp.einsum("yb,abz->ayz", along, fine, precision=HIGHEST)
    return jnp.einsum("xa,ayz->xyz", across, fine, precision=HIGHEST)


def spectral_tables(count):
    index = jnp.arange(count, dtype=jnp.int32)
    angle = 2.0 * np.pi / count * (index[:, None] * index[None, :] % count).astype(jnp.float32)
    hartley = (jnp.cos(angle) + jnp.sin(angle)) / np.sqrt(count)
    eigen = 2.0 - 2.0 * jnp.cos(2.0 * np.pi / count * index.astype(jnp.float32))
    return (hartley.astype(jnp.float32), eigen.astype(jnp.float32))


def cosine_tables(count):
    index = jnp.arange(count, dtype=jnp.int32).astype(jnp.float32)
    angle = np.pi / count * (index[:, None] + 0.5) * index[None, :]
    norms = jnp.where(index == 0, np.sqrt(1.0 / count), np.sqrt(2.0 / count))
    basis = jnp.cos(angle) * norms[None, :]
    eigen = 2.0 - 2.0 * jnp.cos(np.pi / count * index)
    return (basis.astype(jnp.float32), eigen.astype(jnp.float32))


def coarse_solve_levels(grid):
    levels, first, second = grid.shape
    hartley_x, eigen_x = spectral_tables(first)
    hartley_y, eigen_y = spectral_tables(second)
    cosine_z, eigen_z = cosine_tables(levels)
    modes = jnp.einsum("ai,kij->kaj", hartley_x, grid, precision=HIGHEST)
    modes = jnp.einsum("bj,kaj->kab", hartley_y, modes, precision=HIGHEST)
    modes = jnp.einsum("kc,kab->cab", cosine_z, modes, precision=HIGHEST)
    modes = modes / (
        2.0 * (eigen_z[:, None, None] + eigen_x[None, :, None] + eigen_y[None, None, :])
        + coarse_shift
    )
    values = jnp.einsum("kc,cab->kab", cosine_z, modes, precision=HIGHEST)
    values = jnp.einsum("bj,kab->kaj", hartley_y, values, precision=HIGHEST)
    return jnp.einsum("ai,kaj->kij", hartley_x, values, precision=HIGHEST)


def coarse_whole(piece):
    rows, columns, levels = piece.shape
    gathered = lax.all_gather(
        piece.reshape(1, rows * columns * levels), ("gx", "gy"), axis=0, tiled=True
    )
    parts_x = lax.axis_size("gx")
    parts_y = lax.axis_size("gy")
    grid = gathered.reshape(parts_x, parts_y, rows, columns, levels).transpose(4, 2, 3, 0, 1)
    inner_x = rows - 1
    inner_y = columns - 1
    core = grid[:, :inner_x, :inner_y]
    core = core.at[:, 0].add(jnp.roll(grid[:, inner_x, :inner_y], 1, axis=2))
    core = core.at[:, :, 0].add(jnp.roll(grid[:, :inner_x, inner_y], 1, axis=3))
    core = core.at[:, 0, 0].add(jnp.roll(grid[:, inner_x, inner_y], (1, 1), axis=(1, 2)))
    whole = core.transpose(0, 3, 1, 4, 2).reshape(levels, parts_x * inner_x, parts_y * inner_y)
    solution = coarse_solve_levels(whole)
    extended = jnp.concatenate([solution, solution[:, :inner_x]], axis=1)
    extended = jnp.concatenate([extended, extended[:, :, :inner_y]], axis=2)
    start_x = lax.axis_index("gx") * inner_x
    start_y = lax.axis_index("gy") * inner_y
    own = lax.dynamic_slice(extended, (jnp.int32(0), start_x, start_y), (levels, rows, columns))
    return own.transpose(1, 2, 0)


def coarse_term(residual, counts, across, along, vertical):
    piece = restrict(residual[0] / counts, across, along, vertical)
    local = coarse_whole(piece)
    return prolong(local, across, along, vertical)[None]


def provisional_state(flow_state, mass, counts, canopy, derivative):
    speed = jnp.sqrt(
        flow_state[0] * flow_state[0]
        + flow_state[1] * flow_state[1]
        + flow_state[2] * flow_state[2]
    )
    drag = drag_strength * canopy * speed
    forcing = jnp.stack(
        [
            -drag * flow_state[0],
            -drag * flow_state[1],
            -drag * flow_state[2] + buoyancy * flow_state[3],
            heating * canopy,
        ]
    )
    advection = -(
        flow_state[0] * along_x(flow_state, derivative)
        + flow_state[1] * along_y(flow_state, derivative)
        + flow_state[2] * along_z(flow_state, derivative)
    )
    rate = mass * (advection + forcing) - viscosity * stiffness_action(flow_state, mass, derivative)
    updated = flow_state + time_step * assemble(rate) / (mass * counts)
    height = flow_state.shape[3]
    vertical_index = jnp.arange(height, dtype=jnp.int32)
    wall = jnp.where((vertical_index == 0) | (vertical_index == height - 1), 0.0, 1.0).astype(
        jnp.float32
    )
    return jnp.concatenate([updated[:2], updated[2:3] * wall, updated[3:]], axis=0)


def pressure_source(provisional, mass, derivative):
    divergence = (
        along_x(provisional[0:1], derivative)
        + along_y(provisional[1:2], derivative)
        + along_z(provisional[2:3], derivative)
    )
    return -assemble(mass * divergence)


def corrected_state(provisional, pressure, mass, counts, derivative):
    gradient = jnp.concatenate(
        [
            along_x(pressure, derivative),
            along_y(pressure, derivative),
            along_z(pressure, derivative),
        ],
        axis=0,
    )
    velocity = provisional[:3] - assemble(mass * gradient) / (mass * counts)
    return jnp.concatenate([velocity, provisional[3:]], axis=0)


def inner_sum(first, second, counts):
    return lax.psum(jnp.sum(first * second / counts), ("gx", "gy"))


def on_device(flow_state, building_height, pressure_old):
    gll_nodes, weights, derivative, eigen_basis, eigen_values = tables()
    first, width, depth, height = flow_state.shape
    mass = weight_grid(weights, width, depth, height)
    counts = multiplicity(width, depth, height)
    canopy = canopy_mask(building_height, height)
    across = interpolation(width, gll_nodes)
    along = interpolation(depth, gll_nodes)
    vertical = interpolation(height, gll_nodes)
    provisional = provisional_state(flow_state, mass, counts, canopy, derivative)
    source = pressure_source(provisional, mass, derivative)

    def operate(field):
        return assemble(stiffness_action(field, mass, derivative) + helmholtz_shift * mass * field)

    def smooth(residual):
        local = assemble(local_solve(residual, eigen_basis, eigen_values))
        return local + coarse_term(residual, counts, across, along, vertical)

    pressure = pressure_old[None]
    residual = source - operate(pressure)
    smoothed = smooth(residual)
    direction = smoothed
    product = inner_sum(residual, smoothed, counts)
    for turn in range(ITERS):
        image = operate(direction)
        alpha = product / inner_sum(direction, image, counts)
        pressure = pressure + alpha * direction
        if turn + 1 < ITERS:
            residual = residual - alpha * image
            smoothed = smooth(residual)
            following = inner_sum(residual, smoothed, counts)
            direction = smoothed + following / product * direction
            product = following
    new_state = corrected_state(provisional, pressure, mass, counts, derivative)
    return (new_state, pressure[0])


def solution(mesh):
    in_specs = (P(None, "gx", "gy", None), P("gx", "gy"), P("gx", "gy", None))
    out_specs = (P(None, "gx", "gy", None), P("gx", "gy", None))
    return jax.shard_map(
        on_device, mesh=mesh, in_specs=in_specs, out_specs=out_specs, check_vma=False
    )
```

profile of v0, /device:TPU:1, one launch (start us, length us, event | category | flops | bytes accessed | tf_op | source)
XLA Modules:
  0.0 722.7 jit_solution(18058484707865034344)
XLA Ops:
  3.5 1.5 broadcast_multiply_fusion
  7.5 4.9 collective-permute-start.8
  12.5 12.2 %collective-permute-start.9 = (f32[1,1,8,128]{3,1,2,0:T(1,128)}, f32[1,1,8,128]{3,1,2,0:T(1,128)}, u32[]{:S(2)}, u32[]{:S(2)}) collective-permute-start(f32[1,1,8,128]{3,1,2,0:T(1,128)} %get-tuple-element.177), channel_id=1, source_target_pairs={{64,0},{128,64},{192,128},{256,192},{320,256},{384,320},{448,384},... | collective-permute-start | bytes 12296 | tf_op jit(solution)/shard_map/ppermute | solution.py:42
  27.0 1.1 reshape.1958
  37.6 1.3 fusion.2
  39.5 2.0 collective-permute-start
  41.6 4.6 collective-permute-start.1
  51.5 1.3 pad_maximum_fusion.29
  52.8 4.6 collective-permute-start.10
  57.4 1.9 collective-permute-start.11
  66.0 3.6 collective-permute-start.2
  69.7 4.1 collective-permute-start.3
  73.8 1.1 collective-permute-done.3
  80.8 1.9 collective-permute-start.4
  82.7 4.6 collective-permute-start.5
  88.0 3.0 collective-permute-start.6
  91.1 7.4 %collective-permute-start.7 = (f32[1,10,1,128]{3,1,2,0:T(8,128)S(1)}, f32[1,10,1,128]{3,1,2,0:T(8,128)S(1)}, u32[]{:S(2)}, u32[]{:S(2)}) collective-permute-start(f32[1,10,1,128]{3,1,2,0:T(8,128)S(1)} %get-tuple-element.155), channel_id=1, source_target_pairs={{1,0},{2,1},{3,2},{4,3},{5,4},{6,5},{7,6},{8,7},{9,8},{10,9},{11,1... | collective-permute-start | bytes 15368 | tf_op jit(solution)/shard_map/ppermute | solution.py:42
  104.0 1.9 collective-permute-start.12
  105.9 5.1 collective-permute-start.13
  111.1 89.5 %all-gather = f32[768,1,68]{2,1,0:T(1,128)S(1)} all-gather(f32[1,1,68]{2,1,0:T(1,128)S(1)} %reshape.1947), channel_id=1, replica_groups=mesh['gx'=12,'gy'=64] {'gx','gy'}, dimensions={0}, use_global_device_ids=true | all-gather | bytes 209168 | tf_op jit(solution)/shard_map/all_gather | solution.py:264
  205.4 2.0 collective-permute-start.14
  207.4 2.4 collective-permute-start.15
  210.0 2.6 collective-permute-done.15
  216.7 2.2 collective-permute-start.16
  218.8 4.3 collective-permute-start.17
  223.9 2.8 collective-permute-start.18
  226.7 5.3 collective-permute-start.19
  234.1 115.3 %all-reduce = (f32[]{:T(128)}, f32[]{:T(128)}) all-reduce(f32[]{:T(128)} %get-tuple-element.81, f32[]{:T(128)} %get-tuple-element.80), channel_id=1, replica_groups=mesh['gx'=12,'gy'=64] {'gx','gy'}, use_global_device_ids=true, to_apply=%region_1.2 | all-reduce | flops 2 | bytes 16 | tf_op jit(solution)/shard_map/psum | solution.py:345
  353.6 1.9 collective-permute-start.20
  355.5 4.6 collective-permute-start.21
  360.1 84.2 %all-gather.1 = f32[768,1,68]{2,1,0:T(1,128)S(1)} all-gather(f32[1,1,68]{2,1,0:T(1,128)S(1)} %reshape.1949), channel_id=1, replica_groups=mesh['gx'=12,'gy'=64] {'gx','gy'}, dimensions={0}, use_global_device_ids=true | all-gather | bytes 209168 | tf_op jit(solution)/shard_map/all_gather | solution.py:264
  448.1 1.9 collective-permute-start.22
  450.0 2.4 collective-permute-start.23
  452.6 2.6 collective-permute-done.23
  457.9 110.6 %psum.30 = f32[]{:T(128)} all-reduce(f32[]{:T(128)} %get-tuple-element.221), channel_id=1, replica_groups=mesh['gx'=12,'gy'=64] {'gx','gy'}, use_global_device_ids=true, to_apply=%region_5.6 | all-reduce | flops 1 | bytes 8 | tf_op jit(solution)/shard_map/psum | solution.py:345
  571.2 3.7 collective-permute-start.24
  574.9 2.8 collective-permute-start.25
  577.7 1.5 collective-permute-done.25
  579.2 2.2 collective-permute-start.26
  581.4 3.8 collective-permute-start.27
  585.2 1.2 collective-permute-done.27
  586.7 0.9 fusion.33
  587.6 113.8 %psum.31 = f32[]{:T(128)} all-reduce(f32[]{:T(128)} %fusion.33), channel_id=1, replica_groups=mesh['gx'=12,'gy'=64] {'gx','gy'}, use_global_device_ids=true, to_apply=%region_7.8 | all-reduce | flops 1 | bytes 8 | tf_op jit(solution)/shard_map/psum | solution.py:345
  704.6 2.4 collective-permute-start.28
  707.1 4.0 collective-permute-start.29
  711.9 1.9 collective-permute-start.30
  713.9 3.7 collective-permute-start.31
  717.6 1.4 collective-permute-done.31
  (456 shorter events, 68.7 us)
Async XLA Ops:
  6.7 19.2 %copy-start.1 = (f32[4,8,8,128]{3,2,1,0:T(8,128)S(1)}, f32[4,8,8,128]{3,2,1,0:T(8,128)}, u32[]{:S(2)}) copy-start(f32[4,8,8,128]{3,2,1,0:T(8,128)} %param.20) | copy-start | bytes 393220
  6.9 18.9 %copy-start.12 = (f32[1,8,8,128]{3,1,2,0:T(8,128)}, f32[1,8,8,128]{3,1,2,0:T(8,128)S(1)}, u32[]{:S(2)}) copy-start(f32[1,8,8,128]{3,1,2,0:T(8,128)S(1)} %fusion.14) | copy-start | bytes 98308
  7.5 18.3 %copy-start.32 = (f32[8,8,1,1]{1,0,3,2:T(8,128)S(1)}, f32[8,8,1,1]{1,0,3,2:T(8,128)}, u32[]{:S(2)}) copy-start(f32[8,8,1,1]{1,0,3,2:T(8,128)} %constant.387) | copy-start | bytes 772
  7.5 43.9 %collective-permute-start.8 = (f32[1,1,8,128]{3,1,2,0:T(1,128)}, f32[1,1,8,128]{3,1,2,0:T(1,128)}, u32[]{:S(2)}, u32[]{:S(2)}) collective-permute-start(f32[1,1,8,128]{3,1,2,0:T(1,128)} %get-tuple-element.176), channel_id=1, source_target_pairs={{0,64},{64,128},{128,192},{192,256},{256,320},{320,384},{384,448},... | collective-permute-start | bytes 12296 | tf_op jit(solution)/shard_map/ppermute | solution.py:40
  12.5 39.0 %collective-permute-start.9 = (f32[1,1,8,128]{3,1,2,0:T(1,128)}, f32[1,1,8,128]{3,1,2,0:T(1,128)}, u32[]{:S(2)}, u32[]{:S(2)}) collective-permute-start(f32[1,1,8,128]{3,1,2,0:T(1,128)} %get-tuple-element.177), channel_id=1, source_target_pairs={{64,0},{128,64},{192,128},{256,192},{320,256},{384,320},{448,384},... | collective-permute-start | bytes 12296 | tf_op jit(solution)/shard_map/ppermute | solution.py:42
  26.3 10.1 %copy-start.2 = (f32[8,4,8,128]{3,0,2,1:T(8,128)}, f32[8,4,8,128]{3,0,2,1:T(8,128)S(1)}, u32[]{:S(2)}) copy-start(f32[8,4,8,128]{3,0,2,1:T(8,128)S(1)} %fusion.351) | copy-start | bytes 393220
  30.9 5.5 copy-start.3
  37.6 12.0 %copy-start.49 = (f32[8]{0:T(128)S(1)}, f32[8]{0:T(128)}, u32[]{:S(2)}) copy-start(f32[8]{0:T(128)} %constant.376.clone) | copy-start | bytes 100
  37.6 25.0 %copy-start = (f32[16,8,16,8]{3,2,1,0:T(8,128)S(1)}, f32[16,8,16,8]{3,2,1,0:T(8,128)}, u32[]{:S(2)}) copy-start(f32[16,8,16,8]{3,2,1,0:T(8,128)} %get-tuple-element.208) | copy-start | bytes 196612
  39.5 11.9 %copy-start.13 = (f32[1,8,8,128]{3,1,2,0:T(8,128)S(1)}, f32[1,8,8,128]{3,1,2,0:T(8,128)}, u32[]{:S(2)}) copy-start(f32[1,8,8,128]{3,1,2,0:T(8,128)} %copy-done.12) | copy-start | bytes 98308
  39.5 25.8 %collective-permute-start = (f32[4,1,8,128]{3,1,2,0:T(1,128)}, f32[4,1,8,128]{3,1,2,0:T(1,128)S(1)}, u32[]{:S(2)}, u32[]{:S(2)}) collective-permute-start(f32[4,1,8,128]{3,1,2,0:T(1,128)} %get-tuple-element.105), channel_id=1, source_target_pairs={{0,64},{64,128},{128,192},{192,256},{256,320},{320,384},{384,448},... | collective-permute-start | bytes 49160 | tf_op jit(solution)/shard_map/ppermute | solution.py:40
  41.6 23.8 %collective-permute-start.1 = (f32[4,1,8,128]{3,1,2,0:T(1,128)}, f32[4,1,8,128]{3,1,2,0:T(1,128)}, u32[]{:S(2)}, u32[]{:S(2)}) collective-permute-start(f32[4,1,8,128]{3,1,2,0:T(1,128)} %get-tuple-element.106), channel_id=1, source_target_pairs={{64,0},{128,64},{192,128},{256,192},{320,256},{384,320},{448,384},... | collective-permute-start | bytes 49160 | tf_op jit(solution)/shard_map/ppermute | solution.py:42
  52.8 10.9 %collective-permute-start.10 = (f32[1,10,1,128]{3,1,2,0:T(8,128)}, f32[1,10,1,128]{3,1,2,0:T(8,128)S(1)}, u32[]{:S(2)}, u32[]{:S(2)}) collective-permute-start(f32[1,10,1,128]{3,1,2,0:T(8,128)} %get-tuple-element.148), channel_id=1, source_target_pairs={{0,1},{1,2},{2,3},{3,4},{4,5},{5,6},{6,7},{7,8},{8,9},{9,10},{10,1... | collective-permute-start | bytes 15368 | tf_op jit(solution)/shard_map/ppermute | solution.py:40
  57.4 6.3 collective-permute-start.11
  61.1 41.4 %copy-start.64 = (f32[128]{0:T(128)}, f32[128]{0:T(128)S(1)}, u32[]{:S(2)}) copy-start(f32[128]{0:T(128)S(1)} %add.708) | copy-start | bytes 1540
  62.5 38.9 %copy-start.43 = (f32[128]{0:T(128)}, f32[128]{0:T(128)S(1)}, u32[]{:S(2)}) copy-start(f32[128]{0:T(128)S(1)} %div.131) | copy-start | bytes 1540
  62.6 38.8 %copy-start.45 = (f32[128]{0:T(128)}, f32[128]{0:T(128)S(1)}, u32[]{:S(2)}) copy-start(f32[128]{0:T(128)S(1)} %div.132) | copy-start | bytes 1540
  62.6 15.9 %copy-start.34 = (f32[8,8,128]{2,1,0:T(8,128)}, f32[8,8,128]{2,1,0:T(8,128)S(1)}, u32[]{:S(2)}) copy-start(f32[8,8,128]{2,1,0:T(8,128)S(1)} %copy.236) | copy-start | bytes 98308
  63.1 40.6 %copy-start.16 = (f32[128,128,1]{1,0,2:T(8,128)}, f32[128,128,1]{1,0,2:T(8,128)S(1)}, u32[]{:S(2)}) copy-start(f32[128,128,1]{1,0,2:T(8,128)S(1)} %reshape.1970) | copy-start | bytes 196612
  66.0 7.7 %collective-permute-start.2 = (f32[4,10,1,128]{3,1,2,0:T(8,128)S(1)}, f32[4,10,1,128]{3,1,2,0:T(8,128)S(1)}, u32[]{:S(2)}, u32[]{:S(2)}) collective-permute-start(f32[4,10,1,128]{3,1,2,0:T(8,128)S(1)} %get-tuple-element.96), channel_id=1, source_target_pairs={{0,1},{1,2},{2,3},{3,4},{4,5},{5,6},{6,7},{7,8},{8,9},{9,10},{10,1... | collective-permute-start | bytes 61448 | tf_op jit(solution)/shard_map/ppermute | solution.py:40
  69.7 5.2 collective-permute-start.3
  79.5 638.1 %copy-start.22 = (f32[4,8,8,128]{3,2,1,0:T(8,128)}, f32[4,8,8,128]{3,2,1,0:T(8,128)S(1)}, u32[]{:S(2)}) copy-start(f32[4,8,8,128]{3,2,1,0:T(8,128)S(1)} %fusion.4) | copy-start | bytes 393220
  80.8 6.5 collective-permute-start.4
  82.7 5.3 collective-permute-start.5
  88.0 10.5 %collective-permute-start.6 = (f32[1,10,1,128]{3,1,2,0:T(8,128)S(1)}, f32[1,10,1,128]{3,1,2,0:T(8,128)S(1)}, u32[]{:S(2)}, u32[]{:S(2)}) collective-permute-start(f32[1,10,1,128]{3,1,2,0:T(8,128)S(1)} %get-tuple-element.154), channel_id=1, source_target_pairs={{0,1},{1,2},{2,3},{3,4},{4,5},{5,6},{6,7},{7,8},{8,9},{9,10},{10,1... | collective-permute-start | bytes 15368 | tf_op jit(solution)/shard_map/ppermute | solution.py:40
  91.1 8.2 %collective-permute-start.7 = (f32[1,10,1,128]{3,1,2,0:T(8,128)S(1)}, f32[1,10,1,128]{3,1,2,0:T(8,128)S(1)}, u32[]{:S(2)}, u32[]{:S(2)}) collective-permute-start(f32[1,10,1,128]{3,1,2,0:T(8,128)S(1)} %get-tuple-element.155), channel_id=1, source_target_pairs={{1,0},{2,1},{3,2},{4,3},{5,4},{6,5},{7,6},{8,7},{9,8},{10,9},{11,1... | collective-permute-start | bytes 15368 | tf_op jit(solution)/shard_map/ppermute | solution.py:42
  104.0 101.4 %collective-permute-start.12 = (f32[1,1,8,128]{3,2,1,0:T(8,128)S(1)}, f32[1,1,8,128]{3,2,1,0:T(8,128)S(1)}, u32[]{:S(2)}, u32[]{:S(2)}) collective-permute-start(f32[1,1,8,128]{3,2,1,0:T(8,128)S(1)} %get-tuple-element.172), channel_id=1, source_target_pairs={{0,64},{64,128},{128,192},{192,256},{256,320},{320,384},{384,448},... | collective-permute-start | bytes 12296 | tf_op jit(solution)/shard_map/ppermute | solution.py:40
  105.9 99.4 %collective-permute-start.13 = (f32[1,1,8,128]{3,2,1,0:T(8,128)S(1)}, f32[1,1,8,128]{3,2,1,0:T(8,128)S(1)}, u32[]{:S(2)}, u32[]{:S(2)}) collective-permute-start(f32[1,1,8,128]{3,2,1,0:T(8,128)S(1)} %get-tuple-element.173), channel_id=1, source_target_pairs={{64,0},{128,64},{192,128},{256,192},{320,256},{384,320},{448,384},... | collective-permute-start | bytes 12296 | tf_op jit(solution)/shard_map/ppermute | solution.py:42
  205.4 4.4 copy-start.41
  205.4 4.6 collective-permute-start.14
  207.4 5.2 collective-permute-start.15
  216.7 6.5 collective-permute-start.16
  218.8 5.1 collective-permute-start.17
  223.9 8.1 %collective-permute-start.18 = (f32[1,10,1,128]{3,1,2,0:T(8,128)S(1)}, f32[1,10,1,128]{3,1,2,0:T(8,128)S(1)}, u32[]{:S(2)}, u32[]{:S(2)}) collective-permute-start(f32[1,10,1,128]{3,1,2,0:T(8,128)S(1)} %get-tuple-element.140), channel_id=1, source_target_pairs={{0,1},{1,2},{2,3},{3,4},{4,5},{5,6},{6,7},{7,8},{8,9},{9,10},{10,1... | collective-permute-start | bytes 15368 | tf_op jit(solution)/shard_map/ppermute | solution.py:40
  226.7 6.2 collective-permute-start.19
  353.6 94.5 %collective-permute-start.20 = (f32[1,1,8,128]{3,2,1,0:T(8,128)S(1)}, f32[1,1,8,128]{3,2,1,0:T(8,128)S(1)}, u32[]{:S(2)}, u32[]{:S(2)}) collective-permute-start(f32[1,1,8,128]{3,2,1,0:T(8,128)S(1)} %get-tuple-element.164), channel_id=1, source_target_pairs={{0,64},{64,128},{128,192},{192,256},{256,320},{320,384},{384,448},... | collective-permute-start | bytes 12296 | tf_op jit(solution)/shard_map/ppermute | solution.py:40
  355.5 92.6 %collective-permute-start.21 = (f32[1,1,8,128]{3,2,1,0:T(8,128)S(1)}, f32[1,1,8,128]{3,2,1,0:T(8,128)S(1)}, u32[]{:S(2)}, u32[]{:S(2)}) collective-permute-start(f32[1,1,8,128]{3,2,1,0:T(8,128)S(1)} %get-tuple-element.165), channel_id=1, source_target_pairs={{64,0},{128,64},{192,128},{256,192},{320,256},{384,320},{448,384},... | collective-permute-start | bytes 12296 | tf_op jit(solution)/shard_map/ppermute | solution.py:42
  448.1 4.5 collective-permute-start.22
  450.0 5.2 collective-permute-start.23
  571.2 6.5 collective-permute-start.24
  574.9 4.4 collective-permute-start.25
  579.2 5.9 collective-permute-start.26
  581.4 5.0 collective-permute-start.27
  586.7 116.1 %copy-start.11 = (f32[8,8,128]{2,1,0:T(8,128)S(1)}, f32[8,8,128]{2,1,0:T(8,128)}, u32[]{:S(2)}) copy-start(f32[8,8,128]{2,1,0:T(8,128)} %param.22) | copy-start | bytes 98308
  704.6 6.5 collective-permute-start.28
  707.1 4.9 collective-permute-start.29
  711.9 5.7 collective-permute-start.30
  713.9 5.1 collective-permute-start.31
  (61 other events, 48.5 us)
where the time goes:
time: 729 us; the launch traced here: 723 us
  blocking collectives  513 us (70%)
  starting transfers between devices  116 us (16%)
  local copies, waits for them, and re-layouts  31.3 us (4%)
  matrix products  21.6 us (3%)
  other arithmetic  18.1 us (2%)
  waiting for transfers between devices  14.3 us (2%)
  between operations  7.7 us (1%)
    psum x3, blocking collectives, inner_sum(): return lax.psum(jnp.sum(first * second / counts), ('gx', 'gy'))  340 us
    all_gather x2, blocking collectives, coarse_whole(): lax.all_gather(piece.reshape(1, rows * columns * levels), ('gx', 'gy'), a...  174 us
    ppermute x16, starting transfers between devices, padded_2(): lax.ppermute(head, axis, [((i + 1) % count, i) for i in range(count)])  73.3 us
    ppermute x16, starting transfers between devices, padded_2(): lax.ppermute(tail, axis, [(i, (i + 1) % count) for i in range(count)])  43 us
    unnamed x160, local copies, waits for them, and re-layouts  17 us
  transfers between devices with their start and end apart: 32, of which 11 were waited for; matrix products, arithmetic and copies ran while one was open for 4% of the time, Pallas kernels for 0%

commit v1 on v0

v1 whole, which is shorter than its diff:
```python
import math

import jax
import jax.numpy as jnp
import ml_dtypes
import numpy as np
from jax import lax
from jax.experimental import pallas as pl
from jax.experimental.pallas import tpu as pltpu
from jax.sharding import PartitionSpec as P

INTERPRET = False

viscosity = 0.05
time_step = 0.01
drag_strength = 20.0
heating = 40.0
buoyancy = 10.0
helmholtz_shift = 0.001
local_shift = 0.5
coarse_shift = 0.02
gll_points = (
    -1.0,
    -0.8717401485096066,
    -0.5917001814331423,
    -0.2092992179024789,
    0.2092992179024789,
    0.5917001814331423,
    0.8717401485096066,
    1.0,
)
EZ = 16
NZ = 128
NV = 17


def legendre_seven(points):
    squared = points * points
    return points * (((429.0 * squared - 693.0) * squared + 315.0) * squared - 35.0) / 16.0


def jacobi_eigen(matrix):
    current = np.array(matrix)
    basis = np.eye(8)
    for rounds in range(12):
        for first in range(7):
            for second in range(first + 1, 8):
                angle = 0.5 * math.atan2(
                    2.0 * float(current[first, second]),
                    float(current[second, second] - current[first, first]),
                )
                cosine = math.cos(angle)
                sine = math.sin(angle)
                rotation = np.eye(8)
                rotation[first, first] = cosine
                rotation[second, second] = cosine
                rotation[first, second] = sine
                rotation[second, first] = -sine
                current = rotation.T @ current @ rotation
                basis = basis @ rotation
    return (np.sum(current * np.eye(8), axis=0), basis)


def gll_tables():
    nodes = np.array(gll_points)
    values = legendre_seven(nodes)
    weights = 2.0 / (56.0 * values * values)
    differ = nodes[:, None] - nodes[None, :] + np.eye(8)
    derivative = values[:, None] / values[None, :] / differ * (1.0 - np.eye(8))
    ends = np.array([-14.0, 0.0, 0.0, 0.0, 0.0, 0.0, 0.0, 14.0])
    derivative = derivative + np.eye(8) * ends[None, :]
    stiffness = derivative.T @ (weights[:, None] * derivative)
    scaled = stiffness / np.sqrt(np.outer(weights, weights))
    scaled = 0.5 * (scaled + scaled.T)
    eigen_values, eigen_vectors = jacobi_eigen(scaled)
    eigen_basis = eigen_vectors / np.sqrt(weights)[:, None]
    return (nodes, weights, derivative, eigen_basis, np.maximum(eigen_values, 0.0))


def parts(table):
    table = np.asarray(table, np.float32)
    high = table.astype(ml_dtypes.bfloat16)
    low = (table - high.astype(np.float32)).astype(ml_dtypes.bfloat16)
    return high, low


def parts_three(table):
    high, low = parts(table)
    rest = np.asarray(table, np.float64) - high.astype(np.float64) - low.astype(np.float64)
    return high, low, rest.astype(ml_dtypes.bfloat16)


def left5(table):
    high, low, rest = parts_three(table)
    return np.concatenate([high, high, low, low, rest], axis=1)


def right5(table):
    high, low, rest = parts_three(table)
    return np.concatenate([high, high, low, low, rest], axis=0)


def left3(table):
    high, low = parts(table)
    return np.concatenate([high, high, low], axis=1)


def right3(table):
    high, low = parts(table)
    return np.concatenate([high, high, low], axis=0)


def split(field):
    high = field.astype(jnp.bfloat16)
    low = (field - high.astype(jnp.float32)).astype(jnp.bfloat16)
    return high, low


def stacked(field, terms, axis):
    high, low = split(field)
    order = [high, low, high, low, high] if terms == 5 else [high, low, high]
    return jnp.concatenate(order, axis=axis)


def lmul(table, field):
    terms = table.shape[1] // field.shape[0]
    return jnp.dot(table, stacked(field, terms, 0), preferred_element_type=jnp.float32)


def rmul(field, table):
    terms = table.shape[0] // field.shape[1]
    return jnp.dot(stacked(field, terms, 1), table, preferred_element_type=jnp.float32)


def lanes_of(field, size=64):
    return jnp.concatenate(
        [field[k * size : (k + 1) * size] for k in range(field.shape[0] // size)], axis=1
    )


def rows_of(field):
    return jnp.concatenate(
        [field[:, k * NZ : (k + 1) * NZ] for k in range(field.shape[1] // NZ)], axis=0
    )


def lane_index(rows):
    return lax.broadcasted_iota(jnp.int32, (rows, NZ), 1)


def turn(field, shift):
    return pltpu.roll(field, shift % NZ, 1)


def join_z(field):
    lane = lane_index(field.shape[0])
    ahead = jnp.where((lane % 8 == 7) & (lane < NZ - 1), turn(field, -1), 0.0)
    behind = jnp.where((lane % 8 == 0) & (lane > 0), turn(field, 1), 0.0)
    return field + ahead + behind


def join_x(rows, count):
    blocks = [rows[k * 64 : (k + 1) * 64] for k in range(count)]
    sums = [blocks[k][0:8] + blocks[(k - 1) % count][56:64] for k in range(count)]
    pieces = []
    for k in range(count):
        pieces += [sums[k], blocks[k][8:56], sums[(k + 1) % count]]
    return jnp.concatenate(pieces, axis=0)


def fold(field):
    return jnp.sum(field.reshape(field.shape[0] // 8, 8, NZ), axis=0)


def total(field):
    return jnp.sum(jnp.sum(field, axis=0, keepdims=True), axis=1, keepdims=True)


def tiled(table, count):
    return jnp.concatenate([table] * count, axis=0)


class Tables:
    def __init__(self, nx, ny):
        nodes, w, d, e, lam = gll_tables()
        self.nx, self.ny = nx, ny
        eye8 = np.eye(8)
        kx = d.T @ (w[:, None] * d)
        bx = np.diag(w)
        eyez = np.eye(EZ)
        join = np.eye(NZ)
        for k in range(EZ - 1):
            join[8 * k + 7, 8 * k + 8] = 1.0
            join[8 * k + 8, 8 * k + 7] = 1.0
        dz_t = np.kron(eyez, d).T
        kz_t = np.kron(eyez, kx).T
        wz = np.tile(w, EZ)
        wxy = np.kron(w, w)
        mz = join.sum(axis=1)
        m1 = np.array([2.0, 1, 1, 1, 1, 1, 1, 2.0])
        mxy = np.kron(m1, m1)
        f32 = np.float32
        mass = np.outer(wxy, wz)
        self.mass = mass.astype(f32)
        self.wz = np.broadcast_to(wz[None, :], (64, NZ)).astype(f32)
        self.wxy = np.broadcast_to(wxy[:, None], (64, NZ)).astype(f32)
        self.inv_bm = (1.0 / (mass * np.outer(mxy, mz))).astype(f32)
        self.inv_m = (1.0 / np.outer(mxy, mz)).astype(f32)
        self.inv_mz = np.broadcast_to(1.0 / mz[None, :], (64, NZ)).astype(f32)
        self.visc = np.stack([self.mass, self.wz, self.wxy]).reshape(192, NZ)
        dx = np.kron(d, eye8)
        dy = np.kron(eye8, d)
        lv = np.kron(kx, bx) + np.kron(bx, kx)
        self.k1_left = left5(np.concatenate([dx, dy, lv], axis=0))
        self.k1_right = right5(np.concatenate([dz_t, kz_t], axis=1))
        self.div_left = left5(np.concatenate([dx, dy], axis=1))
        self.dz_right = right5(dz_t)
        hx = np.stack([(1.0 - nodes) / 2.0, (1.0 + nodes) / 2.0])
        self.hx = hx
        hz = np.zeros((NZ, NV))
        for z in range(NZ):
            hz[z, z // 8] = hx[0, z % 8]
            hz[z, z // 8 + 1] = hx[1, z % 8]
        pxy = np.zeros((8, 64))
        for xv in range(2):
            for yv in range(2):
                pxy[xv * 2 + yv] = np.kron(hx[xv], hx[yv])
        self.pxy_left = left3(pxy)
        hzm = np.zeros((NZ, NZ))
        hzm[:, :NV] = hz / mz[:, None]
        self.hzm_right = right3(hzm)
        self.hy = np.broadcast_to(hx.reshape(16, 1), (16, NZ)).astype(f32)

        def hartley(count):
            angle = 2.0 * np.pi / count * np.outer(np.arange(count), np.arange(count))
            return (np.cos(angle) + np.sin(angle)) / np.sqrt(count)

        self.hart_x = hartley(nx)
        hart_y = hartley(ny)
        ex = 2.0 - 2.0 * np.cos(2.0 * np.pi / nx * np.arange(nx))
        ey = 2.0 - 2.0 * np.cos(2.0 * np.pi / ny * np.arange(ny))
        ez = 2.0 - 2.0 * np.cos(np.pi / NV * np.arange(NV))
        levels = np.arange(NV)
        norms = np.where(levels == 0, np.sqrt(1.0 / NV), np.sqrt(2.0 / NV))
        cz = np.cos(np.pi / NV * np.outer(levels + 0.5, levels)) * norms[None, :]
        inverse = 1.0 / (
            2.0 * (ex[:, None, None] + ey[None, :, None] + ez[None, None, :]) + coarse_shift
        )
        shifted = np.roll(hart_y, -1, axis=1)
        self.hart_cat = left3(np.concatenate([hart_y, shifted], axis=1))
        self.hart_two = left3(np.concatenate([hart_y, shifted], axis=0))
        hb = ny // 2
        self.hb = hb
        coef = np.zeros((nx * nx, NZ))
        for a in range(nx):
            for i in range(nx):
                for base in (0, 64):
                    coef[a * nx + i, base : base + NV] = self.hart_x[a, i]
                    coef[a * nx + i, base + NV : base + 2 * NV] = self.hart_x[a, (i + 1) % nx]
        self.coef = coef.astype(f32)
        twin = np.zeros((NZ, NZ))
        twin[:NV, :NV] = cz
        twin[64 : 64 + NV, 64 : 64 + NV] = cz
        self.twin_right = right3(twin)
        packed = np.zeros((nx, hb, NZ))
        packed[:, :, :NV] = inverse[:, :hb]
        packed[:, :, 64 : 64 + NV] = inverse[:, hb:]
        self.inv_packed = packed.reshape(nx * hb, NZ).astype(f32)
        near = np.zeros((ny, 16, hb))
        for j in range(ny):
            for yv in range(2):
                row = hart_y[(j + yv) % ny]
                near[j, yv] = row[:hb]
                near[j, 8 + yv] = row[hb:]
        self.near = np.stack([left3(block) for block in near])
        czh = np.zeros((NZ, NZ))
        czh[:NV] = (hz @ cz).T
        self.czh_right = right3(czh)
        self.et_left = left3(np.kron(e.T, e.T))
        self.e_left = left3(np.kron(e, e))
        self.et_right = right3(np.kron(eyez, e))
        self.e_right = right3(np.kron(eyez, e.T) @ join)
        lxy = (lam[:, None] + lam[None, :]).reshape(64)
        self.scale = (1.0 / (lxy[:, None] + np.tile(lam, EZ)[None, :] + local_shift)).astype(f32)
        self.a_left = left5(lv + helmholtz_shift * np.kron(bx, bx))
        self.a_right = right5(np.concatenate([wz[:, None] * join, kz_t @ join], axis=0))
        back = np.zeros((32, nx * 8))
        for yv in range(2):
            for a in range(nx):
                for i in range(nx):
                    back[yv * 16 + a, i * 8 : i * 8 + 8] = self.hart_x[a, i] * hx[yv]
        self.back_left = left3(back)
        hzc = np.zeros((NZ, NZ))
        hzc[:, :NV] = (hz / mz[:, None]) @ cz
        self.hzc_right = right3(hzc)
        self.edge_left = left3(np.concatenate([np.kron(eye8, d[:1]), np.kron(eye8, d[7:])], axis=0))
        wide = np.zeros((ny, nx, NZ))
        wide[:, :, :NV] = inverse.transpose(1, 0, 2)
        self.inv_wide = wide.reshape(ny, nx * NZ).astype(f32)
        around = np.zeros((ny, 8, ny))
        for j in range(ny):
            for yv in range(4):
                around[j, yv] = hart_y[(j + yv - 1) % ny]
        self.around = np.stack([left3(block) for block in around])
        reach = np.zeros((nx, 4, nx))
        for i in range(nx):
            for xv in range(4):
                reach[i, xv] = self.hart_x[(i + xv - 1) % nx]
        self.reach = reach.reshape(-1).astype(f32)
        second = np.diag(2.0 * np.ones(NV)) - np.eye(NV, k=1) - np.eye(NV, k=-1)
        second[0, 0] = second[-1, -1] = 1.0
        double = 2.0 * np.ones(NV)
        double[0] = double[-1] = 1.0
        mass_z = np.diag(double) - second / 3.0
        both = np.zeros((NZ, 2 * NZ))
        both[:NV, :NV] = cz.T @ mass_z @ cz
        both[:NV, NZ : NZ + NV] = cz.T @ (second / 2.0) @ cz
        self.galerkin_right = right3(both)
        self.mx = 2.0 - ex / 3.0
        self.kx = ex / 2.0
        my = np.broadcast_to((2.0 - ey / 3.0)[:, None], (ny, NZ))
        ky = np.broadcast_to((ey / 2.0)[:, None], (ny, NZ))
        self.mky = np.concatenate([my, ky], axis=0).astype(f32)
        self.last_left = left5(np.concatenate([dx, dy], axis=0))
        self.d = d


def call(kernel, outs, *args, scratch=(), smem=0):
    specs = [pl.BlockSpec(memory_space=pltpu.SMEM)] * smem
    specs += [pl.BlockSpec(memory_space=pltpu.VMEM)] * (len(args) - smem)
    return pl.pallas_call(
        kernel,
        out_shape=[jax.ShapeDtypeStruct(shape, jnp.float32) for shape in outs],
        in_specs=specs,
        out_specs=[pl.BlockSpec(memory_space=pltpu.VMEM)] * len(outs),
        scratch_shapes=list(scratch),
        interpret=INTERPRET,
        name=kernel.__name__,
    )(*args)


def stage_rate(h, flow, old, left, right, tab, fld, xf0, xf7, kp):
    f = [flow[q * 64 : q * 64 + 64] for q in range(4)]
    p = old[...]
    lx = lmul(left[...], jnp.concatenate(f + [p], axis=1))
    rx = rmul(jnp.concatenate(f + [p], axis=0), right[...])
    mass, wz, wxy = tab[0:64], tab[64:128], tab[128:192]
    u, v, w, theta = f
    drag = drag_strength * jnp.sqrt(u * u + v * v + w * w)
    canopy = (lane_index(64) // 8 < h[0, 0]).astype(jnp.float32)
    drag = drag * canopy
    forcing = [-drag * u, -drag * v, -drag * w + buoyancy * theta, heating * canopy]
    for q in range(5):
        lane = slice(q * NZ, q * NZ + NZ)
        rows = slice(q * 64, q * 64 + 64)
        gx, gy, lv = lx[0:64, lane], lx[64:128, lane], lx[128:192, lane]
        gz, kz = rx[rows, 0:NZ], rx[rows, NZ : 2 * NZ]
        stiff = lv * wz + wxy * kz
        if q < 4:
            rate = mass * (forcing[q] - (u * gx + v * gy + w * gz)) - viscosity * stiff
            fld[rows] = join_z(rate)
        else:
            kp[...] = stiff + helmholtz_shift * mass * p
            for k, grad in enumerate((gx, gy, gz)):
                fld[(4 + k) * 64 : (5 + k) * 64] = join_z(mass * grad)
    for q in range(7):
        xf0[q * 8 : q * 8 + 8] = fld[q * 64 : q * 64 + 8]
        xf7[q * 8 : q * 8 + 8] = fld[q * 64 + 56 : q * 64 + 64]


def stage_faces(fld, below, above, out, yf0, yf7):
    for q in range(7):
        base = q * 64
        out[base : base + 8] = fld[base : base + 8] + below[q * 8 : q * 8 + 8]
        out[base + 8 : base + 56] = fld[base + 8 : base + 56]
        out[base + 56 : base + 64] = fld[base + 56 : base + 64] + above[q * 8 : q * 8 + 8]
    yf0[...] = out[pl.ds(0, 56, stride=8), :]
    yf7[...] = out[pl.ds(7, 56, stride=8), :]


def add_faces(ref, below, above):
    count = ref.shape[0] // 8
    ref[pl.ds(0, count, stride=8), :] = ref[pl.ds(0, count, stride=8), :] + below
    ref[pl.ds(7, count, stride=8), :] = ref[pl.ds(7, count, stride=8), :] + above


def make_stages(t):
    nx, ny, hb = t.nx, t.ny, t.hb

    def stage_state(
        idx, fx, below, above, flow, kp, tab, dleft, dright, pleft, hright, prov, g0, rz, msg, scr
    ):
        scr[...] = fx[...]
        add_faces(scr, below[...], above[...])
        mass, inv_bm = tab[0:64], tab[64:128]
        lane = lane_index(64)
        new = []
        for q in range(4):
            rows = slice(q * 64, q * 64 + 64)
            value = flow[rows] + time_step * scr[rows] * inv_bm
            if q == 2:
                value = jnp.where((lane == 0) | (lane == NZ - 1), 0.0, value)
            prov[rows] = value
            new.append(value)
        for k in range(3):
            g0[k * 64 : k * 64 + 64] = scr[(4 + k) * 64 : (5 + k) * 64] * inv_bm
        div = lmul(dleft[...], jnp.concatenate(new[:2], axis=0)) + rmul(new[2], dright[...])
        joined = join_z(-mass * div - kp[...])
        rz[...] = joined
        coarse = rmul(lmul(pleft[...], joined), hright[...])
        face0 = rz[pl.ds(0, 8, stride=8), :]
        face7 = rz[pl.ds(7, 8, stride=8), :]
        for k in range(ny):
            msg[k * 16 : k * 16 + 8] = face0
            msg[k * 16 + 8 : k * 16 + 16] = coarse
        after = lax.rem(idx[1] + 1, ny)
        msg[pl.ds(pl.multiple_of(after * 16, 16), 8), :] = face7

    def stage_residual(idx, rec, rz, hart, out):
        out[0:64] = rz[...]
        before = lax.rem(idx[1] + ny - 1, ny)
        after = lax.rem(idx[1] + 1, ny)
        below = rec[pl.ds(pl.multiple_of(before * 16, 16), 8), :]
        above = rec[pl.ds(pl.multiple_of(after * 16, 16), 8), :]
        out[pl.ds(0, 8, stride=8), :] = out[pl.ds(0, 8, stride=8), :] + below
        out[pl.ds(7, 8, stride=8), :] = out[pl.ds(7, 8, stride=8), :] + above
        m = [rec[pl.ds(8 + r, ny, stride=16), :] for r in range(4)]
        top = m[0] + turn(m[2], NV)
        low = m[1] + turn(m[3], NV)
        modes = lmul(hart[...], jnp.concatenate([top, low], axis=0))
        out[64 : 64 + hb] = modes[0:hb] + turn(modes[hb:ny], 64)

    def smoothed(field, etl, etr, sc, er, el):
        modal = rmul(rows_of(lmul(etl, lanes_of(field))), etr)
        modal = rmul(modal * tiled(sc, nx), er)
        return rows_of(lmul(el, lanes_of(modal)))

    def stage_smooth(ring, etl, etr, sc, er, el, r0, s, s0, s7):
        size = 64 + hb
        rows = jnp.concatenate([ring[i * size : i * size + 64] for i in range(nx)], axis=0)
        residual = join_x(rows, nx)
        r0[...] = residual
        s[...] = join_x(smoothed(residual, etl[...], etr[...], sc[...], er[...], el[...]), nx)
        s0[...] = s[pl.ds(0, nx * 8, stride=8), :]
        s7[...] = s[pl.ds(7, nx * 8, stride=8), :]

    def stage_coarse(idx, ring, coef, twin, inv, near, czh, out):
        size = 64 + hb
        grid = [ring[i * size + 64 : (i + 1) * size] for i in range(nx)]
        modes = []
        for a in range(nx):
            acc = grid[0] * coef[a * nx : a * nx + 1]
            for i in range(1, nx):
                acc = acc + grid[i] * coef[a * nx + i : a * nx + i + 1]
            modes.append(acc + turn(acc, -NV))
        values = rmul(jnp.concatenate(modes, axis=0), twin[...]) * inv[...]
        pair = lmul(near[idx[1]], lanes_of(values, hb))
        lines = []
        for a in range(nx):
            tile = pair[:, a * NZ : (a + 1) * NZ]
            lines.append(tile[0:8] + turn(tile[8:16], 64))
        columns = []
        for i in range(nx):
            acc = lines[0] * float(t.hart_x[i, 0])
            for a in range(1, nx):
                acc = acc + lines[a] * float(t.hart_x[i, a])
            columns.append(acc)
        out[...] = rmul(jnp.concatenate(columns, axis=0), czh[...])

    def applied(field, al, wxy, ar):
        side = rows_of(lmul(al, lanes_of(field)))
        return rmul(jnp.concatenate([side, field * tiled(wxy, nx)], axis=1), ar)

    def restricted(field, back, hzc):
        columns = []
        for i in range(nx):
            acc = None
            for x in range(8):
                here = field[i * 64 + x * 8 : i * 64 + x * 8 + 8] * float(t.hx[0, x])
                k = (i - 1) % nx
                there = field[k * 64 + x * 8 : k * 64 + x * 8 + 8] * float(t.hx[1, x])
                acc = here + there if acc is None else acc + here + there
            columns.append(acc)
        return rmul(lmul(back, jnp.concatenate(columns, axis=0)), hzc)

    def stage_apply(
        s, below, above, vert, r0, hy, al, tab, ar, back, hzc, z0, q, q0, q7, cq, sums
    ):
        z0[...] = s[...]
        add_faces(z0, below[...], above[...])
        slabs = []
        for i in range(nx):
            slabs.append(
                hy[0:8] * vert[i * 8 : i * 8 + 1] + hy[8:16] * vert[i * 8 + 1 : i * 8 + 2]
            )
        pieces = []
        for i in range(nx):
            for x in range(8):
                pieces.append(
                    slabs[i] * float(t.hx[0, x]) + slabs[(i + 1) % nx] * float(t.hx[1, x])
                )
        field = z0[...] + jnp.concatenate(pieces, axis=0)
        z0[...] = field
        wxy, inv_m, inv_mz = tab[0:64], tab[64:128], tab[128:192]
        image = applied(field, al[...], wxy, ar[...])
        sums[0:8] = fold(r0[...] * field * tiled(inv_m, nx))
        sums[8:16] = fold(field * image * tiled(inv_mz, nx))
        cq[...] = restricted(image, back[...], hzc[...])
        q[...] = join_x(image, nx)
        q0[...] = q[pl.ds(0, nx * 8, stride=8), :]
        q7[...] = q[pl.ds(7, nx * 8, stride=8), :]

    def stage_again(q, below, above, tab, etl, etr, sc, er, el, s, s0, s7, sums, scr):
        scr[...] = q[...]
        add_faces(scr, below[...], above[...])
        field = scr[...]
        local = smoothed(field, etl[...], etr[...], sc[...], er[...], el[...])
        sums[...] = fold(field * local * tiled(tab[...], nx))
        s[...] = join_x(local, nx)
        s0[...] = s[pl.ds(0, nx * 8, stride=8), :]
        s7[...] = s[pl.ds(7, nx * 8, stride=8), :]

    def stage_gather(
        idx, s, below, above, z0, cq, sums1, sums2, al, tab, ar, back, hzc, edge, sq, msg, g0, g7
    ):
        sq[...] = s[...]
        add_faces(sq, below[...], above[...])
        field = sq[...]
        wxy, inv_mz = tab[0:64], tab[128:192]
        image = applied(field, al[...], wxy, ar[...])
        last = total(fold(field * image * tiled(inv_mz, nx)))
        tq = restricted(image, back[...], hzc[...])
        block = cq[0:16] + turn(cq[16:32], 32) + turn(tq[0:16], 64) + turn(tq[16:32], 96)
        lane = lane_index(16)
        row = lax.broadcasted_iota(jnp.int32, (16, NZ), 0)
        values = [total(sums1[0:8]), total(sums1[8:16]), total(sums2[...]), last]
        for k, value in enumerate(values):
            block = block + jnp.where((row == 12) & (lane == NV + k), value, 0.0)
        for k in range(ny):
            msg[k * 16 : k * 16 + 16] = block
        base = pl.multiple_of(idx[0] * 64, 64)
        pair = jnp.concatenate([z0[pl.ds(base, 64), :], sq[pl.ds(base, 64), :]], axis=1)
        slopes = lmul(edge[...], pair)
        g0[...] = jnp.concatenate([slopes[0:8, 0:NZ], slopes[0:8, NZ:]], axis=0)
        g7[...] = jnp.concatenate([slopes[8:16, 0:NZ], slopes[8:16, NZ:]], axis=0)

    def stage_final(
        idx,
        reach,
        rec,
        below,
        above,
        z0,
        sq,
        prov,
        g0,
        old,
        hart,
        inv,
        around,
        czh,
        gal,
        mky,
        hy,
        left,
        right,
        inv_mz,
        new,
        press,
        scr,
    ):
        cells = jnp.concatenate([rec[pl.ds(a, ny, stride=16), :] for a in range(nx)], axis=1)
        both = lmul(hart[...], cells)
        my, ky = mky[0:ny], mky[ny : 2 * ny]
        lane = lane_index(ny)
        found = []
        cross = jnp.zeros((ny, NZ), jnp.float32)
        plain = jnp.zeros((ny, NZ), jnp.float32)
        for a in range(nx):
            tile = slice(a * NZ, (a + 1) * NZ)
            comb = both[0:ny, tile] + turn(both[ny : 2 * ny, tile], -32)
            e = comb * inv[:, tile]
            found.append(e)
            plain = plain + e * comb
            cross = cross + e * turn(comb, -64)
        grown = rmul(jnp.concatenate(found, axis=0), gal[...])
        quad = jnp.zeros((ny, NZ), jnp.float32)
        for a in range(nx):
            rows = slice(a * ny, (a + 1) * ny)
            mxa, kxa = float(t.mx[a]), float(t.kx[a])
            weight_m = my * (kxa + helmholtz_shift * mxa) + ky * mxa
            weight_k = my * mxa
            quad = quad + found[a] * (
                weight_m * grown[rows, 0:NZ] + weight_k * grown[rows, NZ : 2 * NZ]
            )
        scalars = jnp.sum(rec[pl.ds(12, ny, stride=16), :], axis=0, keepdims=True)
        line = lane_index(1)

        def pick(k):
            return jnp.sum(jnp.where(line == NV + k, scalars, 0.0), axis=1, keepdims=True)

        rz0, zq0 = pick(0), pick(1)
        wq = pick(2) + total(plain)
        ww = pick(3) + 2.0 * total(cross) + total(quad)
        first = rz0 / zq0
        rz1 = rz0 - 2.0 * first * zq0 + first * first * wq
        beta = rz1 / rz0
        grow = 1.0 + beta
        curve = grow * grow * zq0 - 2.0 * grow * first * wq + first * first * ww
        second = rz1 / curve
        on_z = first + second * grow
        on_w = -second * first
        lines = lmul(around[idx[1]], jnp.concatenate(found, axis=1))
        stack = []
        for xv in range(4):
            base = (idx[0] * 4 + xv) * nx
            acc = lines[:, 0:NZ] * reach[base]
            for a in range(1, nx):
                acc = acc + lines[:, a * NZ : (a + 1) * NZ] * reach[base + a]
            stack.append(acc)
        scr[...] = rmul(jnp.concatenate(stack, axis=0), czh[...]) * on_w
        hy0, hy1 = hy[0:8], hy[8:16]
        slabs = [hy0 * scr[k * 8 + 1 : k * 8 + 2] + hy1 * scr[k * 8 + 2 : k * 8 + 3] for k in range(4)]
        coarse = jnp.concatenate(
            [slabs[1] * float(t.hx[0, x]) + slabs[2] * float(t.hx[1, x]) for x in range(8)], axis=0
        )

        def own(shift):
            base = pl.multiple_of(lax.rem(idx[0] + shift + nx, nx) * 64, 64)
            return z0[pl.ds(base, 64), :] * on_z + sq[pl.ds(base, 64), :] * on_w

        change = own(0) + coarse
        press[...] = old[...] + change
        slopes = lmul(left[...], change)
        gx, gy = slopes[0:64], slopes[64:128]
        gz = rmul(change, right[...])
        prior, later = own(-1), own(1)
        edge0 = 0.5 * (slabs[1] - slabs[0])
        edge7 = 0.5 * (slabs[3] - slabs[2])
        for x in range(8):
            edge0 = edge0 + prior[x * 8 : x * 8 + 8] * float(t.d[7, x])
            edge7 = edge7 + later[x * 8 : x * 8 + 8] * float(t.d[0, x])
        new[0:8] = prov[0:8] - g0[0:8] - 0.5 * (gx[0:8] + edge0)
        new[8:56] = prov[8:56] - g0[8:56] - gx[8:56]
        new[56:64] = prov[56:64] - g0[56:64] - 0.5 * (gx[56:64] + edge7)
        hx0, hx1 = hy0, hy1
        line1 = [scr[k * 8 + 1 : k * 8 + 2] for k in range(4)]
        step0 = [0.5 * (scr[k * 8 + 1 : k * 8 + 2] - scr[k * 8 : k * 8 + 1]) for k in (1, 2)]
        step7 = [0.5 * (scr[k * 8 + 3 : k * 8 + 4] - scr[k * 8 + 2 : k * 8 + 3]) for k in (1, 2)]
        under = below[0:8] * on_z + below[8:16] * on_w + hx0 * step0[0] + hx1 * step0[1]
        over = above[0:8] * on_z + above[8:16] * on_w + hx0 * step7[0] + hx1 * step7[1]
        press_y = gy
        new[64:128] = press_y
        own0 = new[pl.ds(64, 8, stride=8), :]
        own7 = new[pl.ds(71, 8, stride=8), :]
        new[pl.ds(64, 8, stride=8), :] = 0.5 * (own0 + under)
        new[pl.ds(71, 8, stride=8), :] = 0.5 * (own7 + over)
        new[64:128] = prov[64:128] - g0[64:128] - new[64:128]
        new[128:192] = prov[128:192] - g0[128:192] - join_z(gz) * inv_mz[...]
        new[192:256] = prov[192:256]

    return (
        stage_state,
        stage_residual,
        stage_smooth,
        stage_coarse,
        stage_apply,
        stage_again,
        stage_gather,
        stage_final,
    )


def exchange(axis, first, last):
    count = lax.axis_size(axis)
    below = lax.ppermute(last, axis, [(k, (k + 1) % count) for k in range(count)])
    above = lax.ppermute(first, axis, [((k + 1) % count, k) for k in range(count)])
    return below, above


def make_device(t):
    nx, ny, hb = t.nx, t.ny, t.hb
    (
        stage_state,
        stage_residual,
        stage_smooth,
        stage_coarse,
        stage_apply,
        stage_again,
        stage_gather,
        stage_final,
    ) = make_stages(t)
    c = jnp.asarray
    col, ring, face = (64, NZ), (nx * 64, NZ), (nx * 8, NZ)

    def on_device(flow_state, building_height, pressure_old):
        flow = flow_state.reshape(256, NZ)
        old = pressure_old.reshape(64, NZ)
        idx = jnp.stack([lax.axis_index("gx"), lax.axis_index("gy")]).astype(jnp.int32)
        fld, xf0, xf7, kp = call(
            stage_rate,
            [(448, NZ), (56, NZ), (56, NZ), col],
            building_height,
            flow,
            old,
            c(t.k1_left),
            c(t.k1_right),
            c(t.visc),
            smem=1,
        )
        below, above = exchange("gx", xf0, xf7)
        fld, yf0, yf7 = call(
            stage_faces, [(448, NZ), (56, NZ), (56, NZ)], fld, below, above
        )
        below, above = exchange("gy", yf0, yf7)
        prov, g0, rz, msg = call(
            stage_state,
            [(256, NZ), (192, NZ), col, (ny * 16, NZ)],
            idx,
            fld,
            below,
            above,
            flow,
            kp,
            c(np.concatenate([t.mass, t.inv_bm])),
            c(t.div_left),
            c(t.dz_right),
            c(t.pxy_left),
            c(t.hzm_right),
            smem=1,
            scratch=[pltpu.VMEM((448, NZ), jnp.float32)],
        )
        rec = lax.all_to_all(msg.reshape(ny, 16, NZ), "gy", 0, 0, tiled=True)
        (piece,) = call(
            stage_residual,
            [(64 + hb, NZ)],
            idx,
            rec.reshape(ny * 16, NZ),
            rz,
            c(t.hart_cat),
            smem=1,
        )
        whole = lax.all_gather(piece, "gx", axis=0, tiled=True)
        smoother = (c(t.et_left), c(t.et_right), c(t.scale), c(t.e_right), c(t.e_left))
        r0, s, s0, s7 = call(stage_smooth, [ring, ring, face, face], whole, *smoother)
        below, above = exchange("gy", s0, s7)
        (vert,) = call(
            stage_coarse,
            [face],
            idx,
            whole,
            c(t.coef),
            c(t.twin_right),
            c(t.inv_packed),
            c(t.near),
            c(t.czh_right),
            smem=1,
        )
        tab = c(np.concatenate([t.wxy, t.inv_m, t.inv_mz]))
        operator = (c(t.a_left), tab, c(t.a_right), c(t.back_left), c(t.hzc_right))
        z0, q, q0, q7, cq, sums1 = call(
            stage_apply,
            [ring, ring, face, face, (32, NZ), (16, NZ)],
            s,
            below,
            above,
            vert,
            r0,
            c(t.hy),
            *operator,
        )
        below, above = exchange("gy", q0, q7)
        s, s0, s7, sums2 = call(
            stage_again,
            [ring, face, face, (8, NZ)],
            q,
            below,
            above,
            c(t.inv_mz),
            *smoother,
            scratch=[pltpu.VMEM(ring, jnp.float32)],
        )
        below, above = exchange("gy", s0, s7)
        sq, msg, e0, e7 = call(
            stage_gather,
            [ring, (ny * 16, NZ), (16, NZ), (16, NZ)],
            idx,
            s,
            below,
            above,
            z0,
            cq,
            sums1,
            sums2,
            *operator,
            c(t.edge_left),
            smem=1,
        )
        below, above = exchange("gy", e0, e7)
        rec = lax.all_to_all(msg.reshape(ny, 16, NZ), "gy", 0, 0, tiled=True)
        new, press = call(
            stage_final,
            [(256, NZ), col],
            idx,
            c(t.reach),
            rec.reshape(ny * 16, NZ),
            below,
            above,
            z0,
            sq,
            prov,
            g0,
            old,
            c(t.hart_two),
            c(t.inv_wide),
            c(t.around),
            c(t.czh_right),
            c(t.galerkin_right),
            c(t.mky),
            c(t.hy),
            c(t.last_left),
            c(t.dz_right),
            c(t.inv_mz),
            smem=2,
            scratch=[pltpu.VMEM((32, NZ), jnp.float32)],
        )
        return new.reshape(flow_state.shape), press.reshape(pressure_old.shape)

    return on_device


def solution(mesh):
    t = Tables(mesh.shape["gx"], mesh.shape["gy"])
    in_specs = (P(None, "gx", "gy", None), P("gx", "gy"), P("gx", "gy", None))
    out_specs = (P(None, "gx", "gy", None), P("gx", "gy", None))
    return jax.shard_map(
        make_device(t), mesh=mesh, in_specs=in_specs, out_specs=out_specs, check_vma=False
    )
```

time: 729 us -> 173 us (0.24)
  blocking collectives: 513 us -> 51.1 us
  starting transfers between devices: 116 us -> 68.7 us
  local copies, waits for them, and re-layouts: 31.3 us -> 3.9 us
  Pallas kernels: 0 us -> 27.3 us
  matrix products: 21.6 us -> 0 us
  other arithmetic: 18.1 us -> 0.58 us
    psum x3 -> x0, blocking collectives: 340 us -> none  [inner_sum(): return lax.psum(jnp.sum(first * second / counts), ('gx', 'gy'))]
    all_gather x2 -> x1, blocking collectives: 174 us -> 23.3 us  [on_device(): whole = lax.all_gather(piece, 'gx', axis=0, tiled=True)]
    ppermute x32 -> x12, starting transfers between devices: 116 us -> 55.7 us  [the longest x6 29.8 us: exchange(): lax.ppermute(first, axis, [((k + 1) % count, k) for k in range(count)])]
    all_to_all x0 -> x1, blocking collectives: none -> 27.8 us  [on_device(): rec = lax.all_to_all(msg.reshape(ny, 16, NZ), 'gy', 0, 0, tiled=True)]
    pallas_call x0 -> x10, Pallas kernels: none -> 27.3 us  [call(): pl.pallas_call(kernel, out_shape=[jax.ShapeDtypeStruct(shape, jnp.float32...]
    dot_general x74 -> x0, matrix products: 21.6 us -> none  [the longest x14 4.46 us: along_z(): return jnp.dot(rows, banded.T, precision=HIGHEST).reshape(field.shape)]
    unnamed x160 -> x30, local copies, waits for them, and re-layouts: 17 us -> 3.9 us
    all_to_all x0 -> x1, starting transfers between devices: none -> 13 us  [on_device(): rec = lax.all_to_all(msg.reshape(ny, 16, NZ), 'gy', 0, 0, tiled=True)]
  transfers between devices with their start and end apart: 32 -> 13, of which waited for: 11 -> 8; matrix products, arithmetic and copies ran while one was open for 4% -> 0% of each run, Pallas kernels for 0% -> 2%
where the time goes in v1:
time: 173 us
  starting transfers between devices  68.7 us (40%)
  blocking collectives  51.1 us (30%)
  Pallas kernels  27.3 us (16%)
  waiting for transfers between devices  19.5 us (11%)
  local copies, waits for them, and re-layouts  3.9 us (2%)
    ppermute x6, starting transfers between devices, exchange(): lax.ppermute(first, axis, [((k + 1) % count, k) for k in range(count)])  29.8 us
    all_to_all x1, blocking collectives, on_device(): rec = lax.all_to_all(msg.reshape(ny, 16, NZ), 'gy', 0, 0, tiled=True)  27.8 us
    pallas_call x10, Pallas kernels, call(): pl.pallas_call(kernel, out_shape=[jax.ShapeDtypeStruct(shape, jnp.float32...  27.3 us
    ppermute x6, starting transfers between devices, exchange(): lax.ppermute(last, axis, [(k, (k + 1) % count) for k in range(count)])  25.9 us
    all_gather x1, blocking collectives, on_device(): whole = lax.all_gather(piece, 'gx', axis=0, tiled=True)  23.3 us
    all_to_all x1, starting transfers between devices, on_device(): rec = lax.all_to_all(msg.reshape(ny, 16, NZ), 'gy', 0, 0, tiled=True)  13 us
    ppermute x6, waiting for transfers between devices, exchange(): lax.ppermute(first, axis, [((k + 1) % count, k) for k in range(count)])  12.4 us
    unnamed x30, local copies, waits for them, and re-layouts  3.9 us
  transfers between devices with their start and end apart: 13, of which 8 were waited for; matrix products, arithmetic and copies ran while one was open for 0% of the time, Pallas kernels for 2%

profile of v1, /device:TPU:1, one launch (start us, length us, event | category | flops | bytes accessed | tf_op | source)
XLA Modules:
  0.0 172.6 jit_solution(16412563465198409696)
XLA Ops:
  1.3 2.4 %stage_rate.1 = (f32[448,128]{1,0:T(8,128)}, f32[56,128]{1,0:T(8,128)}, f32[56,128]{1,0:T(8,128)}, f32[64,128]{1,0:T(8,128)}) custom-call(s32[1,1]{1,0:T(1,128)S(6)} %copy.39.h, f32[256,128]{1,0:T(8,128)} %bitcast.14, f32[64,128]{1,0:T(8,128)} %bitcast.16, bf16[192,320]{1,0:T(8,128)(2,1)} %constant.76.clone.left, bf16[640,256]{1,0:T(8,128)(2,1)} %constant.77.clone.right, ...), custom_call_target="tpu_custom_call" | custom-call | tf_op jit(solution)/shard_map/stage_rate/pallas_call | solution.py:331
  3.6 4.8 %collective-permute-start = (f32[56,128]{1,0:T(8,128)}, f32[56,128]{1,0:T(8,128)S(1)}, u32[]{:S(2)}, u32[]{:S(2)}) collective-permute-start(f32[56,128]{1,0:T(8,128)} %get-tuple-element.34), channel_id=1, source_target_pairs={{0,64},{64,128},{128,192},{192,256},{256,320},{320,384},{384,448},... | collective-permute-start | bytes 86024 | tf_op jit(solution)/shard_map/ppermute | solution.py:676
  8.5 12.2 %collective-permute-start.1 = (f32[56,128]{1,0:T(8,128)}, f32[56,128]{1,0:T(8,128)S(1)}, u32[]{:S(2)}, u32[]{:S(2)}) collective-permute-start(f32[56,128]{1,0:T(8,128)} %get-tuple-element.35), channel_id=1, source_target_pairs={{64,0},{128,64},{192,128},{256,192},{320,256},{384,320},{448,384},... | collective-permute-start | bytes 86024 | tf_op jit(solution)/shard_map/ppermute | solution.py:677
  20.7 0.0 collective-permute-done.below
  20.7 1.1 collective-permute-done.1.above
  21.9 0.6 copy-done.8
  22.5 1.7 stage_faces.1
  24.2 4.6 %collective-permute-start.2 = (f32[56,128]{1,0:T(8,128)}, f32[56,128]{1,0:T(8,128)S(1)}, u32[]{:S(2)}, u32[]{:S(2)}) collective-permute-start(f32[56,128]{1,0:T(8,128)} %get-tuple-element.37), channel_id=1, source_target_pairs={{0,1},{1,2},{2,3},{3,4},{4,5},{5,6},{6,7},{7,8},{8,9},{9,10},{10,1... | collective-permute-start | bytes 86024 | tf_op jit(solution)/shard_map/ppermute | solution.py:676
  28.8 1.9 %collective-permute-start.3 = (f32[56,128]{1,0:T(8,128)}, f32[56,128]{1,0:T(8,128)S(1)}, u32[]{:S(2)}, u32[]{:S(2)}) collective-permute-start(f32[56,128]{1,0:T(8,128)} %get-tuple-element.38), channel_id=1, source_target_pairs={{1,0},{2,1},{3,2},{4,3},{5,4},{6,5},{7,6},{8,7},{9,8},{10,9},{11,1... | collective-permute-start | bytes 86024 | tf_op jit(solution)/shard_map/ppermute | solution.py:677
  30.7 0.6 pad_add_fusion.idx
  31.3 0.0 collective-permute-done.2.below
  31.3 2.9 %collective-permute-done.3.above = f32[56,128]{1,0:T(8,128)S(1)} collective-permute-done((f32[56,128]{1,0:T(8,128)}, f32[56,128]{1,0:T(8,128)S(1)}, u32[]{:S(2)}, u32[]{:S(2)}) %collective-permute-start.3) | collective-permute-done | bytes 28704 | tf_op jit(solution)/shard_map/ppermute | solution.py:677
  34.2 0.6 copy-done.10
  34.8 2.7 %stage_state.1 = (f32[256,128]{1,0:T(8,128)}, f32[192,128]{1,0:T(8,128)}, f32[64,128]{1,0:T(8,128)}, f32[1024,128]{1,0:T(8,128)}) custom-call(s32[2]{0:T(128)} %pad_add_fusion.idx, f32[448,128]{1,0:T(8,128)} %get-tuple-element.36.fx, f32[56,128]{1,0:T(8,128)} %copy-done.9, f32[56,128]{1,0:T(8,128)} %copy-done.10, f32[256,128]{1,0:T(8,128)} %bitcast.15, ...), custom_call_target="tpu_custom_call" | custom-call | tf_op jit(solution)/shard_map/stage_state/pallas_call | solution.py:331
  37.5 27.8 %all_to_all.10 = f32[64,16,128]{2,1,0:T(8,128)} all-to-all(f32[64,16,128]{2,1,0:T(8,128)} %bitcast.13), channel_id=1, replica_groups=mesh['gx'=12,'gy'=64] {'gy'}, dimensions={0} | all-to-all | bytes 1048576 | tf_op jit(solution)/shard_map/all_to_all | solution.py:733
  65.3 2.0 %stage_residual.1 = f32[96,128]{1,0:T(8,128)} custom-call(s32[2]{0:T(128)} %pad_add_fusion.idx, f32[1024,128]{1,0:T(8,128)} %bitcast.11, f32[64,128]{1,0:T(8,128)} %get-tuple-element.41.rz, bf16[64,384]{1,0:T(8,128)(2,1)} %constant.84.clone.hart), custom_call_target="tpu_custom_call" | custom-call | tf_op jit(solution)/shard_map/stage_residual/pallas_call | solution.py:331
  67.3 23.3 %all_gather.3.ring = f32[1152,128]{1,0:T(8,128)} all-gather(f32[96,128]{1,0:T(8,128)} %stage_residual.1), channel_id=1, replica_groups=mesh['gx'=12,'gy'=64] {'gx'}, dimensions={0}, use_global_device_ids=true | all-gather | bytes 638976 | tf_op jit(solution)/shard_map/all_gather | solution.py:743
  90.6 2.7 %stage_smooth.1 = (f32[768,128]{1,0:T(8,128)}, f32[768,128]{1,0:T(8,128)}, f32[96,128]{1,0:T(8,128)}, f32[96,128]{1,0:T(8,128)}) custom-call(f32[1152,128]{1,0:T(8,128)} %all_gather.3.ring, bf16[64,192]{1,0:T(8,128)(2,1)} %constant.85.clone.etl, bf16[384,128]{1,0:T(8,128)(2,1)} %constant.86.clone.etr, f32[64,128]{1,0:T(8,128)} %constant.87.clone.sc, ...), custom_call_target="tpu_custom_call" | custom-call | tf_op jit(solution)/shard_map/stage_smooth/pallas_call | solution.py:331
  93.3 8.3 %collective-permute-start.4 = (f32[96,128]{1,0:T(8,128)}, f32[96,128]{1,0:T(8,128)S(1)}, u32[]{:S(2)}, u32[]{:S(2)}) collective-permute-start(f32[96,128]{1,0:T(8,128)} %get-tuple-element.43), channel_id=1, source_target_pairs={{0,1},{1,2},{2,3},{3,4},{4,5},{5,6},{6,7},{7,8},{8,9},{9,10},{10,1... | collective-permute-start | bytes 147464 | tf_op jit(solution)/shard_map/ppermute | solution.py:676
  101.6 1.9 %collective-permute-start.5 = (f32[96,128]{1,0:T(8,128)}, f32[96,128]{1,0:T(8,128)S(1)}, u32[]{:S(2)}, u32[]{:S(2)}) collective-permute-start(f32[96,128]{1,0:T(8,128)} %get-tuple-element.44), channel_id=1, source_target_pairs={{1,0},{2,1},{3,2},{4,3},{5,4},{6,5},{7,6},{8,7},{9,8},{10,9},{11,1... | collective-permute-start | bytes 147464 | tf_op jit(solution)/shard_map/ppermute | solution.py:677
  103.6 2.7 %stage_coarse.1.vert = f32[96,128]{1,0:T(8,128)} custom-call(s32[2]{0:T(128)} %pad_add_fusion.idx, f32[1152,128]{1,0:T(8,128)} %all_gather.3.ring, f32[144,128]{1,0:T(8,128)} %constant.90.clone.coef, bf16[384,128]{1,0:T(8,128)(2,1)} %constant.91.clone.twin, f32[384,128]{1,0:T(8,128)} %constant.92.clone.inv, bf16[64,16,96]{2,1,0:T(8,128)(2,1)} %constant.93.clone.near, ...), custom_call_target="tpu_custom_call" | custom-call | tf_op jit(solution)/shard_map/stage_coarse/pallas_call | solution.py:331
  106.2 0.0 collective-permute-done.4.below
  106.2 1.1 collective-permute-done.5.above
  107.3 0.0 copy-done.2
  107.3 0.6 copy-done.4
  107.9 3.3 %stage_apply.1 = (f32[768,128]{1,0:T(8,128)}, f32[768,128]{1,0:T(8,128)}, f32[96,128]{1,0:T(8,128)}, f32[96,128]{1,0:T(8,128)}, f32[32,128]{1,0:T(8,128)}, /*index=5*/f32[16,128]{1,0:T(8,128)}) custom-call(f32[768,128]{1,0:T(8,128)} %get-tuple-element.42.s, f32[96,128]{1,0:T(8,128)} %copy-done.2, f32[96,128]{1,0:T(8,128)} %copy-done.4, ...), custom_call_target="tpu_custom_call" | custom-call | tf_op jit(solution)/shard_map/stage_apply/pallas_call | solution.py:331
  111.2 2.6 %collective-permute-start.6 = (f32[96,128]{1,0:T(8,128)}, f32[96,128]{1,0:T(8,128)S(1)}, u32[]{:S(2)}, u32[]{:S(2)}) collective-permute-start(f32[96,128]{1,0:T(8,128)} %get-tuple-element.47), channel_id=1, source_target_pairs={{0,1},{1,2},{2,3},{3,4},{4,5},{5,6},{6,7},{7,8},{8,9},{9,10},{10,1... | collective-permute-start | bytes 147464 | tf_op jit(solution)/shard_map/ppermute | solution.py:676
  113.8 4.3 %collective-permute-start.7 = (f32[96,128]{1,0:T(8,128)}, f32[96,128]{1,0:T(8,128)S(1)}, u32[]{:S(2)}, u32[]{:S(2)}) collective-permute-start(f32[96,128]{1,0:T(8,128)} %get-tuple-element.48), channel_id=1, source_target_pairs={{1,0},{2,1},{3,2},{4,3},{5,4},{6,5},{7,6},{8,7},{9,8},{10,9},{11,1... | collective-permute-start | bytes 147464 | tf_op jit(solution)/shard_map/ppermute | solution.py:677
  118.0 0.0 collective-permute-done.6.below
  118.1 0.0 copy-start.5
  118.1 1.3 collective-permute-done.7.above
  119.4 0.6 copy-done.6
  120.0 2.7 %stage_again.1 = (f32[768,128]{1,0:T(8,128)}, f32[96,128]{1,0:T(8,128)}, f32[96,128]{1,0:T(8,128)}, f32[8,128]{1,0:T(8,128)}) custom-call(f32[768,128]{1,0:T(8,128)} %get-tuple-element.46.q, f32[96,128]{1,0:T(8,128)} %copy-done.5, f32[96,128]{1,0:T(8,128)} %copy-done.6, f32[64,128]{1,0:T(8,128)} %constant.101.clone.tab.inv_mz, ...), custom_call_target="tpu_custom_call" | custom-call | tf_op jit(solution)/shard_map/stage_again/pallas_call | solution.py:331
  122.8 2.0 %collective-permute-start.8 = (f32[96,128]{1,0:T(8,128)}, f32[96,128]{1,0:T(8,128)S(1)}, u32[]{:S(2)}, u32[]{:S(2)}) collective-permute-start(f32[96,128]{1,0:T(8,128)} %get-tuple-element.50), channel_id=1, source_target_pairs={{0,1},{1,2},{2,3},{3,4},{4,5},{5,6},{6,7},{7,8},{8,9},{9,10},{10,1... | collective-permute-start | bytes 147464 | tf_op jit(solution)/shard_map/ppermute | solution.py:676
  124.8 7.6 %collective-permute-start.9 = (f32[96,128]{1,0:T(8,128)}, f32[96,128]{1,0:T(8,128)S(1)}, u32[]{:S(2)}, u32[]{:S(2)}) collective-permute-start(f32[96,128]{1,0:T(8,128)} %get-tuple-element.51), channel_id=1, source_target_pairs={{1,0},{2,1},{3,2},{4,3},{5,4},{6,5},{7,6},{8,7},{9,8},{10,9},{11,1... | collective-permute-start | bytes 147464 | tf_op jit(solution)/shard_map/ppermute | solution.py:677
  132.3 0.0 collective-permute-done.8.below
  132.4 0.0 copy-start.1
  132.4 1.0 collective-permute-done.9.above
  133.4 0.6 copy-done.3
  134.0 3.5 %stage_gather.1 = (f32[768,128]{1,0:T(8,128)}, f32[1024,128]{1,0:T(8,128)}, f32[16,128]{1,0:T(8,128)}, f32[16,128]{1,0:T(8,128)}) custom-call(s32[2]{0:T(128)} %pad_add_fusion.idx, f32[768,128]{1,0:T(8,128)} %get-tuple-element.49.s, f32[96,128]{1,0:T(8,128)} %copy-done.1, f32[96,128]{1,0:T(8,128)} %copy-done.3, f32[768,128]{1,0:T(8,128)} %get-tuple-element.52.z0, ...), custom_call_target="tpu_custom_call" | custom-call | tf_op jit(solution)/shard_map/stage_gather/pallas_call | solution.py:331
  137.6 13.0 %all-to-all-start.1 = ((f32[64,16,128]{2,1,0:T(8,128)}), f32[64,16,128]{2,1,0:T(8,128)S(1)}, u32[]{:S(2)}, u32[]{:S(2)}) async-start(f32[64,16,128]{2,1,0:T(8,128)} %bitcast.12), calls=%async_computation.1 | async-start | bytes 1048576 | tf_op jit(solution)/shard_map/all_to_all | solution.py:800
  150.6 3.5 %collective-permute-start.10 = (f32[16,128]{1,0:T(8,128)S(1)}, f32[16,128]{1,0:T(8,128)S(1)}, u32[]{:S(2)}, u32[]{:S(2)}) collective-permute-start(f32[16,128]{1,0:T(8,128)S(1)} %copy-done.14), channel_id=1, source_target_pairs={{0,1},{1,2},{2,3},{3,4},{4,5},{5,6},{6,7},{7,8},{8,9},{9,10},{10,1... | collective-permute-start | bytes 24584 | tf_op jit(solution)/shard_map/ppermute | solution.py:676
  154.1 1.9 %collective-permute-start.11 = (f32[16,128]{1,0:T(8,128)S(1)}, f32[16,128]{1,0:T(8,128)S(1)}, u32[]{:S(2)}, u32[]{:S(2)}) collective-permute-start(f32[16,128]{1,0:T(8,128)S(1)} %copy-done.13), channel_id=1, source_target_pairs={{1,0},{2,1},{3,2},{4,3},{5,4},{6,5},{7,6},{8,7},{9,8},{10,9},{11,1... | collective-permute-start | bytes 24584 | tf_op jit(solution)/shard_map/ppermute | solution.py:677
  156.1 3.3 %collective-permute-done.10.below = f32[16,128]{1,0:T(8,128)S(1)} collective-permute-done((f32[16,128]{1,0:T(8,128)S(1)}, f32[16,128]{1,0:T(8,128)S(1)}, u32[]{:S(2)}, u32[]{:S(2)}) %collective-permute-start.10) | collective-permute-done | bytes 8224 | tf_op jit(solution)/shard_map/ppermute | solution.py:676
  159.4 4.9 %collective-permute-done.11.above = f32[16,128]{1,0:T(8,128)S(1)} collective-permute-done((f32[16,128]{1,0:T(8,128)S(1)}, f32[16,128]{1,0:T(8,128)S(1)}, u32[]{:S(2)}, u32[]{:S(2)}) %collective-permute-start.11) | collective-permute-done | bytes 8224 | tf_op jit(solution)/shard_map/ppermute | solution.py:677
  164.3 3.8 %all-to-all-done.1 = f32[64,16,128]{2,1,0:T(8,128)S(1)} async-done(((f32[64,16,128]{2,1,0:T(8,128)}), f32[64,16,128]{2,1,0:T(8,128)S(1)}, u32[]{:S(2)}, u32[]{:S(2)}) %all-to-all-start.1) | async-done | bytes 524320 | tf_op jit(solution)/shard_map/all_to_all | solution.py:800
  168.2 0.8 copy-done
  168.9 3.6 %stage_final.1 = (f32[256,128]{1,0:T(8,128)}, f32[64,128]{1,0:T(8,128)}) custom-call(s32[2]{0:T(128)} %pad_add_fusion.idx, f32[576]{0:T(1024)} %constant.103.clone.reach, f32[1024,128]{1,0:T(8,128)} %bitcast.10, f32[16,128]{1,0:T(8,128)} %copy-done.11, f32[16,128]{1,0:T(8,128)} %copy-done.12, f32[768,128]{1,0:T(8,128)} %get-tuple-element.52.z0, ...), custom_call_target="tpu_custom_call" | custom-call | tf_op jit(solution)/shard_map/stage_final/pallas_call | solution.py:331
  (21 shorter events, 0.0 us)
Async XLA Ops:
  3.6 17.1 %collective-permute-start = (f32[56,128]{1,0:T(8,128)}, f32[56,128]{1,0:T(8,128)S(1)}, u32[]{:S(2)}, u32[]{:S(2)}) collective-permute-start(f32[56,128]{1,0:T(8,128)} %get-tuple-element.34), channel_id=1, source_target_pairs={{0,64},{64,128},{128,192},{192,256},{256,320},{320,384},{384,448},... | collective-permute-start | bytes 86024 | tf_op jit(solution)/shard_map/ppermute | solution.py:676
  8.5 13.4 %collective-permute-start.1 = (f32[56,128]{1,0:T(8,128)}, f32[56,128]{1,0:T(8,128)S(1)}, u32[]{:S(2)}, u32[]{:S(2)}) collective-permute-start(f32[56,128]{1,0:T(8,128)} %get-tuple-element.35), channel_id=1, source_target_pairs={{64,0},{128,64},{192,128},{256,192},{320,256},{384,320},{448,384},... | collective-permute-start | bytes 86024 | tf_op jit(solution)/shard_map/ppermute | solution.py:677
  20.7 1.2 copy-start.7
  21.9 0.6 copy-start.8
  24.2 7.1 %collective-permute-start.2 = (f32[56,128]{1,0:T(8,128)}, f32[56,128]{1,0:T(8,128)S(1)}, u32[]{:S(2)}, u32[]{:S(2)}) collective-permute-start(f32[56,128]{1,0:T(8,128)} %get-tuple-element.37), channel_id=1, source_target_pairs={{0,1},{1,2},{2,3},{3,4},{4,5},{5,6},{6,7},{7,8},{8,9},{9,10},{10,1... | collective-permute-start | bytes 86024 | tf_op jit(solution)/shard_map/ppermute | solution.py:676
  28.8 5.4 %collective-permute-start.3 = (f32[56,128]{1,0:T(8,128)}, f32[56,128]{1,0:T(8,128)S(1)}, u32[]{:S(2)}, u32[]{:S(2)}) collective-permute-start(f32[56,128]{1,0:T(8,128)} %get-tuple-element.38), channel_id=1, source_target_pairs={{1,0},{2,1},{3,2},{4,3},{5,4},{6,5},{7,6},{8,7},{9,8},{10,9},{11,1... | collective-permute-start | bytes 86024 | tf_op jit(solution)/shard_map/ppermute | solution.py:677
  31.3 2.9 %copy-start.9 = (f32[56,128]{1,0:T(8,128)}, f32[56,128]{1,0:T(8,128)S(1)}, u32[]{:S(2)}) copy-start(f32[56,128]{1,0:T(8,128)S(1)} %collective-permute-done.2.below) | copy-start | bytes 86020
  34.2 0.6 copy-start.10
  93.3 12.9 %collective-permute-start.4 = (f32[96,128]{1,0:T(8,128)}, f32[96,128]{1,0:T(8,128)S(1)}, u32[]{:S(2)}, u32[]{:S(2)}) collective-permute-start(f32[96,128]{1,0:T(8,128)} %get-tuple-element.43), channel_id=1, source_target_pairs={{0,1},{1,2},{2,3},{3,4},{4,5},{5,6},{6,7},{7,8},{8,9},{9,10},{10,1... | collective-permute-start | bytes 147464 | tf_op jit(solution)/shard_map/ppermute | solution.py:676
  101.6 5.6 %collective-permute-start.5 = (f32[96,128]{1,0:T(8,128)}, f32[96,128]{1,0:T(8,128)S(1)}, u32[]{:S(2)}, u32[]{:S(2)}) collective-permute-start(f32[96,128]{1,0:T(8,128)} %get-tuple-element.44), channel_id=1, source_target_pairs={{1,0},{2,1},{3,2},{4,3},{5,4},{6,5},{7,6},{8,7},{9,8},{10,9},{11,1... | collective-permute-start | bytes 147464 | tf_op jit(solution)/shard_map/ppermute | solution.py:677
  106.2 1.1 copy-start.2
  107.3 0.6 copy-start.4
  111.2 6.9 %collective-permute-start.6 = (f32[96,128]{1,0:T(8,128)}, f32[96,128]{1,0:T(8,128)S(1)}, u32[]{:S(2)}, u32[]{:S(2)}) collective-permute-start(f32[96,128]{1,0:T(8,128)} %get-tuple-element.47), channel_id=1, source_target_pairs={{0,1},{1,2},{2,3},{3,4},{4,5},{5,6},{6,7},{7,8},{8,9},{9,10},{10,1... | collective-permute-start | bytes 147464 | tf_op jit(solution)/shard_map/ppermute | solution.py:676
  113.8 5.6 %collective-permute-start.7 = (f32[96,128]{1,0:T(8,128)}, f32[96,128]{1,0:T(8,128)S(1)}, u32[]{:S(2)}, u32[]{:S(2)}) collective-permute-start(f32[96,128]{1,0:T(8,128)} %get-tuple-element.48), channel_id=1, source_target_pairs={{1,0},{2,1},{3,2},{4,3},{5,4},{6,5},{7,6},{8,7},{9,8},{10,9},{11,1... | collective-permute-start | bytes 147464 | tf_op jit(solution)/shard_map/ppermute | solution.py:677
  118.1 1.3 copy-start.5
  119.4 0.6 copy-start.6
  122.8 9.6 %collective-permute-start.8 = (f32[96,128]{1,0:T(8,128)}, f32[96,128]{1,0:T(8,128)S(1)}, u32[]{:S(2)}, u32[]{:S(2)}) collective-permute-start(f32[96,128]{1,0:T(8,128)} %get-tuple-element.50), channel_id=1, source_target_pairs={{0,1},{1,2},{2,3},{3,4},{4,5},{5,6},{6,7},{7,8},{8,9},{9,10},{10,1... | collective-permute-start | bytes 147464 | tf_op jit(solution)/shard_map/ppermute | solution.py:676
  124.8 8.7 %collective-permute-start.9 = (f32[96,128]{1,0:T(8,128)}, f32[96,128]{1,0:T(8,128)S(1)}, u32[]{:S(2)}, u32[]{:S(2)}) collective-permute-start(f32[96,128]{1,0:T(8,128)} %get-tuple-element.51), channel_id=1, source_target_pairs={{1,0},{2,1},{3,2},{4,3},{5,4},{6,5},{7,6},{8,7},{9,8},{10,9},{11,1... | collective-permute-start | bytes 147464 | tf_op jit(solution)/shard_map/ppermute | solution.py:677
  132.4 1.1 copy-start.1
  133.4 0.6 copy-start.3
  137.6 13.0 %copy-start.14 = (f32[16,128]{1,0:T(8,128)S(1)}, f32[16,128]{1,0:T(8,128)}, u32[]{:S(2)}) copy-start(f32[16,128]{1,0:T(8,128)} %get-tuple-element.57) | copy-start | bytes 24580
  137.6 16.6 %copy-start.13 = (f32[16,128]{1,0:T(8,128)S(1)}, f32[16,128]{1,0:T(8,128)}, u32[]{:S(2)}) copy-start(f32[16,128]{1,0:T(8,128)} %get-tuple-element.58) | copy-start | bytes 24580
  137.6 30.6 %all-to-all-start.1 = ((f32[64,16,128]{2,1,0:T(8,128)}), f32[64,16,128]{2,1,0:T(8,128)S(1)}, u32[]{:S(2)}, u32[]{:S(2)}) async-start(f32[64,16,128]{2,1,0:T(8,128)} %bitcast.12), calls=%async_computation.1 | async-start | bytes 1048576 | tf_op jit(solution)/shard_map/all_to_all | solution.py:800
  150.6 8.8 %collective-permute-start.10 = (f32[16,128]{1,0:T(8,128)S(1)}, f32[16,128]{1,0:T(8,128)S(1)}, u32[]{:S(2)}, u32[]{:S(2)}) collective-permute-start(f32[16,128]{1,0:T(8,128)S(1)} %copy-done.14), channel_id=1, source_target_pairs={{0,1},{1,2},{2,3},{3,4},{4,5},{5,6},{6,7},{7,8},{8,9},{9,10},{10,1... | collective-permute-start | bytes 24584 | tf_op jit(solution)/shard_map/ppermute | solution.py:676
  154.1 10.2 %collective-permute-start.11 = (f32[16,128]{1,0:T(8,128)S(1)}, f32[16,128]{1,0:T(8,128)S(1)}, u32[]{:S(2)}, u32[]{:S(2)}) collective-permute-start(f32[16,128]{1,0:T(8,128)S(1)} %copy-done.13), channel_id=1, source_target_pairs={{1,0},{2,1},{3,2},{4,3},{5,4},{6,5},{7,6},{8,7},{9,8},{10,9},{11,1... | collective-permute-start | bytes 24584 | tf_op jit(solution)/shard_map/ppermute | solution.py:677
  159.4 8.7 %copy-start.11 = (f32[16,128]{1,0:T(8,128)}, f32[16,128]{1,0:T(8,128)S(1)}, u32[]{:S(2)}) copy-start(f32[16,128]{1,0:T(8,128)S(1)} %collective-permute-done.10.below) | copy-start | bytes 24580
  164.3 3.8 %copy-start.12 = (f32[16,128]{1,0:T(8,128)}, f32[16,128]{1,0:T(8,128)S(1)}, u32[]{:S(2)}) copy-start(f32[16,128]{1,0:T(8,128)S(1)} %collective-permute-done.11.above) | copy-start | bytes 24580
  168.1 0.8 copy-start

commit v2 on v1

--- a/solution.py
+++ b/solution.py
@@ -10,6 +10,7 @@
 from jax.sharding import PartitionSpec as P
 
 INTERPRET = False
+VMEM_LIMIT = 16 * 1024 * 1024
 
 viscosity = 0.05
 time_step = 0.01
@@ -96,8 +97,7 @@
 
 
 def right5(table):
-    high, low, rest = parts_three(table)
-    return np.concatenate([high, high, low, low, rest], axis=0)
+    return np.concatenate(parts_three(table), axis=0)
 
 
 def left3(table):
@@ -106,8 +106,7 @@
 
 
 def right3(table):
-    high, low = parts(table)
-    return np.concatenate([high, high, low], axis=0)
+    return np.concatenate(parts(table), axis=0)
 
 
 def split(field):
@@ -128,8 +127,22 @@
 
 
 def rmul(field, table):
-    terms = table.shape[0] // field.shape[1]
-    return jnp.dot(stacked(field, terms, 1), table, preferred_element_type=jnp.float32)
+    size = field.shape[1]
+    part = [table[k : k + size] for k in range(0, table.shape[0], size)]
+    order = [part[0], part[0], part[1], part[1], part[2]] if len(part) == 3 else [part[0]] + part
+    return jnp.dot(
+        stacked(field, len(order), 1),
+        jnp.concatenate(order, axis=0),
+        preferred_element_type=jnp.float32,
+    )
+
+
+def thrice(table, field):
+    high, low = split(table)
+    first, second = split(field)
+    out = jnp.dot(high, first, preferred_element_type=jnp.float32)
+    out = out + jnp.dot(high, second, preferred_element_type=jnp.float32)
+    return out + jnp.dot(low, first, preferred_element_type=jnp.float32)
 
 
 def lanes_of(field, size=64):
@@ -266,13 +279,10 @@
         packed[:, :, :NV] = inverse[:, :hb]
         packed[:, :, 64 : 64 + NV] = inverse[:, hb:]
         self.inv_packed = packed.reshape(nx * hb, NZ).astype(f32)
-        near = np.zeros((ny, 16, hb))
-        for j in range(ny):
-            for yv in range(2):
-                row = hart_y[(j + yv) % ny]
-                near[j, yv] = row[:hb]
-                near[j, 8 + yv] = row[hb:]
-        self.near = np.stack([left3(block) for block in near])
+        near = hart_y[(np.arange(ny + 8) - 1) % ny]
+        self.near = near.astype(f32)
+        self.near_low = near[:, :hb].astype(f32)
+        self.near_high = near[:, hb:].astype(f32)
         czh = np.zeros((NZ, NZ))
         czh[:NV] = (hz @ cz).T
         self.czh_right = right3(czh)
@@ -294,14 +304,10 @@
         hzc[:, :NV] = (hz / mz[:, None]) @ cz
         self.hzc_right = right3(hzc)
         self.edge_left = left3(np.concatenate([np.kron(eye8, d[:1]), np.kron(eye8, d[7:])], axis=0))
-        wide = np.zeros((ny, nx, NZ))
-        wide[:, :, :NV] = inverse.transpose(1, 0, 2)
-        self.inv_wide = wide.reshape(ny, nx * NZ).astype(f32)
-        around = np.zeros((ny, 8, ny))
-        for j in range(ny):
-            for yv in range(4):
-                around[j, yv] = hart_y[(j + yv - 1) % ny]
-        self.around = np.stack([left3(block) for block in around])
+        self.ex = ex
+        ez_row = np.zeros((8, NZ))
+        ez_row[:, :NV] = ez
+        self.ez_row = ez_row.astype(f32)
         reach = np.zeros((nx, 4, nx))
         for i in range(nx):
             for xv in range(4):
@@ -335,11 +341,12 @@
         out_specs=[pl.BlockSpec(memory_space=pltpu.VMEM)] * len(outs),
         scratch_shapes=list(scratch),
         interpret=INTERPRET,
+        compiler_params=pltpu.CompilerParams(vmem_limit_bytes=VMEM_LIMIT),
         name=kernel.__name__,
     )(*args)
 
 
-def stage_rate(h, flow, old, left, right, tab, fld, xf0, xf7, kp):
+def stage_rate(idx, h, flow, old, left, right, tab, fld, xa, xb, kp):
     f = [flow[q * 64 : q * 64 + 64] for q in range(4)]
     p = old[...]
     lx = lmul(left[...], jnp.concatenate(f + [p], axis=1))
@@ -363,25 +370,46 @@
             kp[...] = stiff + helmholtz_shift * mass * p
             for k, grad in enumerate((gx, gy, gz)):
                 fld[(4 + k) * 64 : (5 + k) * 64] = join_z(mass * grad)
-    for q in range(7):
-        xf0[q * 8 : q * 8 + 8] = fld[q * 64 : q * 64 + 8]
-        xf7[q * 8 : q * 8 + 8] = fld[q * 64 + 56 : q * 64 + 64]
-
-
-def stage_faces(fld, below, above, out, yf0, yf7):
+    start = jnp.concatenate([fld[q * 64 : q * 64 + 8] for q in range(7)], axis=0)
+    end = jnp.concatenate([fld[q * 64 + 56 : q * 64 + 64] for q in range(7)], axis=0)
+    swap_out(is_odd(idx[0]), start, end, xa, xb)
+
+
+def stage_faces(idx, fld, xa, xb, out, ya, yb):
+    below, above = swap_in(is_odd(idx[0]), xa, xb)
     for q in range(7):
         base = q * 64
         out[base : base + 8] = fld[base : base + 8] + below[q * 8 : q * 8 + 8]
         out[base + 8 : base + 56] = fld[base + 8 : base + 56]
         out[base + 56 : base + 64] = fld[base + 56 : base + 64] + above[q * 8 : q * 8 + 8]
-    yf0[...] = out[pl.ds(0, 56, stride=8), :]
-    yf7[...] = out[pl.ds(7, 56, stride=8), :]
-
-
-def add_faces(ref, below, above):
+    swap_faces(is_odd(idx[1]), out, ya, yb)
+
+
+def swap_faces(odd, ref, first, second):
+    count = ref.shape[0] // 8
+    start = ref[pl.ds(0, count, stride=8), :]
+    end = ref[pl.ds(7, count, stride=8), :]
+    swap_out(odd, start, end, first, second)
+
+
+def add_faces(odd, ref, first, second):
+    below, above = swap_in(odd, first, second)
     count = ref.shape[0] // 8
     ref[pl.ds(0, count, stride=8), :] = ref[pl.ds(0, count, stride=8), :] + below
     ref[pl.ds(7, count, stride=8), :] = ref[pl.ds(7, count, stride=8), :] + above
+
+
+def swap_out(odd, start, end, first, second):
+    first[...] = jnp.where(odd, start, end)
+    second[...] = jnp.where(odd, end, start)
+
+
+def swap_in(odd, first, second):
+    return jnp.where(odd, first[...], second[...]), jnp.where(odd, second[...], first[...])
+
+
+def is_odd(index):
+    return lax.rem(index, 2) == 1
 
 
 def make_stages(t):
@@ -391,7 +419,7 @@
         idx, fx, below, above, flow, kp, tab, dleft, dright, pleft, hright, prov, g0, rz, msg, scr
     ):
         scr[...] = fx[...]
-        add_faces(scr, below[...], above[...])
+        add_faces(is_odd(idx[1]), scr, below, above)
         mass, inv_bm = tab[0:64], tab[64:128]
         lane = lane_index(64)
         new = []
@@ -435,16 +463,15 @@
         modal = rmul(modal * tiled(sc, nx), er)
         return rows_of(lmul(el, lanes_of(modal)))
 
-    def stage_smooth(ring, etl, etr, sc, er, el, r0, s, s0, s7):
+    def stage_smooth(idx, ring, etl, etr, sc, er, el, r0, s, s0, s7):
         size = 64 + hb
         rows = jnp.concatenate([ring[i * size : i * size + 64] for i in range(nx)], axis=0)
         residual = join_x(rows, nx)
         r0[...] = residual
         s[...] = join_x(smoothed(residual, etl[...], etr[...], sc[...], er[...], el[...]), nx)
-        s0[...] = s[pl.ds(0, nx * 8, stride=8), :]
-        s7[...] = s[pl.ds(7, nx * 8, stride=8), :]
-
-    def stage_coarse(idx, ring, coef, twin, inv, near, czh, out):
+        swap_faces(is_odd(idx[1]), s, s0, s7)
+
+    def stage_coarse(idx, ring, coef, twin, inv, near_low, near_high, czh, out):
         size = 64 + hb
         grid = [ring[i * size + 64 : (i + 1) * size] for i in range(nx)]
         modes = []
@@ -454,11 +481,13 @@
                 acc = acc + grid[i] * coef[a * nx + i : a * nx + i + 1]
             modes.append(acc + turn(acc, -NV))
         values = rmul(jnp.concatenate(modes, axis=0), twin[...]) * inv[...]
-        pair = lmul(near[idx[1]], lanes_of(values, hb))
+        wide = lanes_of(values, hb)
+        low = thrice(near_low[pl.ds(idx[1], 8), :], wide)
+        high = thrice(near_high[pl.ds(idx[1], 8), :], wide)
         lines = []
         for a in range(nx):
-            tile = pair[:, a * NZ : (a + 1) * NZ]
-            lines.append(tile[0:8] + turn(tile[8:16], 64))
+            tile = slice(a * NZ, (a + 1) * NZ)
+            lines.append(low[:, tile] + turn(high[:, tile], 64))
         columns = []
         for i in range(nx):
             acc = lines[0] * float(t.hart_x[i, 0])
@@ -484,14 +513,14 @@
         return rmul(lmul(back, jnp.concatenate(columns, axis=0)), hzc)
 
     def stage_apply(
-        s, below, above, vert, r0, hy, al, tab, ar, back, hzc, z0, q, q0, q7, cq, sums
+        idx, s, below, above, vert, r0, hy, al, tab, ar, back, hzc, z0, q, q0, q7, cq, sums
     ):
         z0[...] = s[...]
-        add_faces(z0, below[...], above[...])
+        add_faces(is_odd(idx[1]), z0, below, above)
         slabs = []
         for i in range(nx):
             slabs.append(
-                hy[0:8] * vert[i * 8 : i * 8 + 1] + hy[8:16] * vert[i * 8 + 1 : i * 8 + 2]
+                hy[0:8] * vert[i * 8 + 1 : i * 8 + 2] + hy[8:16] * vert[i * 8 + 2 : i * 8 + 3]
             )
         pieces = []
         for i in range(nx):
@@ -507,24 +536,22 @@
         sums[8:16] = fold(field * image * tiled(inv_mz, nx))
         cq[...] = restricted(image, back[...], hzc[...])
         q[...] = join_x(image, nx)
-        q0[...] = q[pl.ds(0, nx * 8, stride=8), :]
-        q7[...] = q[pl.ds(7, nx * 8, stride=8), :]
-
-    def stage_again(q, below, above, tab, etl, etr, sc, er, el, s, s0, s7, sums, scr):
+        swap_faces(is_odd(idx[1]), q, q0, q7)
+
+    def stage_again(idx, q, below, above, tab, etl, etr, sc, er, el, s, s0, s7, sums, scr):
         scr[...] = q[...]
-        add_faces(scr, below[...], above[...])
+        add_faces(is_odd(idx[1]), scr, below, above)
         field = scr[...]
         local = smoothed(field, etl[...], etr[...], sc[...], er[...], el[...])
         sums[...] = fold(field * local * tiled(tab[...], nx))
         s[...] = join_x(local, nx)
-        s0[...] = s[pl.ds(0, nx * 8, stride=8), :]
-        s7[...] = s[pl.ds(7, nx * 8, stride=8), :]
+        swap_faces(is_odd(idx[1]), s, s0, s7)
 
     def stage_gather(
         idx, s, below, above, z0, cq, sums1, sums2, al, tab, ar, back, hzc, edge, sq, msg, g0, g7
     ):
         sq[...] = s[...]
-        add_faces(sq, below[...], above[...])
+        add_faces(is_odd(idx[1]), sq, below, above)
         field = sq[...]
         wxy, inv_mz = tab[0:64], tab[128:192]
         image = applied(field, al[...], wxy, ar[...])
@@ -541,8 +568,9 @@
         base = pl.multiple_of(idx[0] * 64, 64)
         pair = jnp.concatenate([z0[pl.ds(base, 64), :], sq[pl.ds(base, 64), :]], axis=1)
         slopes = lmul(edge[...], pair)
-        g0[...] = jnp.concatenate([slopes[0:8, 0:NZ], slopes[0:8, NZ:]], axis=0)
-        g7[...] = jnp.concatenate([slopes[8:16, 0:NZ], slopes[8:16, NZ:]], axis=0)
+        start = jnp.concatenate([slopes[0:8, 0:NZ], slopes[0:8, NZ:]], axis=0)
+        end = jnp.concatenate([slopes[8:16, 0:NZ], slopes[8:16, NZ:]], axis=0)
+        swap_out(is_odd(idx[1]), start, end, g0, g7)
 
     def stage_final(
         idx,
@@ -556,7 +584,7 @@
         g0,
         old,
         hart,
-        inv,
+        ez_row,
         around,
         czh,
         gal,
@@ -574,12 +602,13 @@
         my, ky = mky[0:ny], mky[ny : 2 * ny]
         lane = lane_index(ny)
         found = []
+        levels = 2.0 * (2.0 * ky + ez_row[0:1]) + coarse_shift
         cross = jnp.zeros((ny, NZ), jnp.float32)
         plain = jnp.zeros((ny, NZ), jnp.float32)
         for a in range(nx):
             tile = slice(a * NZ, (a + 1) * NZ)
             comb = both[0:ny, tile] + turn(both[ny : 2 * ny, tile], -32)
-            e = comb * inv[:, tile]
+            e = jnp.where(lane < NV, comb / (levels + 2.0 * float(t.ex[a])), 0.0)
             found.append(e)
             plain = plain + e * comb
             cross = cross + e * turn(comb, -64)
@@ -610,7 +639,7 @@
         second = rz1 / curve
         on_z = first + second * grow
         on_w = -second * first
-        lines = lmul(around[idx[1]], jnp.concatenate(found, axis=1))
+        lines = thrice(around[pl.ds(idx[1], 8), :], jnp.concatenate(found, axis=1))
         stack = []
         for xv in range(4):
             base = (idx[0] * 4 + xv) * nx
@@ -647,6 +676,7 @@
         line1 = [scr[k * 8 + 1 : k * 8 + 2] for k in range(4)]
         step0 = [0.5 * (scr[k * 8 + 1 : k * 8 + 2] - scr[k * 8 : k * 8 + 1]) for k in (1, 2)]
         step7 = [0.5 * (scr[k * 8 + 3 : k * 8 + 4] - scr[k * 8 + 2 : k * 8 + 3]) for k in (1, 2)]
+        below, above = swap_in(is_odd(idx[1]), below, above)
         under = below[0:8] * on_z + below[8:16] * on_w + hx0 * step0[0] + hx1 * step0[1]
         over = above[0:8] * on_z + above[8:16] * on_w + hx0 * step7[0] + hx1 * step7[1]
         press_y = gy
@@ -671,11 +701,11 @@
     )
 
 
-def exchange(axis, first, last):
+def exchange(axis, first, second):
     count = lax.axis_size(axis)
-    below = lax.ppermute(last, axis, [(k, (k + 1) % count) for k in range(count)])
-    above = lax.ppermute(first, axis, [((k + 1) % count, k) for k in range(count)])
-    return below, above
+    pairs = [(k, k ^ 1) for k in range(count)]
+    across = [(k, ((k - 1) ^ 1) + 1) for k in range(1, count - 1)] + [(0, count - 1), (count - 1, 0)]
+    return lax.ppermute(first, axis, pairs), lax.ppermute(second, axis, across)
 
 
 def make_device(t):
@@ -700,17 +730,18 @@
         fld, xf0, xf7, kp = call(
             stage_rate,
             [(448, NZ), (56, NZ), (56, NZ), col],
+            idx,
             building_height,
             flow,
             old,
             c(t.k1_left),
             c(t.k1_right),
             c(t.visc),
-            smem=1,
+            smem=2,
         )
         below, above = exchange("gx", xf0, xf7)
         fld, yf0, yf7 = call(
-            stage_faces, [(448, NZ), (56, NZ), (56, NZ)], fld, below, above
+            stage_faces, [(448, NZ), (56, NZ), (56, NZ)], idx, fld, below, above, smem=1
         )
         below, above = exchange("gy", yf0, yf7)
         prov, g0, rz, msg = call(
@@ -742,7 +773,9 @@
         )
         whole = lax.all_gather(piece, "gx", axis=0, tiled=True)
         smoother = (c(t.et_left), c(t.et_right), c(t.scale), c(t.e_right), c(t.e_left))
-        r0, s, s0, s7 = call(stage_smooth, [ring, ring, face, face], whole, *smoother)
+        r0, s, s0, s7 = call(
+            stage_smooth, [ring, ring, face, face], idx, whole, *smoother, smem=1
+        )
         below, above = exchange("gy", s0, s7)
         (vert,) = call(
             stage_coarse,
@@ -752,7 +785,8 @@
             c(t.coef),
             c(t.twin_right),
             c(t.inv_packed),
-            c(t.near),
+            c(t.near_low),
+            c(t.near_high),
             c(t.czh_right),
             smem=1,
         )
@@ -761,6 +795,7 @@
         z0, q, q0, q7, cq, sums1 = call(
             stage_apply,
             [ring, ring, face, face, (32, NZ), (16, NZ)],
+            idx,
             s,
             below,
             above,
@@ -768,16 +803,19 @@
             r0,
             c(t.hy),
             *operator,
+            smem=1,
         )
         below, above = exchange("gy", q0, q7)
         s, s0, s7, sums2 = call(
             stage_again,
             [ring, face, face, (8, NZ)],
+            idx,
             q,
             below,
             above,
             c(t.inv_mz),
             *smoother,
+            smem=1,
             scratch=[pltpu.VMEM(ring, jnp.float32)],
         )
         below, above = exchange("gy", s0, s7)
@@ -812,8 +850,8 @@
             g0,
             old,
             c(t.hart_two),
-            c(t.inv_wide),
-            c(t.around),
+            c(t.ez_row),
+            c(t.near),
             c(t.czh_right),
             c(t.galerkin_right),
             c(t.mky),

time: 173 us -> 158 us (0.913)
  Pallas kernels: 27.3 us -> 14.6 us
  starting transfers between devices: 68.7 us -> 62.7 us
  waiting for transfers between devices: 19.5 us -> 23.3 us
    pallas_call x10, Pallas kernels: 27.3 us -> 14.6 us  [call(): pl.pallas_call(kernel, out_shape=[jax.ShapeDtypeStruct(shape, jnp.float32...]
    all_to_all x1, starting transfers between devices: 13 us -> 8.26 us  [on_device(): rec = lax.all_to_all(msg.reshape(ny, 16, NZ), 'gy', 0, 0, tiled=True)]
    ppermute x12, waiting for transfers between devices: 15.7 us -> 19.5 us  [the longest x6 19.5 us: exchange(): lax.ppermute(second, axis, across)]
    all_gather x1, blocking collectives: 23.3 us -> 21.2 us  [on_device(): whole = lax.all_gather(piece, 'gx', axis=0, tiled=True)]
    unnamed x30 -> x78, local copies, waits for them, and re-layouts: 3.9 us -> 4.58 us
  transfers between devices with their start and end apart: 13 -> 13, of which waited for: 8 -> 7; matrix products, arithmetic and copies ran while one was open for 0% -> 0% of each run, Pallas kernels for 2% -> 1%
where the time goes in v2:
time: 158 us; the launch traced here: 157 us
  starting transfers between devices  62.7 us (40%)
  blocking collectives  49.8 us (32%)
  waiting for transfers between devices  23.3 us (15%)
  Pallas kernels  14.6 us (9%)
  local copies, waits for them, and re-layouts  4.58 us (3%)
  between operations  1.84 us (1%)
    ppermute x6, starting transfers between devices, exchange(): lax.ppermute(first, axis, pairs)  28.8 us
    all_to_all x1, blocking collectives, on_device(): rec = lax.all_to_all(msg.reshape(ny, 16, NZ), 'gy', 0, 0, tiled=True)  28.6 us
    ppermute x6, starting transfers between devices, exchange(): lax.ppermute(second, axis, across)  25.6 us
    all_gather x1, blocking collectives, on_device(): whole = lax.all_gather(piece, 'gx', axis=0, tiled=True)  21.2 us
    ppermute x6, waiting for transfers between devices, exchange(): lax.ppermute(second, axis, across)  19.5 us
    pallas_call x10, Pallas kernels, call(): pl.pallas_call(kernel, out_shape=[jax.ShapeDtypeStruct(shape, jnp.float32...  14.6 us
    all_to_all x1, starting transfers between devices, on_device(): rec = lax.all_to_all(msg.reshape(ny, 16, NZ), 'gy', 0, 0, tiled=True)  8.26 us
    unnamed x78, local copies, waits for them, and re-layouts  4.58 us
  transfers between devices with their start and end apart: 13, of which 7 were waited for; matrix products, arithmetic and copies ran while one was open for 0% of the time, Pallas kernels for 1%

profile of v2, /device:TPU:1, one launch (start us, length us, event | category | flops | bytes accessed | tf_op | source)
XLA Modules:
  0.0 156.9 jit_solution(10448737060918227146)
XLA Ops:
  1.3 0.1 pad_add_fusion.idx
  1.4 0.9 copy-done.1
  2.3 0.9 copy-done.10
  3.2 0.9 copy-done.12
  4.1 0.8 copy-done.13
  4.9 0.9 copy-done.21
  5.8 1.1 stage_rate.1
  6.8 4.8 %collective-permute-start = (f32[56,128]{1,0:T(8,128)S(1)}, f32[56,128]{1,0:T(8,128)S(1)}, u32[]{:S(2)}, u32[]{:S(2)}) collective-permute-start(f32[56,128]{1,0:T(8,128)S(1)} %get-tuple-element.34), channel_id=1, source_target_pairs={{0,64},{64,0},{128,192},{192,128},{256,320},{320,256},{384,448},{4... | collective-permute-start | bytes 86024 | tf_op jit(solution)/shard_map/ppermute | solution.py:708
  11.6 12.5 %collective-permute-start.1 = (f32[56,128]{1,0:T(8,128)S(1)}, f32[56,128]{1,0:T(8,128)S(1)}, u32[]{:S(2)}, u32[]{:S(2)}) collective-permute-start(f32[56,128]{1,0:T(8,128)S(1)} %get-tuple-element.35), channel_id=1, source_target_pairs={{64,128},{128,64},{192,256},{256,192},{320,384},{384,320},{448,512... | collective-permute-start | bytes 86024 | tf_op jit(solution)/shard_map/ppermute | solution.py:708
  24.2 1.2 collective-permute-done.1.xb
  25.4 0.6 stage_faces.1
  26.0 3.7 %collective-permute-start.2 = (f32[56,128]{1,0:T(8,128)S(1)}, f32[56,128]{1,0:T(8,128)S(1)}, u32[]{:S(2)}, u32[]{:S(2)}) collective-permute-start(f32[56,128]{1,0:T(8,128)S(1)} %get-tuple-element.37), channel_id=1, source_target_pairs={{0,1},{1,0},{2,3},{3,2},{4,5},{5,4},{6,7},{7,6},{8,9},{9,8},{10,11... | collective-permute-start | bytes 86024 | tf_op jit(solution)/shard_map/ppermute | solution.py:708
  29.7 3.1 %collective-permute-start.3 = (f32[56,128]{1,0:T(8,128)S(1)}, f32[56,128]{1,0:T(8,128)S(1)}, u32[]{:S(2)}, u32[]{:S(2)}) collective-permute-start(f32[56,128]{1,0:T(8,128)S(1)} %get-tuple-element.38), channel_id=1, source_target_pairs={{1,2},{2,1},{3,4},{4,3},{5,6},{6,5},{7,8},{8,7},{9,10},{10,9},{11,... | collective-permute-start | bytes 86024 | tf_op jit(solution)/shard_map/ppermute | solution.py:708
  32.8 2.1 %collective-permute-done.3.above = f32[56,128]{1,0:T(8,128)S(1)} collective-permute-done((f32[56,128]{1,0:T(8,128)S(1)}, f32[56,128]{1,0:T(8,128)S(1)}, u32[]{:S(2)}, u32[]{:S(2)}) %collective-permute-start.3) | collective-permute-done | bytes 28704 | tf_op jit(solution)/shard_map/ppermute | solution.py:708
  34.9 1.1 stage_state.1
  36.1 0.0 copy-start.30
  36.1 28.6 %all_to_all.10 = f32[64,16,128]{2,1,0:T(8,128)S(1)} all-to-all(f32[64,16,128]{2,1,0:T(8,128)S(1)} %bitcast.12), channel_id=1, replica_groups=mesh['gx'=12,'gy'=64] {'gy'}, dimensions={0} | all-to-all | bytes 1048576 | tf_op jit(solution)/shard_map/all_to_all | solution.py:764
  64.7 0.8 stage_residual.1
  65.5 0.0 copy-start.17
  65.5 0.0 copy-start.18
  65.5 0.0 copy-start.19
  65.5 21.2 %all_gather.3.ring = f32[1152,128]{1,0:T(8,128)S(1)} all-gather(f32[96,128]{1,0:T(8,128)S(1)} %stage_residual.1), channel_id=1, replica_groups=mesh['gx'=12,'gy'=64] {'gx'}, dimensions={0}, use_global_device_ids=true | all-gather | bytes 638976 | tf_op jit(solution)/shard_map/all_gather | solution.py:774
  86.8 0.0 copy-start.5
  86.8 0.0 copy-start.11
  86.8 0.0 copy-start.24
  86.8 0.0 copy-start.27
  86.9 0.0 copy-start.31
  86.9 0.0 copy-start.32
  86.9 1.3 stage_smooth.1
  88.2 7.5 %collective-permute-start.4 = (f32[96,128]{1,0:T(8,128)S(1)}, f32[96,128]{1,0:T(8,128)S(1)}, u32[]{:S(2)}, u32[]{:S(2)}) collective-permute-start(f32[96,128]{1,0:T(8,128)S(1)} %get-tuple-element.43), channel_id=1, source_target_pairs={{0,1},{1,0},{2,3},{3,2},{4,5},{5,4},{6,7},{7,6},{8,9},{9,8},{10,11... | collective-permute-start | bytes 147464 | tf_op jit(solution)/shard_map/ppermute | solution.py:708
  95.7 3.0 %collective-permute-start.5 = (f32[96,128]{1,0:T(8,128)S(1)}, f32[96,128]{1,0:T(8,128)S(1)}, u32[]{:S(2)}, u32[]{:S(2)}) collective-permute-start(f32[96,128]{1,0:T(8,128)S(1)} %get-tuple-element.44), channel_id=1, source_target_pairs={{1,2},{2,1},{3,4},{4,3},{5,6},{6,5},{7,8},{8,7},{9,10},{10,9},{11,... | collective-permute-start | bytes 147464 | tf_op jit(solution)/shard_map/ppermute | solution.py:708
  98.8 1.4 stage_coarse.1.vert
  100.2 1.1 collective-permute-done.5.above
  101.3 1.8 %stage_apply.1 = (f32[768,128]{1,0:T(8,128)S(1)}, f32[768,128]{1,0:T(8,128)S(1)}, f32[96,128]{1,0:T(8,128)S(1)}, f32[96,128]{1,0:T(8,128)S(1)}, f32[32,128]{1,0:T(8,128)S(1)}, /*index=5*/f32[16,128]{1,0:T(8,128)S(1)}) custom-call(s32[2]{0:T(128)S(1)} %pad_add_fusion.idx, f32[768,128]{1,0:T(8,128)S(1)} %get-tuple-element.42.s, ...), custom_call_target="tpu_custom_call" | custom-call | tf_op jit(solution)/shard_map/stage_apply/pallas_call | solution.py:337
  103.2 5.2 %collective-permute-start.6 = (f32[96,128]{1,0:T(8,128)S(1)}, f32[96,128]{1,0:T(8,128)S(1)}, u32[]{:S(2)}, u32[]{:S(2)}) collective-permute-start(f32[96,128]{1,0:T(8,128)S(1)} %get-tuple-element.47), channel_id=1, source_target_pairs={{0,1},{1,0},{2,3},{3,2},{4,5},{5,4},{6,7},{7,6},{8,9},{9,8},{10,11... | collective-permute-start | bytes 147464 | tf_op jit(solution)/shard_map/ppermute | solution.py:708
  108.4 1.9 %collective-permute-start.7 = (f32[96,128]{1,0:T(8,128)S(1)}, f32[96,128]{1,0:T(8,128)S(1)}, u32[]{:S(2)}, u32[]{:S(2)}) collective-permute-start(f32[96,128]{1,0:T(8,128)S(1)} %get-tuple-element.48), channel_id=1, source_target_pairs={{1,2},{2,1},{3,4},{4,3},{5,6},{6,5},{7,8},{8,7},{9,10},{10,9},{11,... | collective-permute-start | bytes 147464 | tf_op jit(solution)/shard_map/ppermute | solution.py:708
  110.4 3.5 %collective-permute-done.7.above = f32[96,128]{1,0:T(8,128)S(1)} collective-permute-done((f32[96,128]{1,0:T(8,128)S(1)}, f32[96,128]{1,0:T(8,128)S(1)}, u32[]{:S(2)}, u32[]{:S(2)}) %collective-permute-start.7) | collective-permute-done | bytes 49184 | tf_op jit(solution)/shard_map/ppermute | solution.py:708
  113.8 1.3 stage_again.1
  115.2 5.2 %collective-permute-start.8 = (f32[96,128]{1,0:T(8,128)S(1)}, f32[96,128]{1,0:T(8,128)S(1)}, u32[]{:S(2)}, u32[]{:S(2)}) collective-permute-start(f32[96,128]{1,0:T(8,128)S(1)} %get-tuple-element.50), channel_id=1, source_target_pairs={{0,1},{1,0},{2,3},{3,2},{4,5},{5,4},{6,7},{7,6},{8,9},{9,8},{10,11... | collective-permute-start | bytes 147464 | tf_op jit(solution)/shard_map/ppermute | solution.py:708
  120.4 1.9 %collective-permute-start.9 = (f32[96,128]{1,0:T(8,128)S(1)}, f32[96,128]{1,0:T(8,128)S(1)}, u32[]{:S(2)}, u32[]{:S(2)}) collective-permute-start(f32[96,128]{1,0:T(8,128)S(1)} %get-tuple-element.51), channel_id=1, source_target_pairs={{1,2},{2,1},{3,4},{4,3},{5,6},{6,5},{7,8},{8,7},{9,10},{10,9},{11,... | collective-permute-start | bytes 147464 | tf_op jit(solution)/shard_map/ppermute | solution.py:708
  122.4 3.5 %collective-permute-done.9.above = f32[96,128]{1,0:T(8,128)S(1)} collective-permute-done((f32[96,128]{1,0:T(8,128)S(1)}, f32[96,128]{1,0:T(8,128)S(1)}, u32[]{:S(2)}, u32[]{:S(2)}) %collective-permute-start.9) | collective-permute-done | bytes 49184 | tf_op jit(solution)/shard_map/ppermute | solution.py:708
  125.8 2.7 %stage_gather.1 = (f32[768,128]{1,0:T(8,128)S(1)}, f32[1024,128]{1,0:T(8,128)}, f32[16,128]{1,0:T(8,128)S(1)}, f32[16,128]{1,0:T(8,128)S(1)}) custom-call(s32[2]{0:T(128)S(1)} %pad_add_fusion.idx, f32[768,128]{1,0:T(8,128)S(1)} %get-tuple-element.49.s, f32[96,128]{1,0:T(8,128)S(1)} %collective-permute-done.8.below, ...), custom_call_target="tpu_custom_call" | custom-call | tf_op jit(solution)/shard_map/stage_gather/pallas_call | solution.py:337
  128.6 8.3 %all-to-all-start.1 = ((f32[64,16,128]{2,1,0:T(8,128)}), f32[64,16,128]{2,1,0:T(8,128)S(1)}, u32[]{:S(2)}, u32[]{:S(2)}) async-start(f32[64,16,128]{2,1,0:T(8,128)} %bitcast.6), calls=%async_computation.1 | async-start | bytes 1048576 | tf_op jit(solution)/shard_map/all_to_all | solution.py:838
  136.9 2.4 %collective-permute-start.10 = (f32[16,128]{1,0:T(8,128)S(1)}, f32[16,128]{1,0:T(8,128)S(1)}, u32[]{:S(2)}, u32[]{:S(2)}) collective-permute-start(f32[16,128]{1,0:T(8,128)S(1)} %get-tuple-element.57), channel_id=1, source_target_pairs={{0,1},{1,0},{2,3},{3,2},{4,5},{5,4},{6,7},{7,6},{8,9},{9,8},{10,11... | collective-permute-start | bytes 24584 | tf_op jit(solution)/shard_map/ppermute | solution.py:708
  139.3 3.2 %collective-permute-start.11 = (f32[16,128]{1,0:T(8,128)S(1)}, f32[16,128]{1,0:T(8,128)S(1)}, u32[]{:S(2)}, u32[]{:S(2)}) collective-permute-start(f32[16,128]{1,0:T(8,128)S(1)} %get-tuple-element.58), channel_id=1, source_target_pairs={{1,2},{2,1},{3,4},{4,3},{5,6},{6,5},{7,8},{8,7},{9,10},{10,9},{11,... | collective-permute-start | bytes 24584 | tf_op jit(solution)/shard_map/ppermute | solution.py:708
  142.5 8.1 %collective-permute-done.11.above = f32[16,128]{1,0:T(8,128)S(1)} collective-permute-done((f32[16,128]{1,0:T(8,128)S(1)}, f32[16,128]{1,0:T(8,128)S(1)}, u32[]{:S(2)}, u32[]{:S(2)}) %collective-permute-start.11) | collective-permute-done | bytes 8224 | tf_op jit(solution)/shard_map/ppermute | solution.py:708
  150.6 3.8 %all-to-all-done.1 = f32[64,16,128]{2,1,0:T(8,128)S(1)} async-done(((f32[64,16,128]{2,1,0:T(8,128)}), f32[64,16,128]{2,1,0:T(8,128)S(1)}, u32[]{:S(2)}, u32[]{:S(2)}) %all-to-all-start.1) | async-done | bytes 524320 | tf_op jit(solution)/shard_map/all_to_all | solution.py:838
  154.5 2.4 %stage_final.1 = (f32[256,128]{1,0:T(8,128)}, f32[64,128]{1,0:T(8,128)}) custom-call(s32[2]{0:T(128)S(1)} %pad_add_fusion.idx, f32[576]{0:T(1024)S(1)} %copy-done.37, f32[1024,128]{1,0:T(8,128)S(1)} %bitcast.10, f32[16,128]{1,0:T(8,128)S(1)} %collective-permute-done.10.below, f32[16,128]{1,0:T(8,128)S(1)} %collective-permute-done.11.above, ...), custom_call_target="tpu_custom_call" | custom-call | tf_op jit(solution)/shard_map/stage_final/pallas_call | solution.py:337
  (69 shorter events, 0.2 us)
Async XLA Ops:
  2.3 0.9 copy-start.10
  5.8 29.2 %copy-start.23 = (bf16[64,640]{1,0:T(8,128)(2,1)S(1)}, bf16[64,640]{1,0:T(8,128)(2,1)}, u32[]{:S(2)}) copy-start(bf16[64,640]{1,0:T(8,128)(2,1)} %constant.82.clone.dleft) | copy-start | bytes 245764
  5.8 29.2 %copy-start.29 = (f32[128,128]{1,0:T(8,128)S(1)}, f32[128,128]{1,0:T(8,128)}, u32[]{:S(2)}) copy-start(f32[128,128]{1,0:T(8,128)} %constant.81.clone.tab) | copy-start | bytes 196612
  5.8 29.2 %copy-start.38 = (bf16[8,192]{1,0:T(8,128)(2,1)S(1)}, bf16[8,192]{1,0:T(8,128)(2,1)}, u32[]{:S(2)}) copy-start(bf16[8,192]{1,0:T(8,128)(2,1)} %constant.84.clone.pleft) | copy-start | bytes 9220
  6.8 17.3 %collective-permute-start = (f32[56,128]{1,0:T(8,128)S(1)}, f32[56,128]{1,0:T(8,128)S(1)}, u32[]{:S(2)}, u32[]{:S(2)}) collective-permute-start(f32[56,128]{1,0:T(8,128)S(1)} %get-tuple-element.34), channel_id=1, source_target_pairs={{0,64},{64,0},{128,192},{192,128},{256,320},{320,256},{384,448},{4... | collective-permute-start | bytes 86024 | tf_op jit(solution)/shard_map/ppermute | solution.py:708
  11.6 13.7 %collective-permute-start.1 = (f32[56,128]{1,0:T(8,128)S(1)}, f32[56,128]{1,0:T(8,128)S(1)}, u32[]{:S(2)}, u32[]{:S(2)}) collective-permute-start(f32[56,128]{1,0:T(8,128)S(1)} %get-tuple-element.35), channel_id=1, source_target_pairs={{64,128},{128,64},{192,256},{256,192},{320,384},{384,320},{448,512... | collective-permute-start | bytes 86024 | tf_op jit(solution)/shard_map/ppermute | solution.py:708
  25.4 9.5 %copy-start.2 = (f32[4,8,8,128]{3,2,1,0:T(8,128)S(1)}, f32[4,8,8,128]{3,2,1,0:T(8,128)}, u32[]{:S(2)}) copy-start(f32[4,8,8,128]{3,2,1,0:T(8,128)} %param.38) | copy-start | bytes 393220
  25.4 9.5 %copy-start.3 = (bf16[384,128]{1,0:T(8,128)(2,1)S(1)}, bf16[384,128]{1,0:T(8,128)(2,1)}, u32[]{:S(2)}) copy-start(bf16[384,128]{1,0:T(8,128)(2,1)} %constant.83.clone.dright.right) | copy-start | bytes 294916
  25.4 9.5 %copy-start.28 = (bf16[256,128]{1,0:T(8,128)(2,1)S(1)}, bf16[256,128]{1,0:T(8,128)(2,1)}, u32[]{:S(2)}) copy-start(bf16[256,128]{1,0:T(8,128)(2,1)} %constant.85.clone.hright) | copy-start | bytes 196612
  26.0 6.9 %collective-permute-start.2 = (f32[56,128]{1,0:T(8,128)S(1)}, f32[56,128]{1,0:T(8,128)S(1)}, u32[]{:S(2)}, u32[]{:S(2)}) collective-permute-start(f32[56,128]{1,0:T(8,128)S(1)} %get-tuple-element.37), channel_id=1, source_target_pairs={{0,1},{1,0},{2,3},{3,2},{4,5},{5,4},{6,7},{7,6},{8,9},{9,8},{10,11... | collective-permute-start | bytes 86024 | tf_op jit(solution)/shard_map/ppermute | solution.py:708
  29.7 5.2 %collective-permute-start.3 = (f32[56,128]{1,0:T(8,128)S(1)}, f32[56,128]{1,0:T(8,128)S(1)}, u32[]{:S(2)}, u32[]{:S(2)}) collective-permute-start(f32[56,128]{1,0:T(8,128)S(1)} %get-tuple-element.38), channel_id=1, source_target_pairs={{1,2},{2,1},{3,4},{4,3},{5,6},{6,5},{7,8},{8,7},{9,10},{10,9},{11,... | collective-permute-start | bytes 86024 | tf_op jit(solution)/shard_map/ppermute | solution.py:708
  36.1 28.6 %copy-start.30 = (bf16[64,384]{1,0:T(8,128)(2,1)S(1)}, bf16[64,384]{1,0:T(8,128)(2,1)}, u32[]{:S(2)}) copy-start(bf16[64,384]{1,0:T(8,128)(2,1)} %constant.86.clone.hart) | copy-start | bytes 147460
  65.5 21.3 %copy-start.7 = (bf16[256,128]{1,0:T(8,128)(2,1)S(1)}, bf16[256,128]{1,0:T(8,128)(2,1)}, u32[]{:S(2)}) copy-start(bf16[256,128]{1,0:T(8,128)(2,1)} %constant.90.clone.er) | copy-start | bytes 196612
  65.5 21.3 %copy-start.8 = (bf16[256,128]{1,0:T(8,128)(2,1)S(1)}, bf16[256,128]{1,0:T(8,128)(2,1)}, u32[]{:S(2)}) copy-start(bf16[256,128]{1,0:T(8,128)(2,1)} %constant.88.clone.etr) | copy-start | bytes 196612
  65.5 21.3 %copy-start.17 = (bf16[64,192]{1,0:T(8,128)(2,1)S(1)}, bf16[64,192]{1,0:T(8,128)(2,1)}, u32[]{:S(2)}) copy-start(bf16[64,192]{1,0:T(8,128)(2,1)} %constant.91.clone.el) | copy-start | bytes 73732
  65.5 21.3 %copy-start.18 = (f32[64,128]{1,0:T(8,128)S(1)}, f32[64,128]{1,0:T(8,128)}, u32[]{:S(2)}) copy-start(f32[64,128]{1,0:T(8,128)} %constant.89.clone.sc) | copy-start | bytes 98308
  65.5 21.3 %copy-start.19 = (bf16[64,192]{1,0:T(8,128)(2,1)S(1)}, bf16[64,192]{1,0:T(8,128)(2,1)}, u32[]{:S(2)}) copy-start(bf16[64,192]{1,0:T(8,128)(2,1)} %constant.87.clone.etl) | copy-start | bytes 73732
  86.8 11.9 %copy-start.5 = (bf16[256,128]{1,0:T(8,128)(2,1)S(1)}, bf16[256,128]{1,0:T(8,128)(2,1)}, u32[]{:S(2)}) copy-start(bf16[256,128]{1,0:T(8,128)(2,1)} %constant.97.clone.czh) | copy-start | bytes 196612
  86.8 11.9 %copy-start.11 = (f32[384,128]{1,0:T(8,128)S(1)}, f32[384,128]{1,0:T(8,128)}, u32[]{:S(2)}) copy-start(f32[384,128]{1,0:T(8,128)} %constant.94.clone.inv) | copy-start | bytes 589828
  86.8 11.9 %copy-start.24 = (f32[144,128]{1,0:T(8,128)S(1)}, f32[144,128]{1,0:T(8,128)}, u32[]{:S(2)}) copy-start(f32[144,128]{1,0:T(8,128)} %constant.92.clone.coef) | copy-start | bytes 221188
  86.8 11.9 %copy-start.27 = (bf16[256,128]{1,0:T(8,128)(2,1)S(1)}, bf16[256,128]{1,0:T(8,128)(2,1)}, u32[]{:S(2)}) copy-start(bf16[256,128]{1,0:T(8,128)(2,1)} %constant.93.clone.twin) | copy-start | bytes 196612
  86.9 11.9 %copy-start.31 = (f32[72,32]{1,0:T(8,128)S(1)}, f32[72,32]{1,0:T(8,128)}, u32[]{:S(2)}) copy-start(f32[72,32]{1,0:T(8,128)} %constant.96.clone.near_high) | copy-start | bytes 27652
  86.9 11.9 %copy-start.32 = (f32[72,32]{1,0:T(8,128)S(1)}, f32[72,32]{1,0:T(8,128)}, u32[]{:S(2)}) copy-start(f32[72,32]{1,0:T(8,128)} %constant.95.clone.near_low) | copy-start | bytes 27652
  88.2 11.9 %collective-permute-start.4 = (f32[96,128]{1,0:T(8,128)S(1)}, f32[96,128]{1,0:T(8,128)S(1)}, u32[]{:S(2)}, u32[]{:S(2)}) collective-permute-start(f32[96,128]{1,0:T(8,128)S(1)} %get-tuple-element.43), channel_id=1, source_target_pairs={{0,1},{1,0},{2,3},{3,2},{4,5},{5,4},{6,7},{7,6},{8,9},{9,8},{10,11... | collective-permute-start | bytes 147464 | tf_op jit(solution)/shard_map/ppermute | solution.py:708
  95.7 5.6 %copy-start = (bf16[768,128]{1,0:T(8,128)(2,1)S(1)}, bf16[768,128]{1,0:T(8,128)(2,1)}, u32[]{:S(2)}) copy-start(bf16[768,128]{1,0:T(8,128)(2,1)} %constant.100.clone.ar) | copy-start | bytes 589828
  95.7 5.6 %copy-start.4 = (f32[192,128]{1,0:T(8,128)S(1)}, f32[192,128]{1,0:T(8,128)}, u32[]{:S(2)}) copy-start(f32[192,128]{1,0:T(8,128)} %constant.98.clone.tab) | copy-start | bytes 294916
  95.7 5.6 %copy-start.6 = (bf16[256,128]{1,0:T(8,128)(2,1)S(1)}, bf16[256,128]{1,0:T(8,128)(2,1)}, u32[]{:S(2)}) copy-start(bf16[256,128]{1,0:T(8,128)(2,1)} %constant.102.clone.hzc) | copy-start | bytes 196612
  95.7 5.6 %copy-start.9 = (bf16[64,320]{1,0:T(8,128)(2,1)S(1)}, bf16[64,320]{1,0:T(8,128)(2,1)}, u32[]{:S(2)}) copy-start(bf16[64,320]{1,0:T(8,128)(2,1)} %constant.99.clone.al) | copy-start | bytes 122884
  95.7 5.6 %copy-start.22 = (bf16[32,288]{1,0:T(8,128)(2,1)S(1)}, bf16[32,288]{1,0:T(8,128)(2,1)}, u32[]{:S(2)}) copy-start(bf16[32,288]{1,0:T(8,128)(2,1)} %constant.101.clone.back) | copy-start | bytes 55300
  95.7 5.5 %collective-permute-start.5 = (f32[96,128]{1,0:T(8,128)S(1)}, f32[96,128]{1,0:T(8,128)S(1)}, u32[]{:S(2)}, u32[]{:S(2)}) collective-permute-start(f32[96,128]{1,0:T(8,128)S(1)} %get-tuple-element.44), channel_id=1, source_target_pairs={{1,2},{2,1},{3,4},{4,3},{5,6},{6,5},{7,8},{8,7},{9,10},{10,9},{11,... | collective-permute-start | bytes 147464 | tf_op jit(solution)/shard_map/ppermute | solution.py:708
  98.8 2.5 %copy-start.34 = (f32[16,128]{1,0:T(8,128)S(1)}, f32[16,128]{1,0:T(8,128)}, u32[]{:S(2)}) copy-start(f32[16,128]{1,0:T(8,128)} %constant.103.clone.hy) | copy-start | bytes 24580
  101.3 12.5 %copy-start.15 = (f32[64,128]{1,0:T(8,128)S(1)}, f32[64,128]{1,0:T(8,128)}, u32[]{:S(2)}) copy-start(f32[64,128]{1,0:T(8,128)} %constant.104.clone.tab.inv_mz) | copy-start | bytes 98308
  103.2 7.2 %collective-permute-start.6 = (f32[96,128]{1,0:T(8,128)S(1)}, f32[96,128]{1,0:T(8,128)S(1)}, u32[]{:S(2)}, u32[]{:S(2)}) collective-permute-start(f32[96,128]{1,0:T(8,128)S(1)} %get-tuple-element.47), channel_id=1, source_target_pairs={{0,1},{1,0},{2,3},{3,2},{4,5},{5,4},{6,7},{7,6},{8,9},{9,8},{10,11... | collective-permute-start | bytes 147464 | tf_op jit(solution)/shard_map/ppermute | solution.py:708
  108.4 5.4 %collective-permute-start.7 = (f32[96,128]{1,0:T(8,128)S(1)}, f32[96,128]{1,0:T(8,128)S(1)}, u32[]{:S(2)}, u32[]{:S(2)}) collective-permute-start(f32[96,128]{1,0:T(8,128)S(1)} %get-tuple-element.48), channel_id=1, source_target_pairs={{1,2},{2,1},{3,4},{4,3},{5,6},{6,5},{7,8},{8,7},{9,10},{10,9},{11,... | collective-permute-start | bytes 147464 | tf_op jit(solution)/shard_map/ppermute | solution.py:708
  115.2 10.7 %copy-start.35 = (bf16[16,192]{1,0:T(8,128)(2,1)S(1)}, bf16[16,192]{1,0:T(8,128)(2,1)}, u32[]{:S(2)}) copy-start(bf16[16,192]{1,0:T(8,128)(2,1)} %constant.105.clone.edge) | copy-start | bytes 18436
  115.2 7.2 %collective-permute-start.8 = (f32[96,128]{1,0:T(8,128)S(1)}, f32[96,128]{1,0:T(8,128)S(1)}, u32[]{:S(2)}, u32[]{:S(2)}) collective-permute-start(f32[96,128]{1,0:T(8,128)S(1)} %get-tuple-element.50), channel_id=1, source_target_pairs={{0,1},{1,0},{2,3},{3,2},{4,5},{5,4},{6,7},{7,6},{8,9},{9,8},{10,11... | collective-permute-start | bytes 147464 | tf_op jit(solution)/shard_map/ppermute | solution.py:708
  120.4 5.4 %collective-permute-start.9 = (f32[96,128]{1,0:T(8,128)S(1)}, f32[96,128]{1,0:T(8,128)S(1)}, u32[]{:S(2)}, u32[]{:S(2)}) collective-permute-start(f32[96,128]{1,0:T(8,128)S(1)} %get-tuple-element.51), channel_id=1, source_target_pairs={{1,2},{2,1},{3,4},{4,3},{5,6},{6,5},{7,8},{8,7},{9,10},{10,9},{11,... | collective-permute-start | bytes 147464 | tf_op jit(solution)/shard_map/ppermute | solution.py:708
  128.6 25.9 %copy-start.14 = (f32[8,8,128]{2,1,0:T(8,128)S(1)}, f32[8,8,128]{2,1,0:T(8,128)}, u32[]{:S(2)}) copy-start(f32[8,8,128]{2,1,0:T(8,128)} %param.40) | copy-start | bytes 98308
  128.6 25.9 %copy-start.16 = (bf16[256,256]{1,0:T(8,128)(2,1)S(1)}, bf16[256,256]{1,0:T(8,128)(2,1)}, u32[]{:S(2)}) copy-start(bf16[256,256]{1,0:T(8,128)(2,1)} %constant.110.clone.gal) | copy-start | bytes 393220
  128.6 25.9 %copy-start.20 = (bf16[128,320]{1,0:T(8,128)(2,1)S(1)}, bf16[128,320]{1,0:T(8,128)(2,1)}, u32[]{:S(2)}) copy-start(bf16[128,320]{1,0:T(8,128)(2,1)} %constant.112.clone.left) | copy-start | bytes 245764
  128.6 25.9 %copy-start.25 = (f32[128,128]{1,0:T(8,128)S(1)}, f32[128,128]{1,0:T(8,128)}, u32[]{:S(2)}) copy-start(f32[128,128]{1,0:T(8,128)} %constant.111.clone.mky) | copy-start | bytes 196612
  128.6 25.9 %copy-start.26 = (bf16[128,192]{1,0:T(8,128)(2,1)S(1)}, bf16[128,192]{1,0:T(8,128)(2,1)}, u32[]{:S(2)}) copy-start(bf16[128,192]{1,0:T(8,128)(2,1)} %constant.107.clone.hart) | copy-start | bytes 147460
  128.6 25.9 %copy-start.33 = (f32[72,64]{1,0:T(8,128)S(1)}, f32[72,64]{1,0:T(8,128)}, u32[]{:S(2)}) copy-start(f32[72,64]{1,0:T(8,128)} %constant.109.clone.around) | copy-start | bytes 55300
  128.6 25.8 %all-to-all-start.1 = ((f32[64,16,128]{2,1,0:T(8,128)}), f32[64,16,128]{2,1,0:T(8,128)S(1)}, u32[]{:S(2)}, u32[]{:S(2)}) async-start(f32[64,16,128]{2,1,0:T(8,128)} %bitcast.6), calls=%async_computation.1 | async-start | bytes 1048576 | tf_op jit(solution)/shard_map/all_to_all | solution.py:838
  136.9 5.6 %collective-permute-start.10 = (f32[16,128]{1,0:T(8,128)S(1)}, f32[16,128]{1,0:T(8,128)S(1)}, u32[]{:S(2)}, u32[]{:S(2)}) collective-permute-start(f32[16,128]{1,0:T(8,128)S(1)} %get-tuple-element.57), channel_id=1, source_target_pairs={{0,1},{1,0},{2,3},{3,2},{4,5},{5,4},{6,7},{7,6},{8,9},{9,8},{10,11... | collective-permute-start | bytes 24584 | tf_op jit(solution)/shard_map/ppermute | solution.py:708
  139.3 15.2 %copy-start.37 = (f32[576]{0:T(1024)S(1)}, f32[576]{0:T(1024)}, u32[]{:S(2)}) copy-start(f32[576]{0:T(1024)} %constant.106.clone.reach) | copy-start | bytes 6916
  139.3 15.2 %copy-start.36 = (f32[8,128]{1,0:T(8,128)S(1)}, f32[8,128]{1,0:T(8,128)}, u32[]{:S(2)}) copy-start(f32[8,128]{1,0:T(8,128)} %constant.108.clone.ez_row) | copy-start | bytes 12292
  139.3 11.4 %collective-permute-start.11 = (f32[16,128]{1,0:T(8,128)S(1)}, f32[16,128]{1,0:T(8,128)S(1)}, u32[]{:S(2)}, u32[]{:S(2)}) collective-permute-start(f32[16,128]{1,0:T(8,128)S(1)} %get-tuple-element.58), channel_id=1, source_target_pairs={{1,2},{2,1},{3,4},{4,3},{5,6},{6,5},{7,8},{8,7},{9,10},{10,9},{11,... | collective-permute-start | bytes 24584 | tf_op jit(solution)/shard_map/ppermute | solution.py:708
  (4 other events, 3.5 us)

commit v3 on v2

--- a/solution.py
+++ b/solution.py
@@ -260,29 +260,20 @@
             2.0 * (ex[:, None, None] + ey[None, :, None] + ez[None, None, :]) + coarse_shift
         )
         shifted = np.roll(hart_y, -1, axis=1)
-        self.hart_cat = left3(np.concatenate([hart_y, shifted], axis=1))
         self.hart_two = left3(np.concatenate([hart_y, shifted], axis=0))
-        hb = ny // 2
-        self.hb = hb
-        coef = np.zeros((nx * nx, NZ))
-        for a in range(nx):
-            for i in range(nx):
-                for base in (0, 64):
-                    coef[a * nx + i, base : base + NV] = self.hart_x[a, i]
-                    coef[a * nx + i, base + NV : base + 2 * NV] = self.hart_x[a, (i + 1) % nx]
-        self.coef = coef.astype(f32)
-        twin = np.zeros((NZ, NZ))
-        twin[:NV, :NV] = cz
-        twin[64 : 64 + NV, 64 : 64 + NV] = cz
-        self.twin_right = right3(twin)
-        packed = np.zeros((nx, hb, NZ))
-        packed[:, :, :NV] = inverse[:, :hb]
-        packed[:, :, 64 : 64 + NV] = inverse[:, hb:]
-        self.inv_packed = packed.reshape(nx * hb, NZ).astype(f32)
+        toward = np.zeros((32, nx * 8))
+        for yv in range(2):
+            for xv in range(2):
+                for i in range(nx):
+                    toward[yv * 16 : yv * 16 + nx, i * 8 + xv * 2 + yv] = self.hart_x[
+                        :, (i + xv) % nx
+                    ]
+        self.toward_left = left3(toward)
+        levels_only = np.zeros((NZ, NZ))
+        levels_only[:NV, :NV] = cz
+        self.levels_right = right3(levels_only)
         near = hart_y[(np.arange(ny + 8) - 1) % ny]
         self.near = near.astype(f32)
-        self.near_low = near[:, :hb].astype(f32)
-        self.near_high = near[:, hb:].astype(f32)
         czh = np.zeros((NZ, NZ))
         czh[:NV] = (hz @ cz).T
         self.czh_right = right3(czh)
@@ -331,9 +322,9 @@
         self.d = d
 
 
-def call(kernel, outs, *args, scratch=(), smem=0):
+def call(kernel, outs, *args, scratch=(), smem=0, space=pltpu.VMEM, limit=VMEM_LIMIT):
     specs = [pl.BlockSpec(memory_space=pltpu.SMEM)] * smem
-    specs += [pl.BlockSpec(memory_space=pltpu.VMEM)] * (len(args) - smem)
+    specs += [pl.BlockSpec(memory_space=space)] * (len(args) - smem)
     return pl.pallas_call(
         kernel,
         out_shape=[jax.ShapeDtypeStruct(shape, jnp.float32) for shape in outs],
@@ -341,12 +332,22 @@
         out_specs=[pl.BlockSpec(memory_space=pltpu.VMEM)] * len(outs),
         scratch_shapes=list(scratch),
         interpret=INTERPRET,
-        compiler_params=pltpu.CompilerParams(vmem_limit_bytes=VMEM_LIMIT),
+        compiler_params=pltpu.CompilerParams(vmem_limit_bytes=limit),
         name=kernel.__name__,
     )(*args)
 
 
-def stage_rate(idx, h, flow, old, left, right, tab, fld, xa, xb, kp):
+def stage_rate(idx, h, *refs):
+    sources, (fld, xa, xb, kp), landed, sems = refs[:5], refs[5:9], refs[9:14], refs[14]
+    copies = [
+        pltpu.make_async_copy(source, place, sems.at[k])
+        for k, (source, place) in enumerate(zip(sources, landed))
+    ]
+    for copy in copies:
+        copy.start()
+    for copy in copies:
+        copy.wait()
+    flow, old, left, right, tab = landed
     f = [flow[q * 64 : q * 64 + 64] for q in range(4)]
     p = old[...]
     lx = lmul(left[...], jnp.concatenate(f + [p], axis=1))
@@ -413,10 +414,10 @@
 
 
 def make_stages(t):
-    nx, ny, hb = t.nx, t.ny, t.hb
+    nx, ny = t.nx, t.ny
 
     def stage_state(
-        idx, fx, below, above, flow, kp, tab, dleft, dright, pleft, hright, prov, g0, rz, msg, scr
+        idx, fx, below, above, flow, kp, tab, dleft, dright, pleft, hright, prov, g0, piece, scr
     ):
         scr[...] = fx[...]
         add_faces(is_odd(idx[1]), scr, below, above)
@@ -434,65 +435,55 @@
             g0[k * 64 : k * 64 + 64] = scr[(4 + k) * 64 : (5 + k) * 64] * inv_bm
         div = lmul(dleft[...], jnp.concatenate(new[:2], axis=0)) + rmul(new[2], dright[...])
         joined = join_z(-mass * div - kp[...])
-        rz[...] = joined
-        coarse = rmul(lmul(pleft[...], joined), hright[...])
-        face0 = rz[pl.ds(0, 8, stride=8), :]
-        face7 = rz[pl.ds(7, 8, stride=8), :]
+        piece[0:64] = joined
+        piece[64:72] = rmul(lmul(pleft[...], joined), hright[...])
+
+    def send(msg, block):
         for k in range(ny):
-            msg[k * 16 : k * 16 + 8] = face0
-            msg[k * 16 + 8 : k * 16 + 16] = coarse
-        after = lax.rem(idx[1] + 1, ny)
-        msg[pl.ds(pl.multiple_of(after * 16, 16), 8), :] = face7
-
-    def stage_residual(idx, rec, rz, hart, out):
-        out[0:64] = rz[...]
-        before = lax.rem(idx[1] + ny - 1, ny)
-        after = lax.rem(idx[1] + 1, ny)
-        below = rec[pl.ds(pl.multiple_of(before * 16, 16), 8), :]
-        above = rec[pl.ds(pl.multiple_of(after * 16, 16), 8), :]
-        out[pl.ds(0, 8, stride=8), :] = out[pl.ds(0, 8, stride=8), :] + below
-        out[pl.ds(7, 8, stride=8), :] = out[pl.ds(7, 8, stride=8), :] + above
-        m = [rec[pl.ds(8 + r, ny, stride=16), :] for r in range(4)]
-        top = m[0] + turn(m[2], NV)
-        low = m[1] + turn(m[3], NV)
-        modes = lmul(hart[...], jnp.concatenate([top, low], axis=0))
-        out[64 : 64 + hb] = modes[0:hb] + turn(modes[hb:ny], 64)
+            msg[k * 16 : k * 16 + 16] = block
+
+    def stage_ring(idx, ring, toward, levels, r, ra, rb, msg):
+        rows = jnp.concatenate([ring[i * 72 : i * 72 + 64] for i in range(nx)], axis=0)
+        r[...] = join_x(rows, nx)
+        swap_faces(is_odd(idx[1]), r, ra, rb)
+        corners = jnp.concatenate([ring[i * 72 + 64 : i * 72 + 72] for i in range(nx)], axis=0)
+        modes = rmul(lmul(toward[...], corners), levels[...])
+        send(msg, modes[0:16] + turn(modes[16:32], 32))
 
     def smoothed(field, etl, etr, sc, er, el):
         modal = rmul(rows_of(lmul(etl, lanes_of(field))), etr)
         modal = rmul(modal * tiled(sc, nx), er)
         return rows_of(lmul(el, lanes_of(modal)))
 
-    def stage_smooth(idx, ring, etl, etr, sc, er, el, r0, s, s0, s7):
-        size = 64 + hb
-        rows = jnp.concatenate([ring[i * size : i * size + 64] for i in range(nx)], axis=0)
-        residual = join_x(rows, nx)
-        r0[...] = residual
-        s[...] = join_x(smoothed(residual, etl[...], etr[...], sc[...], er[...], el[...]), nx)
+    def stage_smooth(idx, r, ra, rb, etl, etr, sc, er, el, r0, s, s0, s7):
+        r0[...] = r[...]
+        add_faces(is_odd(idx[1]), r0, ra, rb)
+        local = smoothed(r0[...], etl[...], etr[...], sc[...], er[...], el[...])
+        s[...] = join_x(local, nx)
         swap_faces(is_odd(idx[1]), s, s0, s7)
 
-    def stage_coarse(idx, ring, coef, twin, inv, near_low, near_high, czh, out):
-        size = 64 + hb
-        grid = [ring[i * size + 64 : (i + 1) * size] for i in range(nx)]
-        modes = []
-        for a in range(nx):
-            acc = grid[0] * coef[a * nx : a * nx + 1]
-            for i in range(1, nx):
-                acc = acc + grid[i] * coef[a * nx + i : a * nx + i + 1]
-            modes.append(acc + turn(acc, -NV))
-        values = rmul(jnp.concatenate(modes, axis=0), twin[...]) * inv[...]
-        wide = lanes_of(values, hb)
-        low = thrice(near_low[pl.ds(idx[1], 8), :], wide)
-        high = thrice(near_high[pl.ds(idx[1], 8), :], wide)
-        lines = []
+    def spectra(rec, hart, ez_row, ky):
+        cells = jnp.concatenate([rec[pl.ds(a, ny, stride=16), :] for a in range(nx)], axis=1)
+        both = lmul(hart, cells)
+        lane = lane_index(ny)
+        levels = 2.0 * (2.0 * ky + ez_row) + coarse_shift
+        found = []
         for a in range(nx):
             tile = slice(a * NZ, (a + 1) * NZ)
-            lines.append(low[:, tile] + turn(high[:, tile], 64))
+            comb = both[0:ny, tile] + turn(both[ny : 2 * ny, tile], -32)
+            e = jnp.where(lane < NV, comb / (levels + 2.0 * float(t.ex[a])), 0.0)
+            found.append((comb, e))
+        return found
+
+    def stage_coarse(idx, rec, hart, ez_row, mky, around, czh, out):
+        found = spectra(rec, hart[...], ez_row[0:1], mky[ny : 2 * ny])
+        wide = jnp.concatenate([e for _, e in found], axis=1)
+        lines = thrice(around[pl.ds(idx[1], 8), :], wide)
         columns = []
         for i in range(nx):
-            acc = lines[0] * float(t.hart_x[i, 0])
+            acc = lines[:, 0:NZ] * float(t.hart_x[i, 0])
             for a in range(1, nx):
-                acc = acc + lines[a] * float(t.hart_x[i, a])
+                acc = acc + lines[:, a * NZ : (a + 1) * NZ] * float(t.hart_x[i, a])
             columns.append(acc)
         out[...] = rmul(jnp.concatenate(columns, axis=0), czh[...])
 
@@ -563,8 +554,7 @@
         values = [total(sums1[0:8]), total(sums1[8:16]), total(sums2[...]), last]
         for k, value in enumerate(values):
             block = block + jnp.where((row == 12) & (lane == NV + k), value, 0.0)
-        for k in range(ny):
-            msg[k * 16 : k * 16 + 16] = block
+        send(msg, block)
         base = pl.multiple_of(idx[0] * 64, 64)
         pair = jnp.concatenate([z0[pl.ds(base, 64), :], sq[pl.ds(base, 64), :]], axis=1)
         slopes = lmul(edge[...], pair)
@@ -597,18 +587,11 @@
         press,
         scr,
     ):
-        cells = jnp.concatenate([rec[pl.ds(a, ny, stride=16), :] for a in range(nx)], axis=1)
-        both = lmul(hart[...], cells)
         my, ky = mky[0:ny], mky[ny : 2 * ny]
-        lane = lane_index(ny)
-        found = []
-        levels = 2.0 * (2.0 * ky + ez_row[0:1]) + coarse_shift
         cross = jnp.zeros((ny, NZ), jnp.float32)
         plain = jnp.zeros((ny, NZ), jnp.float32)
-        for a in range(nx):
-            tile = slice(a * NZ, (a + 1) * NZ)
-            comb = both[0:ny, tile] + turn(both[ny : 2 * ny, tile], -32)
-            e = jnp.where(lane < NV, comb / (levels + 2.0 * float(t.ex[a])), 0.0)
+        found = []
+        for comb, e in spectra(rec, hart[...], ez_row[0:1], ky):
             found.append(e)
             plain = plain + e * comb
             cross = cross + e * turn(comb, -64)
@@ -691,7 +674,7 @@
 
     return (
         stage_state,
-        stage_residual,
+        stage_ring,
         stage_smooth,
         stage_coarse,
         stage_apply,
@@ -709,10 +692,10 @@
 
 
 def make_device(t):
-    nx, ny, hb = t.nx, t.ny, t.hb
+    nx, ny = t.nx, t.ny
     (
         stage_state,
-        stage_residual,
+        stage_ring,
         stage_smooth,
         stage_coarse,
         stage_apply,
@@ -738,15 +721,25 @@
             c(t.k1_right),
             c(t.visc),
             smem=2,
+            space=pltpu.HBM,
+            limit=60 * 1024 * 1024,
+            scratch=[
+                pltpu.VMEM((256, NZ), jnp.float32),
+                pltpu.VMEM((64, NZ), jnp.float32),
+                pltpu.VMEM(t.k1_left.shape, jnp.bfloat16),
+                pltpu.VMEM(t.k1_right.shape, jnp.bfloat16),
+                pltpu.VMEM(t.visc.shape, jnp.float32),
+                pltpu.SemaphoreType.DMA((5,)),
+            ],
         )
         below, above = exchange("gx", xf0, xf7)
         fld, yf0, yf7 = call(
             stage_faces, [(448, NZ), (56, NZ), (56, NZ)], idx, fld, below, above, smem=1
         )
         below, above = exchange("gy", yf0, yf7)
-        prov, g0, rz, msg = call(
+        prov, g0, piece = call(
             stage_state,
-            [(256, NZ), (192, NZ), col, (ny * 16, NZ)],
+            [(256, NZ), (192, NZ), (72, NZ)],
             idx,
             fld,
             below,
@@ -761,32 +754,32 @@
             smem=1,
             scratch=[pltpu.VMEM((448, NZ), jnp.float32)],
         )
+        whole = lax.all_gather(piece, "gx", axis=0, tiled=True)
+        r, ra, rb, msg = call(
+            stage_ring,
+            [ring, face, face, (ny * 16, NZ)],
+            idx,
+            whole,
+            c(t.toward_left),
+            c(t.levels_right),
+            smem=1,
+        )
         rec = lax.all_to_all(msg.reshape(ny, 16, NZ), "gy", 0, 0, tiled=True)
-        (piece,) = call(
-            stage_residual,
-            [(64 + hb, NZ)],
-            idx,
-            rec.reshape(ny * 16, NZ),
-            rz,
-            c(t.hart_cat),
-            smem=1,
-        )
-        whole = lax.all_gather(piece, "gx", axis=0, tiled=True)
+        below, above = exchange("gy", ra, rb)
         smoother = (c(t.et_left), c(t.et_right), c(t.scale), c(t.e_right), c(t.e_left))
         r0, s, s0, s7 = call(
-            stage_smooth, [ring, ring, face, face], idx, whole, *smoother, smem=1
+            stage_smooth, [ring, ring, face, face], idx, r, below, above, *smoother, smem=1
         )
         below, above = exchange("gy", s0, s7)
         (vert,) = call(
             stage_coarse,
             [face],
             idx,
-            whole,
-            c(t.coef),
-            c(t.twin_right),
-            c(t.inv_packed),
-            c(t.near_low),
-            c(t.near_high),
+            rec.reshape(ny * 16, NZ),
+            c(t.hart_two),
+            c(t.ez_row),
+            c(t.mky),
+            c(t.near),
             c(t.czh_right),
             smem=1,
         )

time: 158 us -> 157 us (level)
  blocking collectives: 49.8 us -> 20.5 us
  starting transfers between devices: 62.7 us -> 80.9 us
  waiting for transfers between devices: 23.3 us -> 33.2 us
  Pallas kernels: 14.6 us -> 17.5 us
  local copies, waits for them, and re-layouts: 4.58 us -> 1.87 us
    all_to_all x1 -> x0, blocking collectives: 28.6 us -> none  [on_device(): rec = lax.all_to_all(msg.reshape(ny, 16, NZ), 'gy', 0, 0, tiled=True)]
    all_to_all x1 -> x2, starting transfers between devices: 8.26 us -> 24.2 us  [on_device(): rec = lax.all_to_all(msg.reshape(ny, 16, NZ), 'gy', 0, 0, tiled=True)]
    ppermute x6 -> x7, waiting for transfers between devices: 19.5 us -> 29.3 us  [exchange(): lax.ppermute(second, axis, across)]
    pallas_call x10, Pallas kernels: 14.6 us -> 17.5 us  [call(): pl.pallas_call(kernel, out_shape=[jax.ShapeDtypeStruct(shape, jnp.float32...]
    unnamed x78 -> x66, local copies, waits for them, and re-layouts: 4.58 us -> 1.87 us
    ppermute x6 -> x7, starting transfers between devices: 25.6 us -> 27.6 us  [exchange(): lax.ppermute(second, axis, across)]
    ppermute x6 -> x7, starting transfers between devices: 28.8 us -> 29 us  [exchange(): lax.ppermute(first, axis, pairs)]
    all_to_all x1 -> x2, waiting for transfers between devices: 3.81 us -> 3.91 us  [on_device(): rec = lax.all_to_all(msg.reshape(ny, 16, NZ), 'gy', 0, 0, tiled=True)]
  transfers between devices with their start and end apart: 13 -> 16, of which waited for: 7 -> 8; matrix products, arithmetic and copies ran while one was open for 0% -> 0% of each run, Pallas kernels for 1% -> 2%
where the time goes in v3:
time: 157 us; the launch traced here: 156 us
  starting transfers between devices  80.9 us (52%)
  waiting for transfers between devices  33.2 us (21%)
  blocking collectives  20.5 us (13%)
  Pallas kernels  17.5 us (11%)
  local copies, waits for them, and re-layouts  1.87 us (1%)
  between operations  1.79 us (1%)
    ppermute x7, waiting for transfers between devices, exchange(): lax.ppermute(second, axis, across)  29.3 us
    ppermute x7, starting transfers between devices, exchange(): lax.ppermute(first, axis, pairs)  29 us
    ppermute x7, starting transfers between devices, exchange(): lax.ppermute(second, axis, across)  27.6 us
    all_to_all x2, starting transfers between devices, on_device(): rec = lax.all_to_all(msg.reshape(ny, 16, NZ), 'gy', 0, 0, tiled=True)  24.2 us
    all_gather x1, blocking collectives, on_device(): whole = lax.all_gather(piece, 'gx', axis=0, tiled=True)  20.5 us
    pallas_call x10, Pallas kernels, call(): pl.pallas_call(kernel, out_shape=[jax.ShapeDtypeStruct(shape, jnp.float32...  17.5 us
    all_to_all x2, waiting for transfers between devices, on_device(): rec = lax.all_to_all(msg.reshape(ny, 16, NZ), 'gy', 0, 0, tiled=True)  3.91 us
  transfers between devices with their start and end apart: 16, of which 8 were waited for; matrix products, arithmetic and copies ran while one was open for 0% of the time, Pallas kernels for 2%

profile of v3, /device:TPU:1, one launch (start us, length us, event | category | flops | bytes accessed | tf_op | source)
XLA Modules:
  0.0 156.3 jit_solution(4976816266913673386)
XLA Ops:
  1.3 0.6 pad_add_fusion.idx
  1.9 3.2 %stage_rate.1 = (f32[448,128]{1,0:T(8,128)}, f32[56,128]{1,0:T(8,128)}, f32[56,128]{1,0:T(8,128)}, f32[64,128]{1,0:T(8,128)}) custom-call(s32[2]{0:T(128)} %pad_add_fusion.idx, s32[1,1]{1,0:T(1,128)S(6)} %copy.36.h, f32[256,128]{1,0:T(8,128)} %bitcast.12, f32[64,128]{1,0:T(8,128)} %bitcast.14, bf16[192,320]{1,0:T(8,128)(2,1)} %constant.70.clone.refs_2_, ...), custom_call_target="tpu_custom_call" | custom-call | tf_op jit(solution)/shard_map/stage_rate/pallas_call | solution.py:328
  5.1 4.8 %collective-permute-start = (f32[56,128]{1,0:T(8,128)}, f32[56,128]{1,0:T(8,128)S(1)}, u32[]{:S(2)}, u32[]{:S(2)}) collective-permute-start(f32[56,128]{1,0:T(8,128)} %get-tuple-element.37), channel_id=1, source_target_pairs={{0,64},{64,0},{128,192},{192,128},{256,320},{320,256},{384,448},{4... | collective-permute-start | bytes 86024 | tf_op jit(solution)/shard_map/ppermute | solution.py:691
  9.9 12.5 %collective-permute-start.1 = (f32[56,128]{1,0:T(8,128)}, f32[56,128]{1,0:T(8,128)S(1)}, u32[]{:S(2)}, u32[]{:S(2)}) collective-permute-start(f32[56,128]{1,0:T(8,128)} %get-tuple-element.38), channel_id=1, source_target_pairs={{64,128},{128,64},{192,256},{256,192},{320,384},{384,320},{448,512... | collective-permute-start | bytes 86024 | tf_op jit(solution)/shard_map/ppermute | solution.py:691
  22.4 1.4 collective-permute-done.1.xb
  23.9 0.9 copy-done.10
  24.8 0.6 stage_faces.1
  25.4 3.7 %collective-permute-start.2 = (f32[56,128]{1,0:T(8,128)S(1)}, f32[56,128]{1,0:T(8,128)S(1)}, u32[]{:S(2)}, u32[]{:S(2)}) collective-permute-start(f32[56,128]{1,0:T(8,128)S(1)} %get-tuple-element.40), channel_id=1, source_target_pairs={{0,1},{1,0},{2,3},{3,2},{4,5},{5,4},{6,7},{7,6},{8,9},{9,8},{10,11... | collective-permute-start | bytes 86024 | tf_op jit(solution)/shard_map/ppermute | solution.py:691
  29.1 3.1 %collective-permute-start.3 = (f32[56,128]{1,0:T(8,128)S(1)}, f32[56,128]{1,0:T(8,128)S(1)}, u32[]{:S(2)}, u32[]{:S(2)}) collective-permute-start(f32[56,128]{1,0:T(8,128)S(1)} %get-tuple-element.41), channel_id=1, source_target_pairs={{1,2},{2,1},{3,4},{4,3},{5,6},{6,5},{7,8},{8,7},{9,10},{10,9},{11,... | collective-permute-start | bytes 86024 | tf_op jit(solution)/shard_map/ppermute | solution.py:691
  32.2 2.1 %collective-permute-done.3.above = f32[56,128]{1,0:T(8,128)S(1)} collective-permute-done((f32[56,128]{1,0:T(8,128)S(1)}, f32[56,128]{1,0:T(8,128)S(1)}, u32[]{:S(2)}, u32[]{:S(2)}) %collective-permute-start.3) | collective-permute-done | bytes 28704 | tf_op jit(solution)/shard_map/ppermute | solution.py:691
  34.4 0.7 copy-done.27
  35.1 1.1 stage_state.1
  36.2 0.0 copy-start.28
  36.2 20.5 %all_gather.3.ring = f32[864,128]{1,0:T(8,128)S(1)} all-gather(f32[72,128]{1,0:T(8,128)S(1)} %get-tuple-element.43), channel_id=1, replica_groups=mesh['gx'=12,'gy'=64] {'gx'}, dimensions={0}, use_global_device_ids=true | all-gather | bytes 479232 | tf_op jit(solution)/shard_map/all_gather | solution.py:757
  56.7 1.8 %stage_ring.1 = (f32[768,128]{1,0:T(8,128)S(1)}, f32[96,128]{1,0:T(8,128)S(1)}, f32[96,128]{1,0:T(8,128)S(1)}, f32[1024,128]{1,0:T(8,128)}) custom-call(s32[2]{0:T(128)S(1)} %copy-done.25, f32[864,128]{1,0:T(8,128)S(1)} %all_gather.3.ring, bf16[32,288]{1,0:T(8,128)(2,1)S(1)} %copy-done.28, bf16[256,128]{1,0:T(8,128)(2,1)S(1)} %copy-done.22), custom_call_target="tpu_custom_call" | custom-call | tf_op jit(solution)/shard_map/stage_ring/pallas_call | solution.py:328
  58.5 0.0 copy-start.18
  58.5 16.7 %all-to-all-start = ((f32[64,16,128]{2,1,0:T(8,128)}), f32[64,16,128]{2,1,0:T(8,128)S(1)}, u32[]{:S(2)}, u32[]{:S(2)}) async-start(f32[64,16,128]{2,1,0:T(8,128)} %bitcast.4), calls=%async_computation | async-start | bytes 1048576 | tf_op jit(solution)/shard_map/all_to_all | solution.py:767
  75.2 2.4 %collective-permute-start.4 = (f32[96,128]{1,0:T(8,128)S(1)}, f32[96,128]{1,0:T(8,128)S(1)}, u32[]{:S(2)}, u32[]{:S(2)}) collective-permute-start(f32[96,128]{1,0:T(8,128)S(1)} %get-tuple-element.45), channel_id=1, source_target_pairs={{0,1},{1,0},{2,3},{3,2},{4,5},{5,4},{6,7},{7,6},{8,9},{9,8},{10,11... | collective-permute-start | bytes 147464 | tf_op jit(solution)/shard_map/ppermute | solution.py:691
  77.5 3.2 %collective-permute-start.5 = (f32[96,128]{1,0:T(8,128)S(1)}, f32[96,128]{1,0:T(8,128)S(1)}, u32[]{:S(2)}, u32[]{:S(2)}) collective-permute-start(f32[96,128]{1,0:T(8,128)S(1)} %get-tuple-element.46), channel_id=1, source_target_pairs={{1,2},{2,1},{3,4},{4,3},{5,6},{6,5},{7,8},{8,7},{9,10},{10,9},{11,... | collective-permute-start | bytes 147464 | tf_op jit(solution)/shard_map/ppermute | solution.py:691
  80.8 8.6 %collective-permute-done.5.rb = f32[96,128]{1,0:T(8,128)S(1)} collective-permute-done((f32[96,128]{1,0:T(8,128)S(1)}, f32[96,128]{1,0:T(8,128)S(1)}, u32[]{:S(2)}, u32[]{:S(2)}) %collective-permute-start.5) | collective-permute-done | bytes 49184 | tf_op jit(solution)/shard_map/ppermute | solution.py:691
  89.4 0.0 copy-start.7
  89.4 0.0 copy-start.8
  89.4 0.0 copy-start.9
  89.5 1.3 stage_smooth.1
  90.8 5.2 %collective-permute-start.6 = (f32[96,128]{1,0:T(8,128)S(1)}, f32[96,128]{1,0:T(8,128)S(1)}, u32[]{:S(2)}, u32[]{:S(2)}) collective-permute-start(f32[96,128]{1,0:T(8,128)S(1)} %get-tuple-element.48), channel_id=1, source_target_pairs={{0,1},{1,0},{2,3},{3,2},{4,5},{5,4},{6,7},{7,6},{8,9},{9,8},{10,11... | collective-permute-start | bytes 147464 | tf_op jit(solution)/shard_map/ppermute | solution.py:691
  96.0 1.9 %collective-permute-start.7 = (f32[96,128]{1,0:T(8,128)S(1)}, f32[96,128]{1,0:T(8,128)S(1)}, u32[]{:S(2)}, u32[]{:S(2)}) collective-permute-start(f32[96,128]{1,0:T(8,128)S(1)} %get-tuple-element.49), channel_id=1, source_target_pairs={{1,2},{2,1},{3,4},{4,3},{5,6},{6,5},{7,8},{8,7},{9,10},{10,9},{11,... | collective-permute-start | bytes 147464 | tf_op jit(solution)/shard_map/ppermute | solution.py:691
  98.0 0.0 copy-start
  98.0 0.0 copy-start.3
  98.0 0.0 copy-start.4
  98.0 0.0 copy-start.11
  98.0 0.0 copy-start.20
  98.0 1.3 stage_coarse.1.vert
  99.3 2.1 %collective-permute-done.7.above = f32[96,128]{1,0:T(8,128)S(1)} collective-permute-done((f32[96,128]{1,0:T(8,128)S(1)}, f32[96,128]{1,0:T(8,128)S(1)}, u32[]{:S(2)}, u32[]{:S(2)}) %collective-permute-start.7) | collective-permute-done | bytes 49184 | tf_op jit(solution)/shard_map/ppermute | solution.py:691
  101.4 1.8 %stage_apply.1 = (f32[768,128]{1,0:T(8,128)S(1)}, f32[768,128]{1,0:T(8,128)S(1)}, f32[96,128]{1,0:T(8,128)S(1)}, f32[96,128]{1,0:T(8,128)S(1)}, f32[32,128]{1,0:T(8,128)S(1)}, /*index=5*/f32[16,128]{1,0:T(8,128)S(1)}) custom-call(s32[2]{0:T(128)S(1)} %copy-done.25, f32[768,128]{1,0:T(8,128)S(1)} %get-tuple-element.47.s, ...), custom_call_target="tpu_custom_call" | custom-call | tf_op jit(solution)/shard_map/stage_apply/pallas_call | solution.py:328
  103.3 5.2 %collective-permute-start.8 = (f32[96,128]{1,0:T(8,128)S(1)}, f32[96,128]{1,0:T(8,128)S(1)}, u32[]{:S(2)}, u32[]{:S(2)}) collective-permute-start(f32[96,128]{1,0:T(8,128)S(1)} %get-tuple-element.53), channel_id=1, source_target_pairs={{0,1},{1,0},{2,3},{3,2},{4,5},{5,4},{6,7},{7,6},{8,9},{9,8},{10,11... | collective-permute-start | bytes 147464 | tf_op jit(solution)/shard_map/ppermute | solution.py:691
  108.5 1.9 %collective-permute-start.9 = (f32[96,128]{1,0:T(8,128)S(1)}, f32[96,128]{1,0:T(8,128)S(1)}, u32[]{:S(2)}, u32[]{:S(2)}) collective-permute-start(f32[96,128]{1,0:T(8,128)S(1)} %get-tuple-element.54), channel_id=1, source_target_pairs={{1,2},{2,1},{3,4},{4,3},{5,6},{6,5},{7,8},{8,7},{9,10},{10,9},{11,... | collective-permute-start | bytes 147464 | tf_op jit(solution)/shard_map/ppermute | solution.py:691
  110.5 3.5 %collective-permute-done.9.above = f32[96,128]{1,0:T(8,128)S(1)} collective-permute-done((f32[96,128]{1,0:T(8,128)S(1)}, f32[96,128]{1,0:T(8,128)S(1)}, u32[]{:S(2)}, u32[]{:S(2)}) %collective-permute-start.9) | collective-permute-done | bytes 49184 | tf_op jit(solution)/shard_map/ppermute | solution.py:691
  113.9 1.4 stage_again.1
  115.3 5.2 %collective-permute-start.10 = (f32[96,128]{1,0:T(8,128)S(1)}, f32[96,128]{1,0:T(8,128)S(1)}, u32[]{:S(2)}, u32[]{:S(2)}) collective-permute-start(f32[96,128]{1,0:T(8,128)S(1)} %get-tuple-element.56), channel_id=1, source_target_pairs={{0,1},{1,0},{2,3},{3,2},{4,5},{5,4},{6,7},{7,6},{8,9},{9,8},{10,11... | collective-permute-start | bytes 147464 | tf_op jit(solution)/shard_map/ppermute | solution.py:691
  120.5 1.9 %collective-permute-start.11 = (f32[96,128]{1,0:T(8,128)S(1)}, f32[96,128]{1,0:T(8,128)S(1)}, u32[]{:S(2)}, u32[]{:S(2)}) collective-permute-start(f32[96,128]{1,0:T(8,128)S(1)} %get-tuple-element.57), channel_id=1, source_target_pairs={{1,2},{2,1},{3,4},{4,3},{5,6},{6,5},{7,8},{8,7},{9,10},{10,9},{11,... | collective-permute-start | bytes 147464 | tf_op jit(solution)/shard_map/ppermute | solution.py:691
  122.5 3.5 %collective-permute-done.11.above = f32[96,128]{1,0:T(8,128)S(1)} collective-permute-done((f32[96,128]{1,0:T(8,128)S(1)}, f32[96,128]{1,0:T(8,128)S(1)}, u32[]{:S(2)}, u32[]{:S(2)}) %collective-permute-start.11) | collective-permute-done | bytes 49184 | tf_op jit(solution)/shard_map/ppermute | solution.py:691
  126.0 2.7 %stage_gather.1 = (f32[768,128]{1,0:T(8,128)S(1)}, f32[1024,128]{1,0:T(8,128)}, f32[16,128]{1,0:T(8,128)S(1)}, f32[16,128]{1,0:T(8,128)S(1)}) custom-call(s32[2]{0:T(128)S(1)} %copy-done.25, f32[768,128]{1,0:T(8,128)S(1)} %get-tuple-element.55.s, f32[96,128]{1,0:T(8,128)S(1)} %collective-permute-done.10.below, f32[96,128]{1,0:T(8,128)S(1)} %collective-permute-done.11.above, ...), custom_call_target="tpu_custom_call" | custom-call | tf_op jit(solution)/shard_map/stage_gather/pallas_call | solution.py:328
  128.7 7.5 %all-to-all-start.1 = ((f32[64,16,128]{2,1,0:T(8,128)}), f32[64,16,128]{2,1,0:T(8,128)S(1)}, u32[]{:S(2)}, u32[]{:S(2)}) async-start(f32[64,16,128]{2,1,0:T(8,128)} %bitcast.6), calls=%async_computation.1 | async-start | bytes 1048576 | tf_op jit(solution)/shard_map/all_to_all | solution.py:831
  136.2 2.5 %collective-permute-start.12 = (f32[16,128]{1,0:T(8,128)S(1)}, f32[16,128]{1,0:T(8,128)S(1)}, u32[]{:S(2)}, u32[]{:S(2)}) collective-permute-start(f32[16,128]{1,0:T(8,128)S(1)} %get-tuple-element.63), channel_id=1, source_target_pairs={{0,1},{1,0},{2,3},{3,2},{4,5},{5,4},{6,7},{7,6},{8,9},{9,8},{10,11... | collective-permute-start | bytes 24584 | tf_op jit(solution)/shard_map/ppermute | solution.py:691
  138.7 3.1 %collective-permute-start.13 = (f32[16,128]{1,0:T(8,128)S(1)}, f32[16,128]{1,0:T(8,128)S(1)}, u32[]{:S(2)}, u32[]{:S(2)}) collective-permute-start(f32[16,128]{1,0:T(8,128)S(1)} %get-tuple-element.64), channel_id=1, source_target_pairs={{1,2},{2,1},{3,4},{4,3},{5,6},{6,5},{7,8},{8,7},{9,10},{10,9},{11,... | collective-permute-start | bytes 24584 | tf_op jit(solution)/shard_map/ppermute | solution.py:691
  141.8 8.2 %collective-permute-done.13.above = f32[16,128]{1,0:T(8,128)S(1)} collective-permute-done((f32[16,128]{1,0:T(8,128)S(1)}, f32[16,128]{1,0:T(8,128)S(1)}, u32[]{:S(2)}, u32[]{:S(2)}) %collective-permute-start.13) | collective-permute-done | bytes 8224 | tf_op jit(solution)/shard_map/ppermute | solution.py:691
  150.0 3.9 %all-to-all-done.1 = f32[64,16,128]{2,1,0:T(8,128)S(1)} async-done(((f32[64,16,128]{2,1,0:T(8,128)}), f32[64,16,128]{2,1,0:T(8,128)S(1)}, u32[]{:S(2)}, u32[]{:S(2)}) %all-to-all-start.1) | async-done | bytes 524320 | tf_op jit(solution)/shard_map/all_to_all | solution.py:831
  153.9 2.4 %stage_final.1 = (f32[256,128]{1,0:T(8,128)}, f32[64,128]{1,0:T(8,128)}) custom-call(s32[2]{0:T(128)S(1)} %copy-done.25, f32[576]{0:T(1024)S(1)} %copy-done.31, f32[1024,128]{1,0:T(8,128)S(1)} %bitcast.10, f32[16,128]{1,0:T(8,128)S(1)} %collective-permute-done.12.below, f32[16,128]{1,0:T(8,128)S(1)} %collective-permute-done.13.above, ...), custom_call_target="tpu_custom_call" | custom-call | tf_op jit(solution)/shard_map/stage_final/pallas_call | solution.py:328
  (62 shorter events, 0.1 us)
Async XLA Ops:
  1.9 32.5 %copy-start.21 = (bf16[64,640]{1,0:T(8,128)(2,1)S(1)}, bf16[64,640]{1,0:T(8,128)(2,1)}, u32[]{:S(2)}) copy-start(bf16[64,640]{1,0:T(8,128)(2,1)} %constant.74.clone.dleft) | copy-start | bytes 245764
  1.9 32.5 %copy-start.24 = (f32[128,128]{1,0:T(8,128)S(1)}, f32[128,128]{1,0:T(8,128)}, u32[]{:S(2)}) copy-start(f32[128,128]{1,0:T(8,128)} %constant.73.clone.tab) | copy-start | bytes 196612
  1.9 32.5 %copy-start.32 = (bf16[8,192]{1,0:T(8,128)(2,1)S(1)}, bf16[8,192]{1,0:T(8,128)(2,1)}, u32[]{:S(2)}) copy-start(bf16[8,192]{1,0:T(8,128)(2,1)} %constant.76.clone.pleft) | copy-start | bytes 9220
  5.1 17.3 %collective-permute-start = (f32[56,128]{1,0:T(8,128)}, f32[56,128]{1,0:T(8,128)S(1)}, u32[]{:S(2)}, u32[]{:S(2)}) collective-permute-start(f32[56,128]{1,0:T(8,128)} %get-tuple-element.37), channel_id=1, source_target_pairs={{0,64},{64,0},{128,192},{192,128},{256,320},{320,256},{384,448},{4... | collective-permute-start | bytes 86024 | tf_op jit(solution)/shard_map/ppermute | solution.py:691
  9.9 14.0 %copy-start.25 = (s32[2]{0:T(128)S(1)}, s32[2]{0:T(128)}, u32[]{:S(2)}) copy-start(s32[2]{0:T(128)} %pad_add_fusion.idx) | copy-start | bytes 28
  9.9 13.9 %collective-permute-start.1 = (f32[56,128]{1,0:T(8,128)}, f32[56,128]{1,0:T(8,128)S(1)}, u32[]{:S(2)}, u32[]{:S(2)}) collective-permute-start(f32[56,128]{1,0:T(8,128)} %get-tuple-element.38), channel_id=1, source_target_pairs={{64,128},{128,64},{192,256},{256,192},{320,384},{384,320},{448,512... | collective-permute-start | bytes 86024 | tf_op jit(solution)/shard_map/ppermute | solution.py:691
  23.9 0.9 copy-start.10
  24.8 9.5 %copy-start.1 = (f32[4,8,8,128]{3,2,1,0:T(8,128)S(1)}, f32[4,8,8,128]{3,2,1,0:T(8,128)}, u32[]{:S(2)}) copy-start(f32[4,8,8,128]{3,2,1,0:T(8,128)} %param.34) | copy-start | bytes 393220
  24.8 9.5 %copy-start.2 = (bf16[384,128]{1,0:T(8,128)(2,1)S(1)}, bf16[384,128]{1,0:T(8,128)(2,1)}, u32[]{:S(2)}) copy-start(bf16[384,128]{1,0:T(8,128)(2,1)} %constant.75.clone.dright.right) | copy-start | bytes 294916
  24.8 9.5 %copy-start.23 = (bf16[256,128]{1,0:T(8,128)(2,1)S(1)}, bf16[256,128]{1,0:T(8,128)(2,1)}, u32[]{:S(2)}) copy-start(bf16[256,128]{1,0:T(8,128)(2,1)} %constant.77.clone.hright) | copy-start | bytes 196612
  25.4 6.9 %collective-permute-start.2 = (f32[56,128]{1,0:T(8,128)S(1)}, f32[56,128]{1,0:T(8,128)S(1)}, u32[]{:S(2)}, u32[]{:S(2)}) collective-permute-start(f32[56,128]{1,0:T(8,128)S(1)} %get-tuple-element.40), channel_id=1, source_target_pairs={{0,1},{1,0},{2,3},{3,2},{4,5},{5,4},{6,7},{7,6},{8,9},{9,8},{10,11... | collective-permute-start | bytes 86024 | tf_op jit(solution)/shard_map/ppermute | solution.py:691
  29.1 5.2 %collective-permute-start.3 = (f32[56,128]{1,0:T(8,128)S(1)}, f32[56,128]{1,0:T(8,128)S(1)}, u32[]{:S(2)}, u32[]{:S(2)}) collective-permute-start(f32[56,128]{1,0:T(8,128)S(1)} %get-tuple-element.41), channel_id=1, source_target_pairs={{1,2},{2,1},{3,4},{4,3},{5,6},{6,5},{7,8},{8,7},{9,10},{10,9},{11,... | collective-permute-start | bytes 86024 | tf_op jit(solution)/shard_map/ppermute | solution.py:691
  36.2 20.5 %copy-start.22 = (bf16[256,128]{1,0:T(8,128)(2,1)S(1)}, bf16[256,128]{1,0:T(8,128)(2,1)}, u32[]{:S(2)}) copy-start(bf16[256,128]{1,0:T(8,128)(2,1)} %constant.79.clone.levels) | copy-start | bytes 196612
  36.2 20.5 %copy-start.28 = (bf16[32,288]{1,0:T(8,128)(2,1)S(1)}, bf16[32,288]{1,0:T(8,128)(2,1)}, u32[]{:S(2)}) copy-start(bf16[32,288]{1,0:T(8,128)(2,1)} %constant.78.clone.toward) | copy-start | bytes 55300
  58.5 30.9 %copy-start.5 = (bf16[256,128]{1,0:T(8,128)(2,1)S(1)}, bf16[256,128]{1,0:T(8,128)(2,1)}, u32[]{:S(2)}) copy-start(bf16[256,128]{1,0:T(8,128)(2,1)} %constant.83.clone.er) | copy-start | bytes 196612
  58.5 30.9 %copy-start.6 = (bf16[256,128]{1,0:T(8,128)(2,1)S(1)}, bf16[256,128]{1,0:T(8,128)(2,1)}, u32[]{:S(2)}) copy-start(bf16[256,128]{1,0:T(8,128)(2,1)} %constant.81.clone.etr) | copy-start | bytes 196612
  58.5 30.9 %copy-start.16 = (bf16[64,192]{1,0:T(8,128)(2,1)S(1)}, bf16[64,192]{1,0:T(8,128)(2,1)}, u32[]{:S(2)}) copy-start(bf16[64,192]{1,0:T(8,128)(2,1)} %constant.84.clone.el) | copy-start | bytes 73732
  58.5 30.9 %copy-start.17 = (f32[64,128]{1,0:T(8,128)S(1)}, f32[64,128]{1,0:T(8,128)}, u32[]{:S(2)}) copy-start(f32[64,128]{1,0:T(8,128)} %constant.82.clone.sc) | copy-start | bytes 98308
  58.5 30.9 %copy-start.18 = (bf16[64,192]{1,0:T(8,128)(2,1)S(1)}, bf16[64,192]{1,0:T(8,128)(2,1)}, u32[]{:S(2)}) copy-start(bf16[64,192]{1,0:T(8,128)(2,1)} %constant.80.clone.etl) | copy-start | bytes 73732
  58.5 39.4 %all-to-all-start = ((f32[64,16,128]{2,1,0:T(8,128)}), f32[64,16,128]{2,1,0:T(8,128)S(1)}, u32[]{:S(2)}, u32[]{:S(2)}) async-start(f32[64,16,128]{2,1,0:T(8,128)} %bitcast.4), calls=%async_computation | async-start | bytes 1048576 | tf_op jit(solution)/shard_map/all_to_all | solution.py:767
  75.2 5.6 %collective-permute-start.4 = (f32[96,128]{1,0:T(8,128)S(1)}, f32[96,128]{1,0:T(8,128)S(1)}, u32[]{:S(2)}, u32[]{:S(2)}) collective-permute-start(f32[96,128]{1,0:T(8,128)S(1)} %get-tuple-element.45), channel_id=1, source_target_pairs={{0,1},{1,0},{2,3},{3,2},{4,5},{5,4},{6,7},{7,6},{8,9},{9,8},{10,11... | collective-permute-start | bytes 147464 | tf_op jit(solution)/shard_map/ppermute | solution.py:691
  77.5 11.8 %collective-permute-start.5 = (f32[96,128]{1,0:T(8,128)S(1)}, f32[96,128]{1,0:T(8,128)S(1)}, u32[]{:S(2)}, u32[]{:S(2)}) collective-permute-start(f32[96,128]{1,0:T(8,128)S(1)} %get-tuple-element.46), channel_id=1, source_target_pairs={{1,2},{2,1},{3,4},{4,3},{5,6},{6,5},{7,8},{8,7},{9,10},{10,9},{11,... | collective-permute-start | bytes 147464 | tf_op jit(solution)/shard_map/ppermute | solution.py:691
  89.4 8.5 %copy-start.7 = (bf16[256,128]{1,0:T(8,128)(2,1)S(1)}, bf16[256,128]{1,0:T(8,128)(2,1)}, u32[]{:S(2)}) copy-start(bf16[256,128]{1,0:T(8,128)(2,1)} %constant.89.clone.czh) | copy-start | bytes 196612
  89.4 8.5 %copy-start.8 = (f32[128,128]{1,0:T(8,128)S(1)}, f32[128,128]{1,0:T(8,128)}, u32[]{:S(2)}) copy-start(f32[128,128]{1,0:T(8,128)} %constant.87.clone.mky) | copy-start | bytes 196612
  89.4 8.5 %copy-start.9 = (bf16[128,192]{1,0:T(8,128)(2,1)S(1)}, bf16[128,192]{1,0:T(8,128)(2,1)}, u32[]{:S(2)}) copy-start(bf16[128,192]{1,0:T(8,128)(2,1)} %constant.85.clone.hart) | copy-start | bytes 147460
  89.4 8.5 %copy-start.12 = (f32[72,64]{1,0:T(8,128)S(1)}, f32[72,64]{1,0:T(8,128)}, u32[]{:S(2)}) copy-start(f32[72,64]{1,0:T(8,128)} %constant.88.clone.around) | copy-start | bytes 55300
  90.8 7.2 %copy-start.29 = (f32[8,128]{1,0:T(8,128)S(1)}, f32[8,128]{1,0:T(8,128)}, u32[]{:S(2)}) copy-start(f32[8,128]{1,0:T(8,128)} %constant.86.clone.ez_row) | copy-start | bytes 12292
  90.8 8.5 %collective-permute-start.6 = (f32[96,128]{1,0:T(8,128)S(1)}, f32[96,128]{1,0:T(8,128)S(1)}, u32[]{:S(2)}, u32[]{:S(2)}) collective-permute-start(f32[96,128]{1,0:T(8,128)S(1)} %get-tuple-element.48), channel_id=1, source_target_pairs={{0,1},{1,0},{2,3},{3,2},{4,5},{5,4},{6,7},{7,6},{8,9},{9,8},{10,11... | collective-permute-start | bytes 147464 | tf_op jit(solution)/shard_map/ppermute | solution.py:691
  96.0 5.4 %collective-permute-start.7 = (f32[96,128]{1,0:T(8,128)S(1)}, f32[96,128]{1,0:T(8,128)S(1)}, u32[]{:S(2)}, u32[]{:S(2)}) collective-permute-start(f32[96,128]{1,0:T(8,128)S(1)} %get-tuple-element.49), channel_id=1, source_target_pairs={{1,2},{2,1},{3,4},{4,3},{5,6},{6,5},{7,8},{8,7},{9,10},{10,9},{11,... | collective-permute-start | bytes 147464 | tf_op jit(solution)/shard_map/ppermute | solution.py:691
  98.0 3.4 %copy-start = (bf16[768,128]{1,0:T(8,128)(2,1)S(1)}, bf16[768,128]{1,0:T(8,128)(2,1)}, u32[]{:S(2)}) copy-start(bf16[768,128]{1,0:T(8,128)(2,1)} %constant.92.clone.ar) | copy-start | bytes 589828
  98.0 3.4 %copy-start.3 = (f32[192,128]{1,0:T(8,128)S(1)}, f32[192,128]{1,0:T(8,128)}, u32[]{:S(2)}) copy-start(f32[192,128]{1,0:T(8,128)} %constant.90.clone.tab) | copy-start | bytes 294916
  98.0 3.4 %copy-start.4 = (bf16[256,128]{1,0:T(8,128)(2,1)S(1)}, bf16[256,128]{1,0:T(8,128)(2,1)}, u32[]{:S(2)}) copy-start(bf16[256,128]{1,0:T(8,128)(2,1)} %constant.94.clone.hzc) | copy-start | bytes 196612
  98.0 3.4 %copy-start.11 = (bf16[64,320]{1,0:T(8,128)(2,1)S(1)}, bf16[64,320]{1,0:T(8,128)(2,1)}, u32[]{:S(2)}) copy-start(bf16[64,320]{1,0:T(8,128)(2,1)} %constant.91.clone.al) | copy-start | bytes 122884
  98.0 3.4 %copy-start.20 = (bf16[32,288]{1,0:T(8,128)(2,1)S(1)}, bf16[32,288]{1,0:T(8,128)(2,1)}, u32[]{:S(2)}) copy-start(bf16[32,288]{1,0:T(8,128)(2,1)} %constant.93.clone.back) | copy-start | bytes 55300
  98.0 3.4 %copy-start.26 = (f32[16,128]{1,0:T(8,128)S(1)}, f32[16,128]{1,0:T(8,128)}, u32[]{:S(2)}) copy-start(f32[16,128]{1,0:T(8,128)} %constant.95.clone.hy) | copy-start | bytes 24580
  101.4 12.5 %copy-start.14 = (f32[64,128]{1,0:T(8,128)S(1)}, f32[64,128]{1,0:T(8,128)}, u32[]{:S(2)}) copy-start(f32[64,128]{1,0:T(8,128)} %constant.96.clone.tab.inv_mz) | copy-start | bytes 98308
  103.3 7.2 %collective-permute-start.8 = (f32[96,128]{1,0:T(8,128)S(1)}, f32[96,128]{1,0:T(8,128)S(1)}, u32[]{:S(2)}, u32[]{:S(2)}) collective-permute-start(f32[96,128]{1,0:T(8,128)S(1)} %get-tuple-element.53), channel_id=1, source_target_pairs={{0,1},{1,0},{2,3},{3,2},{4,5},{5,4},{6,7},{7,6},{8,9},{9,8},{10,11... | collective-permute-start | bytes 147464 | tf_op jit(solution)/shard_map/ppermute | solution.py:691
  108.5 5.4 %collective-permute-start.9 = (f32[96,128]{1,0:T(8,128)S(1)}, f32[96,128]{1,0:T(8,128)S(1)}, u32[]{:S(2)}, u32[]{:S(2)}) collective-permute-start(f32[96,128]{1,0:T(8,128)S(1)} %get-tuple-element.54), channel_id=1, source_target_pairs={{1,2},{2,1},{3,4},{4,3},{5,6},{6,5},{7,8},{8,7},{9,10},{10,9},{11,... | collective-permute-start | bytes 147464 | tf_op jit(solution)/shard_map/ppermute | solution.py:691
  115.3 10.7 %copy-start.30 = (bf16[16,192]{1,0:T(8,128)(2,1)S(1)}, bf16[16,192]{1,0:T(8,128)(2,1)}, u32[]{:S(2)}) copy-start(bf16[16,192]{1,0:T(8,128)(2,1)} %constant.97.clone.edge) | copy-start | bytes 18436
  115.3 7.2 %collective-permute-start.10 = (f32[96,128]{1,0:T(8,128)S(1)}, f32[96,128]{1,0:T(8,128)S(1)}, u32[]{:S(2)}, u32[]{:S(2)}) collective-permute-start(f32[96,128]{1,0:T(8,128)S(1)} %get-tuple-element.56), channel_id=1, source_target_pairs={{0,1},{1,0},{2,3},{3,2},{4,5},{5,4},{6,7},{7,6},{8,9},{9,8},{10,11... | collective-permute-start | bytes 147464 | tf_op jit(solution)/shard_map/ppermute | solution.py:691
  120.5 5.4 %collective-permute-start.11 = (f32[96,128]{1,0:T(8,128)S(1)}, f32[96,128]{1,0:T(8,128)S(1)}, u32[]{:S(2)}, u32[]{:S(2)}) collective-permute-start(f32[96,128]{1,0:T(8,128)S(1)} %get-tuple-element.57), channel_id=1, source_target_pairs={{1,2},{2,1},{3,4},{4,3},{5,6},{6,5},{7,8},{8,7},{9,10},{10,9},{11,... | collective-permute-start | bytes 147464 | tf_op jit(solution)/shard_map/ppermute | solution.py:691
  128.7 25.2 %copy-start.13 = (f32[8,8,128]{2,1,0:T(8,128)S(1)}, f32[8,8,128]{2,1,0:T(8,128)}, u32[]{:S(2)}) copy-start(f32[8,8,128]{2,1,0:T(8,128)} %param.36) | copy-start | bytes 98308
  128.7 25.2 %copy-start.15 = (bf16[256,256]{1,0:T(8,128)(2,1)S(1)}, bf16[256,256]{1,0:T(8,128)(2,1)}, u32[]{:S(2)}) copy-start(bf16[256,256]{1,0:T(8,128)(2,1)} %constant.99.clone.gal) | copy-start | bytes 393220
  128.7 25.2 %copy-start.19 = (bf16[128,320]{1,0:T(8,128)(2,1)S(1)}, bf16[128,320]{1,0:T(8,128)(2,1)}, u32[]{:S(2)}) copy-start(bf16[128,320]{1,0:T(8,128)(2,1)} %constant.100.clone.left) | copy-start | bytes 245764
  128.7 25.2 %all-to-all-start.1 = ((f32[64,16,128]{2,1,0:T(8,128)}), f32[64,16,128]{2,1,0:T(8,128)S(1)}, u32[]{:S(2)}, u32[]{:S(2)}) async-start(f32[64,16,128]{2,1,0:T(8,128)} %bitcast.6), calls=%async_computation.1 | async-start | bytes 1048576 | tf_op jit(solution)/shard_map/all_to_all | solution.py:831
  136.2 5.6 %collective-permute-start.12 = (f32[16,128]{1,0:T(8,128)S(1)}, f32[16,128]{1,0:T(8,128)S(1)}, u32[]{:S(2)}, u32[]{:S(2)}) collective-permute-start(f32[16,128]{1,0:T(8,128)S(1)} %get-tuple-element.63), channel_id=1, source_target_pairs={{0,1},{1,0},{2,3},{3,2},{4,5},{5,4},{6,7},{7,6},{8,9},{9,8},{10,11... | collective-permute-start | bytes 24584 | tf_op jit(solution)/shard_map/ppermute | solution.py:691
  138.7 15.2 %copy-start.31 = (f32[576]{0:T(1024)S(1)}, f32[576]{0:T(1024)}, u32[]{:S(2)}) copy-start(f32[576]{0:T(1024)} %constant.98.clone.reach) | copy-start | bytes 6916
  138.7 11.3 %collective-permute-start.13 = (f32[16,128]{1,0:T(8,128)S(1)}, f32[16,128]{1,0:T(8,128)S(1)}, u32[]{:S(2)}, u32[]{:S(2)}) collective-permute-start(f32[16,128]{1,0:T(8,128)S(1)} %get-tuple-element.64), channel_id=1, source_target_pairs={{1,2},{2,1},{3,4},{4,3},{5,6},{6,5},{7,8},{8,7},{9,10},{10,9},{11,... | collective-permute-start | bytes 24584 | tf_op jit(solution)/shard_map/ppermute | solution.py:691
  (1 other events, 0.8 us)

commit v4 on v3

--- a/solution.py
+++ b/solution.py
@@ -43,7 +43,7 @@
 def jacobi_eigen(matrix):
     current = np.array(matrix)
     basis = np.eye(8)
-    for rounds in range(12):
+    for _ in range(12):
         for first in range(7):
             for second in range(first + 1, 8):
                 angle = 0.5 * math.atan2(
@@ -162,6 +162,8 @@
 
 
 def turn(field, shift):
+    if shift == 0:
+        return field
     return pltpu.roll(field, shift % NZ, 1)
 
 
@@ -261,11 +263,11 @@
         )
         shifted = np.roll(hart_y, -1, axis=1)
         self.hart_two = left3(np.concatenate([hart_y, shifted], axis=0))
-        toward = np.zeros((32, nx * 8))
+        toward = np.zeros((24, nx * 8))
         for yv in range(2):
             for xv in range(2):
                 for i in range(nx):
-                    toward[yv * 16 : yv * 16 + nx, i * 8 + xv * 2 + yv] = self.hart_x[
+                    toward[yv * 12 : yv * 12 + nx, i * 8 + xv * 2 + yv] = self.hart_x[
                         :, (i + xv) % nx
                     ]
         self.toward_left = left3(toward)
@@ -285,11 +287,11 @@
         self.scale = (1.0 / (lxy[:, None] + np.tile(lam, EZ)[None, :] + local_shift)).astype(f32)
         self.a_left = left5(lv + helmholtz_shift * np.kron(bx, bx))
         self.a_right = right5(np.concatenate([wz[:, None] * join, kz_t @ join], axis=0))
-        back = np.zeros((32, nx * 8))
+        back = np.zeros((24, nx * 8))
         for yv in range(2):
             for a in range(nx):
                 for i in range(nx):
-                    back[yv * 16 + a, i * 8 : i * 8 + 8] = self.hart_x[a, i] * hx[yv]
+                    back[yv * 12 + a, i * 8 : i * 8 + 8] = self.hart_x[a, i] * hx[yv]
         self.back_left = left3(back)
         hzc = np.zeros((NZ, NZ))
         hzc[:, :NV] = (hz / mz[:, None]) @ cz
@@ -333,7 +335,6 @@
         scratch_shapes=list(scratch),
         interpret=INTERPRET,
         compiler_params=pltpu.CompilerParams(vmem_limit_bytes=limit),
-        name=kernel.__name__,
     )(*args)
 
 
@@ -377,7 +378,7 @@
 
 
 def stage_faces(idx, fld, xa, xb, out, ya, yb):
-    below, above = swap_in(is_odd(idx[0]), xa, xb)
+    below, above = swap_in(is_odd(idx[0]), xa[...], xb[...])
     for q in range(7):
         base = q * 64
         out[base : base + 8] = fld[base : base + 8] + below[q * 8 : q * 8 + 8]
@@ -393,20 +394,23 @@
     swap_out(odd, start, end, first, second)
 
 
-def add_faces(odd, ref, first, second):
-    below, above = swap_in(odd, first, second)
+def put_faces(ref, below, above):
     count = ref.shape[0] // 8
     ref[pl.ds(0, count, stride=8), :] = ref[pl.ds(0, count, stride=8), :] + below
     ref[pl.ds(7, count, stride=8), :] = ref[pl.ds(7, count, stride=8), :] + above
 
 
+def add_faces(odd, ref, first, second):
+    put_faces(ref, *swap_in(odd, first[...], second[...]))
+
+
 def swap_out(odd, start, end, first, second):
     first[...] = jnp.where(odd, start, end)
     second[...] = jnp.where(odd, end, start)
 
 
 def swap_in(odd, first, second):
-    return jnp.where(odd, first[...], second[...]), jnp.where(odd, second[...], first[...])
+    return jnp.where(odd, first, second), jnp.where(odd, second, first)
 
 
 def is_odd(index):
@@ -438,17 +442,20 @@
         piece[0:64] = joined
         piece[64:72] = rmul(lmul(pleft[...], joined), hright[...])
 
-    def send(msg, block):
-        for k in range(ny):
-            msg[k * 16 : k * 16 + 16] = block
-
-    def stage_ring(idx, ring, toward, levels, r, ra, rb, msg):
+
+    def packed(modes, lane):
+        return sum(turn(modes[8 * g : 8 * g + 8], lane + 20 * g) for g in range(3))
+
+    def stage_ring(idx, ring, r, ra, rb):
         rows = jnp.concatenate([ring[i * 72 : i * 72 + 64] for i in range(nx)], axis=0)
         r[...] = join_x(rows, nx)
         swap_faces(is_odd(idx[1]), r, ra, rb)
+
+    def stage_message(ring, toward, levels, msg):
         corners = jnp.concatenate([ring[i * 72 + 64 : i * 72 + 72] for i in range(nx)], axis=0)
-        modes = rmul(lmul(toward[...], corners), levels[...])
-        send(msg, modes[0:16] + turn(modes[16:32], 32))
+        block = packed(rmul(lmul(toward[...], corners), levels[...]), 0)
+        for k in range(ny):
+            msg[k * 8 : k * 8 + 8] = block
 
     def smoothed(field, etl, etr, sc, er, el):
         modal = rmul(rows_of(lmul(etl, lanes_of(field))), etr)
@@ -462,22 +469,31 @@
         s[...] = join_x(local, nx)
         swap_faces(is_odd(idx[1]), s, s0, s7)
 
-    def spectra(rec, hart, ez_row, ky):
-        cells = jnp.concatenate([rec[pl.ds(a, ny, stride=16), :] for a in range(nx)], axis=1)
+    def spectra(rec, stride, hart):
+        cells = jnp.concatenate([rec[pl.ds(k, ny, stride=stride), :] for k in range(8)], axis=1)
         both = lmul(hart, cells)
-        lane = lane_index(ny)
+
+        def mode(a, lane):
+            tile, shift = slice((a % 8) * NZ, (a % 8 + 1) * NZ), -lane - 20 * (a // 8)
+            line = turn(both[0:ny, tile], shift)
+            n = 12 + a
+            tile, shift = slice((n % 8) * NZ, (n % 8 + 1) * NZ), -lane - 20 * (n // 8)
+            return line + turn(both[ny : 2 * ny, tile], shift)
+
+        return mode
+
+    def solved(comb, a, ez_row, ky):
         levels = 2.0 * (2.0 * ky + ez_row) + coarse_shift
-        found = []
-        for a in range(nx):
-            tile = slice(a * NZ, (a + 1) * NZ)
-            comb = both[0:ny, tile] + turn(both[ny : 2 * ny, tile], -32)
-            e = jnp.where(lane < NV, comb / (levels + 2.0 * float(t.ex[a])), 0.0)
-            found.append((comb, e))
-        return found
+        return jnp.where(
+            lane_index(ny) < NV, comb / (levels + 2.0 * float(t.ex[a])), 0.0
+        )
 
     def stage_coarse(idx, rec, hart, ez_row, mky, around, czh, out):
-        found = spectra(rec, hart[...], ez_row[0:1], mky[ny : 2 * ny])
-        wide = jnp.concatenate([e for _, e in found], axis=1)
+        mode = spectra(rec, 8, hart[...])
+        ky = mky[ny : 2 * ny]
+        wide = jnp.concatenate(
+            [solved(mode(a, 0), a, ez_row[0:1], ky) for a in range(nx)], axis=1
+        )
         lines = thrice(around[pl.ds(idx[1], 8), :], wide)
         columns = []
         for i in range(nx):
@@ -529,45 +545,67 @@
         q[...] = join_x(image, nx)
         swap_faces(is_odd(idx[1]), q, q0, q7)
 
-    def stage_again(idx, q, below, above, tab, etl, etr, sc, er, el, s, s0, s7, sums, scr):
+    def stage_again(
+        idx, q, below, above, z0, edge, tab, etl, etr, sc, er, el, s, s0, s7, sums, scr
+    ):
         scr[...] = q[...]
         add_faces(is_odd(idx[1]), scr, below, above)
         field = scr[...]
         local = smoothed(field, etl[...], etr[...], sc[...], er[...], el[...])
         sums[...] = fold(field * local * tiled(tab[...], nx))
         s[...] = join_x(local, nx)
-        swap_faces(is_odd(idx[1]), s, s0, s7)
+        size = nx * 8
+        odd = is_odd(idx[1])
+        swap_out(
+            odd,
+            s[pl.ds(0, size, stride=8), :],
+            s[pl.ds(7, size, stride=8), :],
+            s0.at[0:size],
+            s7.at[0:size],
+        )
+        base = pl.multiple_of(idx[0] * 64, 64)
+        start, end = slopes(z0[pl.ds(base, 64), :], edge[...])
+        swap_out(odd, start, end, s0.at[size : size + 8], s7.at[size : size + 8])
+
+    def slopes(field, edge):
+        both = lmul(edge, field)
+        return both[0:8], both[8:16]
 
     def stage_gather(
-        idx, s, below, above, z0, cq, sums1, sums2, al, tab, ar, back, hzc, edge, sq, msg, g0, g7
+        idx, s, first, second, z0, cq, sums1, sums2, al, tab, ar, back, hzc, edge, sq, msg, ends
     ):
+        odd = is_odd(idx[1])
+        size = nx * 8
+        faces = swap_in(odd, first[0:size], second[0:size])
+        below, above = swap_in(odd, first[size : size + 8], second[size : size + 8])
+        ends[0:8] = below
+        ends[8:16] = above
         sq[...] = s[...]
-        add_faces(is_odd(idx[1]), sq, below, above)
+        put_faces(sq, *faces)
         field = sq[...]
         wxy, inv_mz = tab[0:64], tab[128:192]
         image = applied(field, al[...], wxy, ar[...])
         last = total(fold(field * image * tiled(inv_mz, nx)))
         tq = restricted(image, back[...], hzc[...])
-        block = cq[0:16] + turn(cq[16:32], 32) + turn(tq[0:16], 64) + turn(tq[16:32], 96)
-        lane = lane_index(16)
-        row = lax.broadcasted_iota(jnp.int32, (16, NZ), 0)
+        block = packed(cq[...], 0) + packed(tq, 60)
+        lane = lane_index(8)
+        row = lax.broadcasted_iota(jnp.int32, (8, NZ), 0)
         values = [total(sums1[0:8]), total(sums1[8:16]), total(sums2[...]), last]
         for k, value in enumerate(values):
-            block = block + jnp.where((row == 12) & (lane == NV + k), value, 0.0)
-        send(msg, block)
+            block = block + jnp.where((row == 0) & (lane == 120 + k), value, 0.0)
         base = pl.multiple_of(idx[0] * 64, 64)
-        pair = jnp.concatenate([z0[pl.ds(base, 64), :], sq[pl.ds(base, 64), :]], axis=1)
-        slopes = lmul(edge[...], pair)
-        start = jnp.concatenate([slopes[0:8, 0:NZ], slopes[0:8, NZ:]], axis=0)
-        end = jnp.concatenate([slopes[8:16, 0:NZ], slopes[8:16, NZ:]], axis=0)
-        swap_out(is_odd(idx[1]), start, end, g0, g7)
+        start, end = slopes(sq[pl.ds(base, 64), :], edge[...])
+        for k in range(ny):
+            msg[k * 16 : k * 16 + 8] = block
+            msg[k * 16 + 8 : k * 16 + 16] = start
+        after = lax.rem(idx[1] + 1, ny)
+        msg[pl.ds(pl.multiple_of(after * 16 + 8, 8), 8), :] = end
 
     def stage_final(
         idx,
         reach,
         rec,
-        below,
-        above,
+        ends,
         z0,
         sq,
         prov,
@@ -591,10 +629,13 @@
         cross = jnp.zeros((ny, NZ), jnp.float32)
         plain = jnp.zeros((ny, NZ), jnp.float32)
         found = []
-        for comb, e in spectra(rec, hart[...], ez_row[0:1], ky):
+        mode = spectra(rec, 16, hart[...])
+        for a in range(nx):
+            comb = mode(a, 0)
+            e = solved(comb, a, ez_row[0:1], ky)
             found.append(e)
             plain = plain + e * comb
-            cross = cross + e * turn(comb, -64)
+            cross = cross + e * mode(a, 60)
         grown = rmul(jnp.concatenate(found, axis=0), gal[...])
         quad = jnp.zeros((ny, NZ), jnp.float32)
         for a in range(nx):
@@ -605,11 +646,11 @@
             quad = quad + found[a] * (
                 weight_m * grown[rows, 0:NZ] + weight_k * grown[rows, NZ : 2 * NZ]
             )
-        scalars = jnp.sum(rec[pl.ds(12, ny, stride=16), :], axis=0, keepdims=True)
+        scalars = jnp.sum(rec[pl.ds(0, ny, stride=16), :], axis=0, keepdims=True)
         line = lane_index(1)
 
         def pick(k):
-            return jnp.sum(jnp.where(line == NV + k, scalars, 0.0), axis=1, keepdims=True)
+            return jnp.sum(jnp.where(line == 120 + k, scalars, 0.0), axis=1, keepdims=True)
 
         rz0, zq0 = pick(0), pick(1)
         wq = pick(2) + total(plain)
@@ -656,12 +697,14 @@
         new[8:56] = prov[8:56] - g0[8:56] - gx[8:56]
         new[56:64] = prov[56:64] - g0[56:64] - 0.5 * (gx[56:64] + edge7)
         hx0, hx1 = hy0, hy1
-        line1 = [scr[k * 8 + 1 : k * 8 + 2] for k in range(4)]
         step0 = [0.5 * (scr[k * 8 + 1 : k * 8 + 2] - scr[k * 8 : k * 8 + 1]) for k in (1, 2)]
         step7 = [0.5 * (scr[k * 8 + 3 : k * 8 + 4] - scr[k * 8 + 2 : k * 8 + 3]) for k in (1, 2)]
-        below, above = swap_in(is_odd(idx[1]), below, above)
-        under = below[0:8] * on_z + below[8:16] * on_w + hx0 * step0[0] + hx1 * step0[1]
-        over = above[0:8] * on_z + above[8:16] * on_w + hx0 * step7[0] + hx1 * step7[1]
+        before = lax.rem(idx[1] + ny - 1, ny)
+        after = lax.rem(idx[1] + 1, ny)
+        below = rec[pl.ds(pl.multiple_of(before * 16 + 8, 8), 8), :]
+        above = rec[pl.ds(pl.multiple_of(after * 16 + 8, 8), 8), :]
+        under = ends[0:8] * on_z + below * on_w + hx0 * step0[0] + hx1 * step0[1]
+        over = ends[8:16] * on_z + above * on_w + hx0 * step7[0] + hx1 * step7[1]
         press_y = gy
         new[64:128] = press_y
         own0 = new[pl.ds(64, 8, stride=8), :]
@@ -675,6 +718,7 @@
     return (
         stage_state,
         stage_ring,
+        stage_message,
         stage_smooth,
         stage_coarse,
         stage_apply,
@@ -696,6 +740,7 @@
     (
         stage_state,
         stage_ring,
+        stage_message,
         stage_smooth,
         stage_coarse,
         stage_apply,
@@ -704,7 +749,7 @@
         stage_final,
     ) = make_stages(t)
     c = jnp.asarray
-    col, ring, face = (64, NZ), (nx * 64, NZ), (nx * 8, NZ)
+    col, ring, face, more = (64, NZ), (nx * 64, NZ), (nx * 8, NZ), (nx * 8 + 8, NZ)
 
     def on_device(flow_state, building_height, pressure_old):
         flow = flow_state.reshape(256, NZ)
@@ -755,17 +800,12 @@
             scratch=[pltpu.VMEM((448, NZ), jnp.float32)],
         )
         whole = lax.all_gather(piece, "gx", axis=0, tiled=True)
-        r, ra, rb, msg = call(
-            stage_ring,
-            [ring, face, face, (ny * 16, NZ)],
-            idx,
-            whole,
-            c(t.toward_left),
-            c(t.levels_right),
-            smem=1,
-        )
-        rec = lax.all_to_all(msg.reshape(ny, 16, NZ), "gy", 0, 0, tiled=True)
+        r, ra, rb = call(stage_ring, [ring, face, face], idx, whole, smem=1)
         below, above = exchange("gy", ra, rb)
+        (msg,) = call(
+            stage_message, [(ny * 8, NZ)], whole, c(t.toward_left), c(t.levels_right)
+        )
+        rec = lax.all_to_all(msg.reshape(ny, 8, NZ), "gy", 0, 0, tiled=True)
         smoother = (c(t.et_left), c(t.et_right), c(t.scale), c(t.e_right), c(t.e_left))
         r0, s, s0, s7 = call(
             stage_smooth, [ring, ring, face, face], idx, r, below, above, *smoother, smem=1
@@ -775,7 +815,7 @@
             stage_coarse,
             [face],
             idx,
-            rec.reshape(ny * 16, NZ),
+            rec.reshape(ny * 8, NZ),
             c(t.hart_two),
             c(t.ez_row),
             c(t.mky),
@@ -787,7 +827,7 @@
         operator = (c(t.a_left), tab, c(t.a_right), c(t.back_left), c(t.hzc_right))
         z0, q, q0, q7, cq, sums1 = call(
             stage_apply,
-            [ring, ring, face, face, (32, NZ), (16, NZ)],
+            [ring, ring, face, face, (24, NZ), (16, NZ)],
             idx,
             s,
             below,
@@ -801,20 +841,22 @@
         below, above = exchange("gy", q0, q7)
         s, s0, s7, sums2 = call(
             stage_again,
-            [ring, face, face, (8, NZ)],
+            [ring, more, more, (8, NZ)],
             idx,
             q,
             below,
             above,
+            z0,
+            c(t.edge_left),
             c(t.inv_mz),
             *smoother,
             smem=1,
             scratch=[pltpu.VMEM(ring, jnp.float32)],
         )
         below, above = exchange("gy", s0, s7)
-        sq, msg, e0, e7 = call(
+        sq, msg, ends = call(
             stage_gather,
-            [ring, (ny * 16, NZ), (16, NZ), (16, NZ)],
+            [ring, (ny * 16, NZ), (16, NZ)],
             idx,
             s,
             below,
@@ -827,7 +869,6 @@
             c(t.edge_left),
             smem=1,
         )
-        below, above = exchange("gy", e0, e7)
         rec = lax.all_to_all(msg.reshape(ny, 16, NZ), "gy", 0, 0, tiled=True)
         new, press = call(
             stage_final,
@@ -835,8 +876,7 @@
             idx,
             c(t.reach),
             rec.reshape(ny * 16, NZ),
-            below,
-            above,
+            ends,
             z0,
             sq,
             prov,

time: 157 us -> 153 us (0.975)
  blocking collectives: 20.5 us -> 47.3 us
  waiting for transfers between devices: 33.2 us -> 15.1 us
  starting transfers between devices: 80.9 us -> 68.2 us
    all_to_all x0 -> x1, blocking collectives: none -> 26.8 us  [on_device(): rec = lax.all_to_all(msg.reshape(ny, 16, NZ), 'gy', 0, 0, tiled=True)]
    ppermute x7 -> x6, waiting for transfers between devices: 29.3 us -> 15.1 us  [exchange(): lax.ppermute(second, axis, across)]
    all_to_all x2 -> x1, starting transfers between devices: 24.2 us -> 16.5 us  [on_device(): rec = lax.all_to_all(msg.reshape(ny, 8, NZ), 'gy', 0, 0, tiled=True)]
    all_to_all x2 -> x1, waiting for transfers between devices: 3.91 us -> 0.01 us  [on_device(): rec = lax.all_to_all(msg.reshape(ny, 8, NZ), 'gy', 0, 0, tiled=True)]
    ppermute x7 -> x6, starting transfers between devices: 27.6 us -> 24.5 us  [exchange(): lax.ppermute(second, axis, across)]
    ppermute x7 -> x6, starting transfers between devices: 29 us -> 27.2 us  [exchange(): lax.ppermute(first, axis, pairs)]
    pallas_call x10 -> x11, Pallas kernels: 17.5 us -> 16.6 us  [call(): pl.pallas_call(kernel, out_shape=[jax.ShapeDtypeStruct(shape, jnp.float32...]
  transfers between devices with their start and end apart: 16 -> 13, of which waited for: 8 -> 6; matrix products, arithmetic and copies ran while one was open for 0% -> 0% of each run, Pallas kernels for 2% -> 2%
where the time goes in v4:
time: 153 us; the launch traced here: 152 us
  starting transfers between devices  68.2 us (45%)
  blocking collectives  47.3 us (31%)
  Pallas kernels  16.6 us (11%)
  waiting for transfers between devices  15.1 us (10%)
  local copies, waits for them, and re-layouts  2.56 us (2%)
  between operations  1.81 us (1%)
    ppermute x6, starting transfers between devices, exchange(): lax.ppermute(first, axis, pairs)  27.2 us
    all_to_all x1, blocking collectives, on_device(): rec = lax.all_to_all(msg.reshape(ny, 16, NZ), 'gy', 0, 0, tiled=True)  26.8 us
    ppermute x6, starting transfers between devices, exchange(): lax.ppermute(second, axis, across)  24.5 us
    all_gather x1, blocking collectives, on_device(): whole = lax.all_gather(piece, 'gx', axis=0, tiled=True)  20.5 us
    pallas_call x11, Pallas kernels, call(): pl.pallas_call(kernel, out_shape=[jax.ShapeDtypeStruct(shape, jnp.float32...  16.6 us
    all_to_all x1, starting transfers between devices, on_device(): rec = lax.all_to_all(msg.reshape(ny, 8, NZ), 'gy', 0, 0, tiled=True)  16.5 us
    ppermute x6, waiting for transfers between devices, exchange(): lax.ppermute(second, axis, across)  15.1 us
  transfers between devices with their start and end apart: 13, of which 6 were waited for; matrix products, arithmetic and copies ran while one was open for 0% of the time, Pallas kernels for 2%

profile of v4, /device:TPU:1, one launch (start us, length us, event | category | flops | bytes accessed | tf_op | source)
XLA Modules:
  0.0 152.3 jit_solution(3943271220452616629)
XLA Ops:
  1.3 0.6 pad_add_fusion.idx
  1.9 3.2 %shard_map.329 = (f32[448,128]{1,0:T(8,128)}, f32[56,128]{1,0:T(8,128)}, f32[56,128]{1,0:T(8,128)}, f32[64,128]{1,0:T(8,128)}) custom-call(s32[2]{0:T(128)} %pad_add_fusion.idx, s32[1,1]{1,0:T(1,128)S(6)} %copy.36.h, f32[256,128]{1,0:T(8,128)} %bitcast.13, f32[64,128]{1,0:T(8,128)} %bitcast.15, bf16[192,320]{1,0:T(8,128)(2,1)} %constant.70.clone.refs_2_, ...), custom_call_target="tpu_custom_call" | custom-call | tf_op jit(solution)/shard_map/pallas_call | solution.py:330
  5.1 4.8 %collective-permute-start = (f32[56,128]{1,0:T(8,128)}, f32[56,128]{1,0:T(8,128)S(1)}, u32[]{:S(2)}, u32[]{:S(2)}) collective-permute-start(f32[56,128]{1,0:T(8,128)} %get-tuple-element.35), channel_id=1, source_target_pairs={{0,64},{64,0},{128,192},{192,128},{256,320},{320,256},{384,448},{4... | collective-permute-start | bytes 86024 | tf_op jit(solution)/shard_map/ppermute | solution.py:735
  10.0 12.5 %collective-permute-start.1 = (f32[56,128]{1,0:T(8,128)}, f32[56,128]{1,0:T(8,128)S(1)}, u32[]{:S(2)}, u32[]{:S(2)}) collective-permute-start(f32[56,128]{1,0:T(8,128)} %get-tuple-element.36), channel_id=1, source_target_pairs={{64,128},{128,64},{192,256},{256,192},{320,384},{384,320},{448,512... | collective-permute-start | bytes 86024 | tf_op jit(solution)/shard_map/ppermute | solution.py:735
  22.5 1.4 collective-permute-done.1.xb
  23.9 0.9 copy-done.10
  24.9 0.6 shard_map.330
  25.5 3.7 %collective-permute-start.2 = (f32[56,128]{1,0:T(8,128)S(1)}, f32[56,128]{1,0:T(8,128)S(1)}, u32[]{:S(2)}, u32[]{:S(2)}) collective-permute-start(f32[56,128]{1,0:T(8,128)S(1)} %get-tuple-element.38), channel_id=1, source_target_pairs={{0,1},{1,0},{2,3},{3,2},{4,5},{5,4},{6,7},{7,6},{8,9},{9,8},{10,11... | collective-permute-start | bytes 86024 | tf_op jit(solution)/shard_map/ppermute | solution.py:735
  29.2 3.1 %collective-permute-start.3 = (f32[56,128]{1,0:T(8,128)S(1)}, f32[56,128]{1,0:T(8,128)S(1)}, u32[]{:S(2)}, u32[]{:S(2)}) collective-permute-start(f32[56,128]{1,0:T(8,128)S(1)} %get-tuple-element.39), channel_id=1, source_target_pairs={{1,2},{2,1},{3,4},{4,3},{5,6},{6,5},{7,8},{8,7},{9,10},{10,9},{11,... | collective-permute-start | bytes 86024 | tf_op jit(solution)/shard_map/ppermute | solution.py:735
  32.3 2.1 %collective-permute-done.3.above = f32[56,128]{1,0:T(8,128)S(1)} collective-permute-done((f32[56,128]{1,0:T(8,128)S(1)}, f32[56,128]{1,0:T(8,128)S(1)}, u32[]{:S(2)}, u32[]{:S(2)}) %collective-permute-start.3) | collective-permute-done | bytes 28704 | tf_op jit(solution)/shard_map/ppermute | solution.py:735
  34.4 0.7 copy-done.28
  35.2 1.1 shard_map.331
  36.3 0.0 copy-start.29
  36.3 20.5 %all_gather.3.ring = f32[864,128]{1,0:T(8,128)S(1)} all-gather(f32[72,128]{1,0:T(8,128)S(1)} %get-tuple-element.41), channel_id=1, replica_groups=mesh['gx'=12,'gy'=64] {'gx'}, dimensions={0}, use_global_device_ids=true | all-gather | bytes 479232 | tf_op jit(solution)/shard_map/all_gather | solution.py:802
  56.8 1.0 shard_map.334
  57.8 16.5 %all-to-all-start = ((f32[64,8,128]{2,1,0:T(8,128)}), f32[64,8,128]{2,1,0:T(8,128)S(1)}, u32[]{:S(2)}, u32[]{:S(2)}) async-start(f32[64,8,128]{2,1,0:T(8,128)} %bitcast.4), calls=%async_computation | async-start | bytes 524288 | tf_op jit(solution)/shard_map/all_to_all | solution.py:808
  74.4 0.0 copy-start.8
  74.4 0.0 copy-start.16
  74.4 0.0 copy-start.17
  74.4 0.0 copy-start.18
  74.4 0.6 shard_map.332
  75.0 2.4 %collective-permute-start.4 = (f32[96,128]{1,0:T(8,128)S(1)}, f32[96,128]{1,0:T(8,128)S(1)}, u32[]{:S(2)}, u32[]{:S(2)}) collective-permute-start(f32[96,128]{1,0:T(8,128)S(1)} %get-tuple-element.43), channel_id=1, source_target_pairs={{0,1},{1,0},{2,3},{3,2},{4,5},{5,4},{6,7},{7,6},{8,9},{9,8},{10,11... | collective-permute-start | bytes 147464 | tf_op jit(solution)/shard_map/ppermute | solution.py:735
  77.4 3.2 %collective-permute-start.5 = (f32[96,128]{1,0:T(8,128)S(1)}, f32[96,128]{1,0:T(8,128)S(1)}, u32[]{:S(2)}, u32[]{:S(2)}) collective-permute-start(f32[96,128]{1,0:T(8,128)S(1)} %get-tuple-element.44), channel_id=1, source_target_pairs={{1,2},{2,1},{3,4},{4,3},{5,6},{6,5},{7,8},{8,7},{9,10},{10,9},{11,... | collective-permute-start | bytes 147464 | tf_op jit(solution)/shard_map/ppermute | solution.py:735
  80.6 2.5 %collective-permute-done.5.rb = f32[96,128]{1,0:T(8,128)S(1)} collective-permute-done((f32[96,128]{1,0:T(8,128)S(1)}, f32[96,128]{1,0:T(8,128)S(1)}, u32[]{:S(2)}, u32[]{:S(2)}) %collective-permute-start.5) | collective-permute-done | bytes 49184 | tf_op jit(solution)/shard_map/ppermute | solution.py:735
  83.1 0.0 copy-start.5
  83.2 0.0 copy-start.6
  83.2 0.0 copy-start.12
  83.2 1.3 shard_map.333
  84.5 0.0 copy-start.30
  84.5 5.8 %collective-permute-start.6 = (f32[96,128]{1,0:T(8,128)S(1)}, f32[96,128]{1,0:T(8,128)S(1)}, u32[]{:S(2)}, u32[]{:S(2)}) collective-permute-start(f32[96,128]{1,0:T(8,128)S(1)} %get-tuple-element.46), channel_id=1, source_target_pairs={{0,1},{1,0},{2,3},{3,2},{4,5},{5,4},{6,7},{7,6},{8,9},{9,8},{10,11... | collective-permute-start | bytes 147464 | tf_op jit(solution)/shard_map/ppermute | solution.py:735
  90.3 1.9 %collective-permute-start.7 = (f32[96,128]{1,0:T(8,128)S(1)}, f32[96,128]{1,0:T(8,128)S(1)}, u32[]{:S(2)}, u32[]{:S(2)}) collective-permute-start(f32[96,128]{1,0:T(8,128)S(1)} %get-tuple-element.47), channel_id=1, source_target_pairs={{1,2},{2,1},{3,4},{4,3},{5,6},{6,5},{7,8},{8,7},{9,10},{10,9},{11,... | collective-permute-start | bytes 147464 | tf_op jit(solution)/shard_map/ppermute | solution.py:735
  92.3 0.0 copy-start
  92.3 0.0 copy-start.3
  92.3 0.0 copy-start.7
  92.4 1.2 shard_map.335.vert
  93.6 2.1 %collective-permute-done.7.above = f32[96,128]{1,0:T(8,128)S(1)} collective-permute-done((f32[96,128]{1,0:T(8,128)S(1)}, f32[96,128]{1,0:T(8,128)S(1)}, u32[]{:S(2)}, u32[]{:S(2)}) %collective-permute-start.7) | collective-permute-done | bytes 49184 | tf_op jit(solution)/shard_map/ppermute | solution.py:735
  95.8 1.8 %shard_map.336 = (f32[768,128]{1,0:T(8,128)S(1)}, f32[768,128]{1,0:T(8,128)S(1)}, f32[96,128]{1,0:T(8,128)S(1)}, f32[96,128]{1,0:T(8,128)S(1)}, f32[24,128]{1,0:T(8,128)S(1)}, /*index=5*/f32[16,128]{1,0:T(8,128)S(1)}) custom-call(s32[2]{0:T(128)S(1)} %copy-done.25, f32[768,128]{1,0:T(8,128)S(1)} %get-tuple-element.45.s, ...), custom_call_target="tpu_custom_call" | custom-call | tf_op jit(solution)/shard_map/pallas_call | solution.py:330
  97.6 5.2 %collective-permute-start.8 = (f32[96,128]{1,0:T(8,128)S(1)}, f32[96,128]{1,0:T(8,128)S(1)}, u32[]{:S(2)}, u32[]{:S(2)}) collective-permute-start(f32[96,128]{1,0:T(8,128)S(1)} %get-tuple-element.50), channel_id=1, source_target_pairs={{0,1},{1,0},{2,3},{3,2},{4,5},{5,4},{6,7},{7,6},{8,9},{9,8},{10,11... | collective-permute-start | bytes 147464 | tf_op jit(solution)/shard_map/ppermute | solution.py:735
  102.9 1.9 %collective-permute-start.9 = (f32[96,128]{1,0:T(8,128)S(1)}, f32[96,128]{1,0:T(8,128)S(1)}, u32[]{:S(2)}, u32[]{:S(2)}) collective-permute-start(f32[96,128]{1,0:T(8,128)S(1)} %get-tuple-element.51), channel_id=1, source_target_pairs={{1,2},{2,1},{3,4},{4,3},{5,6},{6,5},{7,8},{8,7},{9,10},{10,9},{11,... | collective-permute-start | bytes 147464 | tf_op jit(solution)/shard_map/ppermute | solution.py:735
  104.8 3.5 %collective-permute-done.9.above = f32[96,128]{1,0:T(8,128)S(1)} collective-permute-done((f32[96,128]{1,0:T(8,128)S(1)}, f32[96,128]{1,0:T(8,128)S(1)}, u32[]{:S(2)}, u32[]{:S(2)}) %collective-permute-start.9) | collective-permute-done | bytes 49184 | tf_op jit(solution)/shard_map/ppermute | solution.py:735
  108.3 1.4 shard_map.337
  109.7 5.2 %collective-permute-start.10 = (f32[104,128]{1,0:T(8,128)S(1)}, f32[104,128]{1,0:T(8,128)S(1)}, u32[]{:S(2)}, u32[]{:S(2)}) collective-permute-start(f32[104,128]{1,0:T(8,128)S(1)} %get-tuple-element.54), channel_id=1, source_target_pairs={{0,1},{1,0},{2,3},{3,2},{4,5},{5,4},{6,7},{7,6},{8,9},{9,8},{10,11... | collective-permute-start | bytes 159752 | tf_op jit(solution)/shard_map/ppermute | solution.py:735
  114.9 1.9 %collective-permute-start.11 = (f32[104,128]{1,0:T(8,128)S(1)}, f32[104,128]{1,0:T(8,128)S(1)}, u32[]{:S(2)}, u32[]{:S(2)}) collective-permute-start(f32[104,128]{1,0:T(8,128)S(1)} %get-tuple-element.55), channel_id=1, source_target_pairs={{1,2},{2,1},{3,4},{4,3},{5,6},{6,5},{7,8},{8,7},{9,10},{10,9},{11,... | collective-permute-start | bytes 159752 | tf_op jit(solution)/shard_map/ppermute | solution.py:735
  116.8 3.5 %collective-permute-done.11.second = f32[104,128]{1,0:T(8,128)S(1)} collective-permute-done((f32[104,128]{1,0:T(8,128)S(1)}, f32[104,128]{1,0:T(8,128)S(1)}, u32[]{:S(2)}, u32[]{:S(2)}) %collective-permute-start.11) | collective-permute-done | bytes 53280 | tf_op jit(solution)/shard_map/ppermute | solution.py:735
  120.4 1.9 %shard_map.338 = (f32[768,128]{1,0:T(8,128)S(1)}, f32[1024,128]{1,0:T(8,128)S(1)}, f32[16,128]{1,0:T(8,128)S(1)}) custom-call(s32[2]{0:T(128)S(1)} %copy-done.25, f32[768,128]{1,0:T(8,128)S(1)} %get-tuple-element.53.s, f32[104,128]{1,0:T(8,128)S(1)} %collective-permute-done.10.first, f32[104,128]{1,0:T(8,128)S(1)} %collective-permute-done.11.second, ...), custom_call_target="tpu_custom_call" | custom-call | tf_op jit(solution)/shard_map/pallas_call | solution.py:330
  122.3 26.8 %all_to_all.10 = f32[64,16,128]{2,1,0:T(8,128)S(1)} all-to-all(f32[64,16,128]{2,1,0:T(8,128)S(1)} %bitcast.12), channel_id=1, replica_groups=mesh['gx'=12,'gy'=64] {'gy'}, dimensions={0} | all-to-all | bytes 1048576 | tf_op jit(solution)/shard_map/all_to_all | solution.py:872
  149.2 0.7 copy-done.31
  149.8 2.4 %shard_map.339 = (f32[256,128]{1,0:T(8,128)}, f32[64,128]{1,0:T(8,128)}) custom-call(s32[2]{0:T(128)S(1)} %copy-done.25, f32[576]{0:T(1024)S(1)} %copy-done.31, f32[1024,128]{1,0:T(8,128)S(1)} %bitcast.10, f32[16,128]{1,0:T(8,128)S(1)} %get-tuple-element.60.ends, f32[768,128]{1,0:T(8,128)S(1)} %get-tuple-element.52.z0, f32[768,128]{1,0:T(8,128)S(1)} %get-tuple-element.61.sq, ...), custom_call_target="tpu_custom_call" | custom-call | tf_op jit(solution)/shard_map/pallas_call | solution.py:330
  (58 shorter events, 0.1 us)
Async XLA Ops:
  1.9 32.5 %copy-start.20 = (bf16[64,640]{1,0:T(8,128)(2,1)S(1)}, bf16[64,640]{1,0:T(8,128)(2,1)}, u32[]{:S(2)}) copy-start(bf16[64,640]{1,0:T(8,128)(2,1)} %constant.74.clone.dleft) | copy-start | bytes 245764
  1.9 32.5 %copy-start.24 = (f32[128,128]{1,0:T(8,128)S(1)}, f32[128,128]{1,0:T(8,128)}, u32[]{:S(2)}) copy-start(f32[128,128]{1,0:T(8,128)} %constant.73.clone.tab) | copy-start | bytes 196612
  1.9 32.5 %copy-start.32 = (bf16[8,192]{1,0:T(8,128)(2,1)S(1)}, bf16[8,192]{1,0:T(8,128)(2,1)}, u32[]{:S(2)}) copy-start(bf16[8,192]{1,0:T(8,128)(2,1)} %constant.76.clone.pleft) | copy-start | bytes 9220
  5.1 17.3 %collective-permute-start = (f32[56,128]{1,0:T(8,128)}, f32[56,128]{1,0:T(8,128)S(1)}, u32[]{:S(2)}, u32[]{:S(2)}) collective-permute-start(f32[56,128]{1,0:T(8,128)} %get-tuple-element.35), channel_id=1, source_target_pairs={{0,64},{64,0},{128,192},{192,128},{256,320},{320,256},{384,448},{4... | collective-permute-start | bytes 86024 | tf_op jit(solution)/shard_map/ppermute | solution.py:735
  10.0 14.0 %copy-start.25 = (s32[2]{0:T(128)S(1)}, s32[2]{0:T(128)}, u32[]{:S(2)}) copy-start(s32[2]{0:T(128)} %pad_add_fusion.idx) | copy-start | bytes 28
  10.0 13.9 %collective-permute-start.1 = (f32[56,128]{1,0:T(8,128)}, f32[56,128]{1,0:T(8,128)S(1)}, u32[]{:S(2)}, u32[]{:S(2)}) collective-permute-start(f32[56,128]{1,0:T(8,128)} %get-tuple-element.36), channel_id=1, source_target_pairs={{64,128},{128,64},{192,256},{256,192},{320,384},{384,320},{448,512... | collective-permute-start | bytes 86024 | tf_op jit(solution)/shard_map/ppermute | solution.py:735
  23.9 0.9 copy-start.10
  24.9 9.5 %copy-start.1 = (f32[4,8,8,128]{3,2,1,0:T(8,128)S(1)}, f32[4,8,8,128]{3,2,1,0:T(8,128)}, u32[]{:S(2)}) copy-start(f32[4,8,8,128]{3,2,1,0:T(8,128)} %param.34) | copy-start | bytes 393220
  24.9 9.5 %copy-start.2 = (bf16[384,128]{1,0:T(8,128)(2,1)S(1)}, bf16[384,128]{1,0:T(8,128)(2,1)}, u32[]{:S(2)}) copy-start(bf16[384,128]{1,0:T(8,128)(2,1)} %constant.75.clone.dright.right) | copy-start | bytes 294916
  24.9 9.5 %copy-start.23 = (bf16[256,128]{1,0:T(8,128)(2,1)S(1)}, bf16[256,128]{1,0:T(8,128)(2,1)}, u32[]{:S(2)}) copy-start(bf16[256,128]{1,0:T(8,128)(2,1)} %constant.77.clone.hright) | copy-start | bytes 196612
  25.5 6.9 %collective-permute-start.2 = (f32[56,128]{1,0:T(8,128)S(1)}, f32[56,128]{1,0:T(8,128)S(1)}, u32[]{:S(2)}, u32[]{:S(2)}) collective-permute-start(f32[56,128]{1,0:T(8,128)S(1)} %get-tuple-element.38), channel_id=1, source_target_pairs={{0,1},{1,0},{2,3},{3,2},{4,5},{5,4},{6,7},{7,6},{8,9},{9,8},{10,11... | collective-permute-start | bytes 86024 | tf_op jit(solution)/shard_map/ppermute | solution.py:735
  29.2 5.2 %collective-permute-start.3 = (f32[56,128]{1,0:T(8,128)S(1)}, f32[56,128]{1,0:T(8,128)S(1)}, u32[]{:S(2)}, u32[]{:S(2)}) collective-permute-start(f32[56,128]{1,0:T(8,128)S(1)} %get-tuple-element.39), channel_id=1, source_target_pairs={{1,2},{2,1},{3,4},{4,3},{5,6},{6,5},{7,8},{8,7},{9,10},{10,9},{11,... | collective-permute-start | bytes 86024 | tf_op jit(solution)/shard_map/ppermute | solution.py:735
  34.4 0.8 copy-start.28
  36.3 20.5 %copy-start.22 = (bf16[256,128]{1,0:T(8,128)(2,1)S(1)}, bf16[256,128]{1,0:T(8,128)(2,1)}, u32[]{:S(2)}) copy-start(bf16[256,128]{1,0:T(8,128)(2,1)} %constant.79.clone.levels) | copy-start | bytes 196612
  36.3 20.5 %copy-start.29 = (bf16[24,288]{1,0:T(8,128)(2,1)S(1)}, bf16[24,288]{1,0:T(8,128)(2,1)}, u32[]{:S(2)}) copy-start(bf16[24,288]{1,0:T(8,128)(2,1)} %constant.78.clone.toward) | copy-start | bytes 41476
  57.8 34.4 %all-to-all-start = ((f32[64,8,128]{2,1,0:T(8,128)}), f32[64,8,128]{2,1,0:T(8,128)S(1)}, u32[]{:S(2)}, u32[]{:S(2)}) async-start(f32[64,8,128]{2,1,0:T(8,128)} %bitcast.4), calls=%async_computation | async-start | bytes 524288 | tf_op jit(solution)/shard_map/all_to_all | solution.py:808
  74.4 8.7 %copy-start.8 = (bf16[256,128]{1,0:T(8,128)(2,1)S(1)}, bf16[256,128]{1,0:T(8,128)(2,1)}, u32[]{:S(2)}) copy-start(bf16[256,128]{1,0:T(8,128)(2,1)} %constant.83.clone.er) | copy-start | bytes 196612
  74.4 8.7 %copy-start.9 = (bf16[256,128]{1,0:T(8,128)(2,1)S(1)}, bf16[256,128]{1,0:T(8,128)(2,1)}, u32[]{:S(2)}) copy-start(bf16[256,128]{1,0:T(8,128)(2,1)} %constant.81.clone.etr) | copy-start | bytes 196612
  74.4 8.7 %copy-start.16 = (bf16[64,192]{1,0:T(8,128)(2,1)S(1)}, bf16[64,192]{1,0:T(8,128)(2,1)}, u32[]{:S(2)}) copy-start(bf16[64,192]{1,0:T(8,128)(2,1)} %constant.84.clone.el) | copy-start | bytes 73732
  74.4 8.7 %copy-start.17 = (f32[64,128]{1,0:T(8,128)S(1)}, f32[64,128]{1,0:T(8,128)}, u32[]{:S(2)}) copy-start(f32[64,128]{1,0:T(8,128)} %constant.82.clone.sc) | copy-start | bytes 98308
  74.4 8.7 %copy-start.18 = (bf16[64,192]{1,0:T(8,128)(2,1)S(1)}, bf16[64,192]{1,0:T(8,128)(2,1)}, u32[]{:S(2)}) copy-start(bf16[64,192]{1,0:T(8,128)(2,1)} %constant.80.clone.etl) | copy-start | bytes 73732
  75.0 5.6 %collective-permute-start.4 = (f32[96,128]{1,0:T(8,128)S(1)}, f32[96,128]{1,0:T(8,128)S(1)}, u32[]{:S(2)}, u32[]{:S(2)}) collective-permute-start(f32[96,128]{1,0:T(8,128)S(1)} %get-tuple-element.43), channel_id=1, source_target_pairs={{0,1},{1,0},{2,3},{3,2},{4,5},{5,4},{6,7},{7,6},{8,9},{9,8},{10,11... | collective-permute-start | bytes 147464 | tf_op jit(solution)/shard_map/ppermute | solution.py:735
  77.4 5.7 %collective-permute-start.5 = (f32[96,128]{1,0:T(8,128)S(1)}, f32[96,128]{1,0:T(8,128)S(1)}, u32[]{:S(2)}, u32[]{:S(2)}) collective-permute-start(f32[96,128]{1,0:T(8,128)S(1)} %get-tuple-element.44), channel_id=1, source_target_pairs={{1,2},{2,1},{3,4},{4,3},{5,6},{6,5},{7,8},{8,7},{9,10},{10,9},{11,... | collective-permute-start | bytes 147464 | tf_op jit(solution)/shard_map/ppermute | solution.py:735
  83.1 9.1 %copy-start.4 = (bf16[256,128]{1,0:T(8,128)(2,1)S(1)}, bf16[256,128]{1,0:T(8,128)(2,1)}, u32[]{:S(2)}) copy-start(bf16[256,128]{1,0:T(8,128)(2,1)} %constant.89.clone.czh) | copy-start | bytes 196612
  83.1 9.1 %copy-start.5 = (f32[128,128]{1,0:T(8,128)S(1)}, f32[128,128]{1,0:T(8,128)}, u32[]{:S(2)}) copy-start(f32[128,128]{1,0:T(8,128)} %constant.87.clone.mky) | copy-start | bytes 196612
  83.2 9.1 %copy-start.6 = (bf16[128,192]{1,0:T(8,128)(2,1)S(1)}, bf16[128,192]{1,0:T(8,128)(2,1)}, u32[]{:S(2)}) copy-start(bf16[128,192]{1,0:T(8,128)(2,1)} %constant.85.clone.hart) | copy-start | bytes 147460
  83.2 9.1 %copy-start.12 = (f32[72,64]{1,0:T(8,128)S(1)}, f32[72,64]{1,0:T(8,128)}, u32[]{:S(2)}) copy-start(f32[72,64]{1,0:T(8,128)} %constant.88.clone.around) | copy-start | bytes 55300
  84.5 7.8 %copy-start.30 = (f32[8,128]{1,0:T(8,128)S(1)}, f32[8,128]{1,0:T(8,128)}, u32[]{:S(2)}) copy-start(f32[8,128]{1,0:T(8,128)} %constant.86.clone.ez_row) | copy-start | bytes 12292
  84.5 9.1 %collective-permute-start.6 = (f32[96,128]{1,0:T(8,128)S(1)}, f32[96,128]{1,0:T(8,128)S(1)}, u32[]{:S(2)}, u32[]{:S(2)}) collective-permute-start(f32[96,128]{1,0:T(8,128)S(1)} %get-tuple-element.46), channel_id=1, source_target_pairs={{0,1},{1,0},{2,3},{3,2},{4,5},{5,4},{6,7},{7,6},{8,9},{9,8},{10,11... | collective-permute-start | bytes 147464 | tf_op jit(solution)/shard_map/ppermute | solution.py:735
  90.3 5.4 %collective-permute-start.7 = (f32[96,128]{1,0:T(8,128)S(1)}, f32[96,128]{1,0:T(8,128)S(1)}, u32[]{:S(2)}, u32[]{:S(2)}) collective-permute-start(f32[96,128]{1,0:T(8,128)S(1)} %get-tuple-element.47), channel_id=1, source_target_pairs={{1,2},{2,1},{3,4},{4,3},{5,6},{6,5},{7,8},{8,7},{9,10},{10,9},{11,... | collective-permute-start | bytes 147464 | tf_op jit(solution)/shard_map/ppermute | solution.py:735
  92.3 3.4 %copy-start = (bf16[768,128]{1,0:T(8,128)(2,1)S(1)}, bf16[768,128]{1,0:T(8,128)(2,1)}, u32[]{:S(2)}) copy-start(bf16[768,128]{1,0:T(8,128)(2,1)} %constant.92.clone.ar) | copy-start | bytes 589828
  92.3 3.4 %copy-start.3 = (f32[192,128]{1,0:T(8,128)S(1)}, f32[192,128]{1,0:T(8,128)}, u32[]{:S(2)}) copy-start(f32[192,128]{1,0:T(8,128)} %constant.90.clone.tab) | copy-start | bytes 294916
  92.3 3.4 %copy-start.7 = (bf16[256,128]{1,0:T(8,128)(2,1)S(1)}, bf16[256,128]{1,0:T(8,128)(2,1)}, u32[]{:S(2)}) copy-start(bf16[256,128]{1,0:T(8,128)(2,1)} %constant.94.clone.hzc) | copy-start | bytes 196612
  92.4 3.4 %copy-start.11 = (bf16[64,320]{1,0:T(8,128)(2,1)S(1)}, bf16[64,320]{1,0:T(8,128)(2,1)}, u32[]{:S(2)}) copy-start(bf16[64,320]{1,0:T(8,128)(2,1)} %constant.91.clone.al) | copy-start | bytes 122884
  92.4 3.4 %copy-start.21 = (bf16[24,288]{1,0:T(8,128)(2,1)S(1)}, bf16[24,288]{1,0:T(8,128)(2,1)}, u32[]{:S(2)}) copy-start(bf16[24,288]{1,0:T(8,128)(2,1)} %constant.93.clone.back) | copy-start | bytes 41476
  92.4 3.4 %copy-start.26 = (f32[16,128]{1,0:T(8,128)S(1)}, f32[16,128]{1,0:T(8,128)}, u32[]{:S(2)}) copy-start(f32[16,128]{1,0:T(8,128)} %constant.95.clone.hy) | copy-start | bytes 24580
  95.8 12.5 %copy-start.14 = (f32[64,128]{1,0:T(8,128)S(1)}, f32[64,128]{1,0:T(8,128)}, u32[]{:S(2)}) copy-start(f32[64,128]{1,0:T(8,128)} %constant.97.clone.tab.inv_mz) | copy-start | bytes 98308
  95.8 12.5 %copy-start.27 = (bf16[16,192]{1,0:T(8,128)(2,1)S(1)}, bf16[16,192]{1,0:T(8,128)(2,1)}, u32[]{:S(2)}) copy-start(bf16[16,192]{1,0:T(8,128)(2,1)} %constant.96.clone.edge) | copy-start | bytes 18436
  97.6 7.2 %collective-permute-start.8 = (f32[96,128]{1,0:T(8,128)S(1)}, f32[96,128]{1,0:T(8,128)S(1)}, u32[]{:S(2)}, u32[]{:S(2)}) collective-permute-start(f32[96,128]{1,0:T(8,128)S(1)} %get-tuple-element.50), channel_id=1, source_target_pairs={{0,1},{1,0},{2,3},{3,2},{4,5},{5,4},{6,7},{7,6},{8,9},{9,8},{10,11... | collective-permute-start | bytes 147464 | tf_op jit(solution)/shard_map/ppermute | solution.py:735
  102.9 5.4 %collective-permute-start.9 = (f32[96,128]{1,0:T(8,128)S(1)}, f32[96,128]{1,0:T(8,128)S(1)}, u32[]{:S(2)}, u32[]{:S(2)}) collective-permute-start(f32[96,128]{1,0:T(8,128)S(1)} %get-tuple-element.51), channel_id=1, source_target_pairs={{1,2},{2,1},{3,4},{4,3},{5,6},{6,5},{7,8},{8,7},{9,10},{10,9},{11,... | collective-permute-start | bytes 147464 | tf_op jit(solution)/shard_map/ppermute | solution.py:735
  109.7 7.2 %collective-permute-start.10 = (f32[104,128]{1,0:T(8,128)S(1)}, f32[104,128]{1,0:T(8,128)S(1)}, u32[]{:S(2)}, u32[]{:S(2)}) collective-permute-start(f32[104,128]{1,0:T(8,128)S(1)} %get-tuple-element.54), channel_id=1, source_target_pairs={{0,1},{1,0},{2,3},{3,2},{4,5},{5,4},{6,7},{7,6},{8,9},{9,8},{10,11... | collective-permute-start | bytes 159752 | tf_op jit(solution)/shard_map/ppermute | solution.py:735
  114.9 5.5 %collective-permute-start.11 = (f32[104,128]{1,0:T(8,128)S(1)}, f32[104,128]{1,0:T(8,128)S(1)}, u32[]{:S(2)}, u32[]{:S(2)}) collective-permute-start(f32[104,128]{1,0:T(8,128)S(1)} %get-tuple-element.55), channel_id=1, source_target_pairs={{1,2},{2,1},{3,4},{4,3},{5,6},{6,5},{7,8},{8,7},{9,10},{10,9},{11,... | collective-permute-start | bytes 159752 | tf_op jit(solution)/shard_map/ppermute | solution.py:735
  122.3 26.9 %copy-start.13 = (f32[8,8,128]{2,1,0:T(8,128)S(1)}, f32[8,8,128]{2,1,0:T(8,128)}, u32[]{:S(2)}) copy-start(f32[8,8,128]{2,1,0:T(8,128)} %param.36) | copy-start | bytes 98308
  122.3 26.9 %copy-start.15 = (bf16[256,256]{1,0:T(8,128)(2,1)S(1)}, bf16[256,256]{1,0:T(8,128)(2,1)}, u32[]{:S(2)}) copy-start(bf16[256,256]{1,0:T(8,128)(2,1)} %constant.99.clone.gal) | copy-start | bytes 393220
  122.3 26.9 %copy-start.19 = (bf16[128,320]{1,0:T(8,128)(2,1)S(1)}, bf16[128,320]{1,0:T(8,128)(2,1)}, u32[]{:S(2)}) copy-start(bf16[128,320]{1,0:T(8,128)(2,1)} %constant.100.clone.left) | copy-start | bytes 245764
  149.1 0.7 copy-start.31
